TPU v7x, 128 devices: a whole 4x4x4 slice. The times are simulated.
128 devices in a mesh: grain: 8 (over z, x_hi), row: 16 (over y, x_lo, core).
Axes of the slice: x: 4 (x_hi: 2, x_lo: 2; x = x_hi * 2 + x_lo), y: 4, z: 4, core: 2. Of those that a mesh axis runs over, the one named last changes fastest.
Arguments:
- order_params: float32 [64, 4, 1024, 1024], P('grain', None, 'row'), may hold values from 0 to 0.5
- eigen_weight: float32 [64], P('grain'), may hold values from -1 to 1
- green: float32 [1024, 1024], replicated, may hold values from 0.25 to 2
Outputs:
- updated: float32 [64, 4, 1024, 1024], P('grain', None, 'row')
- potential: float32 [4, 1024, 1024], P(None, 'row')
All inputs are finite; a program needn't handle non-finite values.
Results may differ from a plain program's by a relative error of at most 0.00016.
Values sent between devices are 32-bit elements; how exact they have to be, the bound alone decides.
No kernel may reach another device: no remote copies, remote signals or barrier semaphores. Data moves between devices by JAX's collectives and lax.ppermute only.
A program may use at most 128 MiB of HBM per device.

v0:
```python
import math

import jax
import jax.numpy as jnp
from jax import lax
from jax.sharding import PartitionSpec as P

STEPS = 3


time_step = 0.1
alpha_coef = 1.0
beta_coef = 1.0
gamma_coef = 0.25
kappa_coef = 1.0
elastic_coef = 2.0


def with_halo(x, sides, width):
    for axis, dim in sides:
        devices, length = (lax.axis_size(axis), x.shape[dim])
        up = [(i, (i + 1) % devices) for i in range(devices)]
        down = [(j, i) for i, j in up]
        last = lax.slice_in_dim(x, length - width, length, axis=dim)
        leading = lax.slice_in_dim(x, 0, width, axis=dim)
        before = lax.ppermute(last, axis, up)
        after = lax.ppermute(leading, axis, down)
        x = jnp.concatenate([before, x, after], axis=dim)
    return x


def cut_along(x, dim, devices):
    dims = x.shape
    blocks = x.reshape(*dims[:dim], devices, dims[dim] // devices, *dims[dim + 1 :])
    return jnp.moveaxis(blocks, dim, 0)


def sum_at_owner(x, axis, dim):
    devices = lax.axis_size(axis)
    blocks = lax.all_to_all(cut_along(x, dim, devices), axis, 0, 0, tiled=True)
    return jnp.sum(blocks, axis=0)


def in_order(blocks, dim):
    dims = list(blocks.shape[1:])
    dims[dim] *= blocks.shape[0]
    return jnp.moveaxis(blocks, 0, dim).reshape(dims)


def copy_for_each(x, axis):
    devices = lax.axis_size(axis)
    return lax.all_to_all(jnp.broadcast_to(x[None], (devices, *x.shape)), axis, 0, 0, tiled=True)


def collect(x, axis, dim):
    return in_order(copy_for_each(x, axis), dim)


def advance(extended):
    center = extended[:, :, 1:-1]
    totals = lax.psum(jnp.sum(center * center, axis=0), "grain")
    laplacian = (
        extended[:, :, 2:]
        + extended[:, :, :-2]
        + jnp.roll(center, 1, 3)
        + jnp.roll(center, -1, 3)
        - 4.0 * center
    )
    others = totals[None] - center * center
    chemical = (
        -alpha_coef * center
        + beta_coef * center**3
        + 2.0 * gamma_coef * center * others
        - kappa_coef * laplacian
    )
    return center - time_step * chemical


def phase_tables(freqs, places, length):
    product = freqs[:, None] * places[None, :] % length
    angle = product.astype(jnp.float32) * (2.0 * math.pi / length)
    return (jnp.cos(angle), jnp.sin(angle))


def forward_rows(matrix, values):
    return jnp.einsum(
        "kq,pqc->pkc",
        matrix,
        values,
        precision=lax.Precision.HIGHEST,
        preferred_element_type=jnp.float32,
    )


def backward_rows(matrix, values):
    return jnp.einsum(
        "kq,pkc->pqc",
        matrix,
        values,
        precision=lax.Precision.HIGHEST,
        preferred_element_type=jnp.float32,
    )


def inner_transform(piece, green, row_index, col_start):
    length = piece.shape[1]
    columns = piece.shape[3]
    freqs = jnp.arange(length, dtype=jnp.int32)
    cosine, sine = phase_tables(freqs, row_index, length)
    real_part = piece[:, :, 0]
    imag_part = piece[:, :, 1]
    fwd_real = forward_rows(cosine, real_part) + forward_rows(sine, imag_part)
    fwd_imag = forward_rows(cosine, imag_part) - forward_rows(sine, real_part)
    local_green = lax.dynamic_slice_in_dim(green, col_start, columns, 1)
    scaled_real = fwd_real * local_green[None]
    scaled_imag = fwd_imag * local_green[None]
    inv_real = backward_rows(cosine, scaled_real) - backward_rows(sine, scaled_imag)
    inv_imag = backward_rows(cosine, scaled_imag) + backward_rows(sine, scaled_real)
    return jnp.stack([inv_real, inv_imag], axis=2)


def row_forward(strain, cosine, sine):
    planes, rows_here, length = strain.shape
    flat = strain.reshape(planes * rows_here, length)
    table = jnp.concatenate([cosine, -sine], axis=1)
    result = jnp.dot(
        flat, table, precision=lax.Precision.HIGHEST, preferred_element_type=jnp.float32
    )
    return result.reshape(planes, rows_here, 2, length)


def row_backward(mixed, cosine, sine):
    planes, rows_here, pair, length = mixed.shape
    flat = mixed.reshape(planes * rows_here, pair * length)
    table = jnp.concatenate([cosine, -sine], axis=0)
    result = jnp.dot(
        flat, table, precision=lax.Precision.HIGHEST, preferred_element_type=jnp.float32
    )
    return (result * (1.0 / (length * length))).reshape(planes, rows_here, length)


def local(order_params, eigen_weight, green):
    order = order_params
    for repeat in range(STEPS):
        extended = with_halo(order, (("row", 2),), 1)
        order = advance(extended)
    strain = jnp.sum(eigen_weight[:, None, None, None] * order * order, axis=0)
    length = order.shape[3]
    grains = lax.axis_size("grain")
    row_count = lax.axis_size("row")
    positions = jnp.arange(length, dtype=jnp.int32)
    cosine, sine = phase_tables(positions, positions, length)
    strain = sum_at_owner(strain, "grain", 1)
    block = strain.shape[1]
    full_rows = block * grains
    source = positions // block
    row_index = source % row_count * full_rows + source // row_count * block + positions % block
    col_start = (lax.axis_index("grain") * row_count + lax.axis_index("row")) * (
        length // (grains * row_count)
    )
    forward = row_forward(strain, cosine, sine)
    mixed_piece = inner_transform(
        lax.all_to_all(forward, ("grain", "row"), split_axis=3, concat_axis=1, tiled=True),
        green,
        row_index,
        col_start,
    )
    mixed = lax.all_to_all(mixed_piece, ("grain", "row"), split_axis=1, concat_axis=3, tiled=True)
    potential = row_backward(mixed, cosine, sine)
    potential = collect(potential, "grain", 1)
    factor = time_step * 2.0 * elastic_coef
    updated = order - factor * eigen_weight[:, None, None, None] * order * potential[None]
    return (updated, potential)


def solution(mesh):
    return jax.shard_map(
        local,
        mesh=mesh,
        in_specs=(P("grain", None, "row", None), P("grain"), P()),
        out_specs=(P("grain", None, "row", None), P(None, "row", None)),
        check_vma=False,
    )
```

profile of v0, /device:TPU:0, one launch (start us, length us, event | category | flops | bytes accessed | tf_op | source)
XLA Modules:
  0.0 708.9 jit_solution(2793407677301446103)
XLA Ops:
  7.2 12.1 %multiply_reduce_fusion.2 = (f32[4,64,1024]{2,1,0:T(8,128)}, f32[8,4,64,1024]{3,0,2,1:T(8,128)S(1)}) fusion(f32[8,4,64,1024]{3,2,1,0:T(8,128)} %param.3), kind=kLoop, calls=%fused_computation.40 | loop fusion | flops 3932160 | bytes 17825792 | tf_op jit(solution)/shard_map/reduce_sum | solution.py:61
  19.3 3.4 copy-done.2
  22.7 3.6 collective-permute-start
  26.5 13.3 %fusion.165 = (f32[8,4,64,1023]{3,0,2,1:T(8,128)}, f32[8,4,64,1023]{3,0,2,1:T(8,128)}) fusion(f32[8,4,64,1024]{3,0,2,1:T(8,128)} %copy-done.2), kind=kLoop, calls=%fused_computation.169 | loop fusion | bytes 33521664 | tf_op jit(solution)/shard_map/jit(_roll_static)/slice | solution.py:65
  39.8 1.9 fusion.164
  41.7 77.4 %all-reduce.4.cloned.1.call-done = f32[4,64,1024]{2,1,0:T(8,128)} async-done(((f32[4,64,1024]{2,1,0:T(8,128)}), f32[4,64,1024]{2,1,0:T(8,128)}) %all-reduce.4.cloned.1.call-update) | async-done | bytes 1048592 | tf_op jit(solution)/shard_map/psum | solution.py:61
  119.2 18.9 %multiply_reduce_fusion.1 = (f32[4,64,1024]{2,1,0:T(8,128)}, f32[8,4,64,1024]{3,0,2,1:T(8,128)S(1)}) fusion(f32[8,4,64,1024]{3,0,2,1:T(8,128)} %copy-done.2, f32[8,4,64,1]{3,0,2,1:T(8,128)S(1)} %get-tuple-element.29, f32[8,4,64,1023]{3,0,2,1:T(8,128)} %get-tuple-element.31, f32[8,4,64,1023]{3,0,2,1:T(8,128)} %get-tuple-element.30, ...), kind=kLoop, calls=%fused_computation.39 | loop fusion | flops 43778048 | bytes 35913728 | tf_op jit(solution)/shard_map/reduce_sum | solution.py:61
  138.1 3.4 copy-done.1
  142.2 13.2 %fusion.162 = (f32[8,4,64,1023]{3,0,2,1:T(8,128)}, f32[8,4,64,1023]{3,0,2,1:T(8,128)}) fusion(f32[8,4,64,1024]{3,0,2,1:T(8,128)} %copy-done.1), kind=kLoop, calls=%fused_computation.166 | loop fusion | bytes 33521664 | tf_op jit(solution)/shard_map/jit(_roll_static)/slice | solution.py:65
  157.3 74.3 %all-reduce.6.cloned.1.call-done = f32[4,64,1024]{2,1,0:T(8,128)} async-done(((f32[4,64,1024]{2,1,0:T(8,128)}), f32[4,64,1024]{2,1,0:T(8,128)}) %all-reduce.6.cloned.1.call-update) | async-done | bytes 1048592 | tf_op jit(solution)/shard_map/psum | solution.py:61
  231.6 18.9 %multiply_reduce_fusion = (f32[4,64,1024]{2,1,0:T(8,128)}, f32[8,4,64,1024]{3,0,2,1:T(8,128)S(1)}) fusion(f32[8,4,64,1024]{3,0,2,1:T(8,128)} %copy-done.1, f32[8,4,64,1]{3,0,2,1:T(8,128)S(1)} %get-tuple-element.21, f32[8,4,64,1023]{3,0,2,1:T(8,128)} %get-tuple-element.23, f32[8,4,64,1023]{3,0,2,1:T(8,128)} %get-tuple-element.22, ...), kind=kLoop, calls=%fused_computation.38 | loop fusion | flops 43778048 | bytes 35913728 | tf_op jit(solution)/shard_map/reduce_sum | solution.py:61
  250.5 3.4 copy-done
  254.6 13.1 %fusion.159 = (f32[8,4,64,1023]{3,0,2,1:T(8,128)}, f32[8,4,64,1023]{3,0,2,1:T(8,128)}) fusion(f32[8,4,64,1024]{3,0,2,1:T(8,128)} %copy-done), kind=kLoop, calls=%fused_computation.163 | loop fusion | bytes 33521664 | tf_op jit(solution)/shard_map/jit(_roll_static)/slice | solution.py:65
  267.7 1.9 fusion.158
  269.6 74.4 %all-reduce.8.cloned.1.call-done = f32[4,64,1024]{2,1,0:T(8,128)} async-done(((f32[4,64,1024]{2,1,0:T(8,128)}), f32[4,64,1024]{2,1,0:T(8,128)}) %all-reduce.8.cloned.1.call-update) | async-done | bytes 1048592 | tf_op jit(solution)/shard_map/psum | solution.py:61
  344.0 21.7 %fusion = (f32[4,64,1024]{2,1,0:T(8,128)S(1)}, f32[8,4,64,1024]{3,0,2,1:T(8,128)}) fusion(f32[8]{0:T(128)S(1)} %copy-done.6, f32[8,4,64,1024]{3,0,2,1:T(8,128)} %copy-done, f32[8,4,64,1]{3,0,2,1:T(8,128)S(1)} %get-tuple-element.15, f32[8,4,64,1023]{3,0,2,1:T(8,128)} %get-tuple-element.17, f32[8,4,64,1023]{3,0,2,1:T(8,128)} %get-tuple-element.16, ...), kind=kLoop, calls=%fused_computation.1 | loop fusion | flops 45875200 | bytes 35913760 | tf_op jit(solution)/shard_map/reduce_sum | solution.py:147
  366.8 3.8 all-to-all-start
  370.6 16.5 %sine_negate_fusion = (f32[1024,1024]{1,0:T(8,128)S(1)}, f32[1024,1024]{1,0:T(8,128)S(1)}) fusion(), kind=kLoop, calls=%fused_computation.73 | loop fusion | flops 15728640 | bytes 8388608 | tf_op jit(solution)/shard_map/neg | solution.py:125
  387.1 1.9 copy-done.3
  390.3 4.0 maximum_bitcast_fusion
  394.3 9.2 %copy.55 = f32[2048,1024]{1,0:T(8,128)} copy(f32[2048,1024]{0,1:T(8,128)} %maximum_bitcast_fusion) | data formatting | bytes 16777216 | tf_op jit(solution)/shard_map/dot_general | solution.py:126
  403.6 10.4 %fusion.101 = f32[4,8,2,1024]{3,1,2,0:T(8,128)S(1)} fusion(f32[2,1024,1024,1]{2,1,0,3:T(8,128)} %bitcast.112, f32[4,8,1024]{2,1,0:T(8,128)S(1)} %reduce_sum.49), kind=kOutput, calls=%fused_computation.97 | convolution fusion | flops 805306368 | bytes 8781824 | tf_op jit(solution)/shard_map/dot_general | solution.py:126
  413.9 4.3 copy.56
  418.2 7.8 %reshape.82 = f32[128,1,512]{2,1,0:T(1,128)} reshape(f32[1024,4,2,8]{3,2,1,0:T(2,128)} %bitcast.113) | data formatting | bytes 524288
  426.0 10.5 %all-to-all-start.1 = ((f32[128,1,512]{2,1,0:T(1,128)}), f32[128,1,512]{2,1,0:T(1,128)S(1)}, u32[]{:S(2)}, u32[]{:S(2)}) async-start(f32[128,1,512]{2,1,0:T(1,128)} %reshape.82), calls=%async_computation.1 | async-start | bytes 524288 | tf_op jit(solution)/shard_map/all_to_all | solution.py:163
  437.9 9.3 %all-to-all-done.1 = f32[128,1,512]{2,1,0:T(1,128)S(1)} async-done(((f32[128,1,512]{2,1,0:T(1,128)}), f32[128,1,512]{2,1,0:T(1,128)S(1)}, u32[]{:S(2)}, u32[]{:S(2)}) %all-to-all-start.1) | async-done | bytes 262176 | tf_op jit(solution)/shard_map/all_to_all | solution.py:163
  449.0 7.7 %reshape.83 = f32[1024,4,2,8]{3,2,1,0:T(2,128)} reshape(f32[128,512]{1,0:T(8,128)S(1)} %reduce) | data formatting | bytes 524288
  456.6 6.6 copy.80
  463.2 4.0 all_to_all.34
  467.2 19.1 %fusion.36 = f32[4,8,1024]{2,1,0:T(8,128)S(1)} fusion(s32[1024]{0:T(1024)S(1)} %fusion.111, f32[4,1024,2,8]{1,3,2,0:T(8,128)S(1)} %all_to_all.34), kind=kOutput, calls=%fused_computation.58 | convolution fusion | flops 417333248 | bytes 266240 | tf_op jit(solution)/shard_map/kq,pqc->pkc/dot_general | solution.py:86
  486.3 19.3 %fusion.38 = f32[4,8,1024]{2,1,0:T(8,128)S(1)} fusion(s32[1024]{0:T(1024)S(1)} %fusion.111, f32[4,1024,2,8]{1,3,2,0:T(8,128)S(1)} %all_to_all.34), kind=kOutput, calls=%fused_computation.60 | convolution fusion | flops 417333248 | bytes 266240 | tf_op jit(solution)/shard_map/kq,pqc->pkc/dot_general | solution.py:86
  505.7 19.0 %fusion.86 = f32[4,1024,8]{1,2,0:T(8,128)S(1)} fusion(f32[4,8,1024]{2,1,0:T(8,128)S(1)} %fusion.36, s32[1024]{0:T(1024)S(1)} %fusion.111, f32[4,1024,2,8]{1,3,2,0:T(8,128)S(1)} %all_to_all.34, f32[1024,8]{0,1:T(8,128)S(1)} %copy.61), kind=kOutput, calls=%fused_computation.88 | convolution fusion | flops 417398784 | bytes 430080 | tf_op jit(solution)/shard_map/kq,pqc->pkc/dot_general | solution.py:86
  524.7 18.3 %fusion.34 = f32[4,8,1024]{2,1,0:T(8,128)S(1)} fusion(f32[4,1024,8]{1,2,0:T(8,128)S(1)} %fusion.86, s32[1024]{0:T(1024)S(1)} %fusion.111), kind=kOutput, calls=%fused_computation.56 | convolution fusion | flops 417333248 | bytes 266240 | tf_op jit(solution)/shard_map/kq,pkc->pqc/dot_general | solution.py:96
  543.0 19.0 %fusion.71 = f32[4,1024,8]{1,2,0:T(8,128)S(1)} fusion(f32[4,8,1024]{2,1,0:T(8,128)S(1)} %fusion.38, s32[1024]{0:T(1024)S(1)} %fusion.111, f32[4,1024,2,8]{1,3,2,0:T(8,128)S(1)} %all_to_all.34, f32[1024,8]{0,1:T(8,128)S(1)} %copy.61), kind=kOutput, calls=%fused_computation.83 | convolution fusion | flops 417398784 | bytes 430080 | tf_op jit(solution)/shard_map/kq,pqc->pkc/dot_general | solution.py:86
  562.0 18.1 %fusion.32 = f32[4,8,1024]{2,1,0:T(8,128)S(1)} fusion(f32[4,1024,8]{1,2,0:T(8,128)S(1)} %fusion.71, s32[1024]{0:T(1024)S(1)} %fusion.111), kind=kOutput, calls=%fused_computation.54 | convolution fusion | flops 417333248 | bytes 266240 | tf_op jit(solution)/shard_map/kq,pkc->pqc/dot_general | solution.py:96
  580.1 17.8 %fusion.77 = f32[4,1024,1,8]{1,3,0,2:T(8,128)S(1)} fusion(f32[4,8,1024]{2,1,0:T(8,128)S(1)} %fusion.34, f32[4,1024,8]{1,2,0:T(8,128)S(1)} %fusion.71, s32[1024]{0:T(1024)S(1)} %fusion.111), kind=kOutput, calls=%fused_computation.85 | convolution fusion | flops 417366016 | bytes 397312 | tf_op jit(solution)/shard_map/kq,pkc->pqc/dot_general | solution.py:96
  598.0 18.1 %fusion.92 = f32[4,1024,1,8]{1,3,0,2:T(8,128)S(1)} fusion(f32[4,8,1024]{2,1,0:T(8,128)S(1)} %fusion.32, f32[4,1024,8]{1,2,0:T(8,128)S(1)} %fusion.86, s32[1024]{0:T(1024)S(1)} %fusion.111), kind=kOutput, calls=%fused_computation.90 | convolution fusion | flops 417366016 | bytes 397312 | tf_op jit(solution)/shard_map/kq,pkc->pqc/dot_general | solution.py:96
  616.1 3.0 copy.62
  619.1 6.3 reshape.84
  625.4 15.5 %all_to_all.43 = f32[128,1,512]{2,1,0:T(1,128)S(1)} all-to-all(f32[128,1,512]{2,1,0:T(1,128)S(1)} %reshape.84), channel_id=1, replica_groups=mesh['grain'=8,'row'=16] {'grain','row'}, dimensions={0} | all-to-all | bytes 524288 | tf_op jit(solution)/shard_map/all_to_all | solution.py:168
  642.2 6.3 reshape.85
  648.5 6.6 copy.79
  655.0 4.0 reshape.77
  659.0 7.2 %fusion.98 = f32[4,8,1024]{2,1,0:T(8,128)S(1)} fusion(f32[32,2048]{1,0:T(8,128)S(1)} %reshape.77, f32[1024,1024]{1,0:T(8,128)} %copy-done.3, f32[1024,1024]{1,0:T(8,128)} %copy-done.4), kind=kOutput, calls=%fused_computation.92 | convolution fusion | flops 807436288 | bytes 8781824 | tf_op jit(solution)/shard_map/dot_general | solution.py:136
  667.4 3.9 all-to-all-start.3
  671.2 17.6 %all-to-all-done.3 = f32[8,4,8,1024]{3,2,1,0:T(8,128)S(1)} async-done(((f32[8,4,8,1024]{3,2,1,0:T(8,128)}), f32[8,4,8,1024]{3,2,1,0:T(8,128)S(1)}, u32[]{:S(2)}, u32[]{:S(2)}) %all-to-all-start.3) | async-done | bytes 1048608 | tf_op jit(solution)/shard_map/all_to_all | solution.py:52
  689.0 4.7 multiply_subtract_fusion
  693.7 8.3 %copy.66 = f32[8,4,64,1024]{3,2,1,0:T(8,128)} copy(f32[8,4,64,1024]{3,0,2,1:T(8,128)S(1)} %multiply_subtract_fusion) | data formatting | bytes 16777216
  (44 shorter events, 11.5 us)
Async XLA Ops:
  7.2 112.0 %all-reduce.4.cloned.1.call-start = ((), (), s32[]{:S(2)}) async-start(), calls=%async_computation.4 | async-start | bytes 2097152 | tf_op jit(solution)/shard_map/psum | solution.py:61
  19.3 3.4 copy-start.2
  22.7 19.0 %collective-permute-start = (f32[8,4,1,1024]{3,0,2,1:T(8,128)S(1)}, f32[8,4,1,1024]{3,0,2,1:T(8,128)S(1)}, u32[]{:S(2)}, u32[]{:S(2)}) collective-permute-start(f32[8,4,1,1024]{3,0,2,1:T(8,128)S(1)} %get-tuple-element.26), channel_id=1, source_target_pairs={{1,0},{2,1},{3,2},{4,3},{5,4},{6,5},{7,6},{8,7},{9,8},{10,9},{11,1... | collective-permute-start | bytes 393224 | tf_op jit(solution)/shard_map/ppermute | solution.py:27
  26.3 15.4 %collective-permute-start.1 = (f32[8,4,1,1024]{3,0,2,1:T(8,128)S(1)}, f32[8,4,1,1024]{3,0,2,1:T(8,128)S(1)}, u32[]{:S(2)}, u32[]{:S(2)}) collective-permute-start(f32[8,4,1,1024]{3,0,2,1:T(8,128)S(1)} %get-tuple-element.27), channel_id=1, source_target_pairs={{0,1},{1,2},{2,3},{3,4},{4,5},{5,6},{6,7},{7,8},{8,9},{9,10},{10,1... | collective-permute-start | bytes 393224 | tf_op jit(solution)/shard_map/ppermute | solution.py:26
  26.3 205.3 %all-reduce.6.cloned.1.call-start = ((), (), s32[]{:S(2)}) async-start(), calls=%async_computation.5 | async-start | bytes 2097152 | tf_op jit(solution)/shard_map/psum | solution.py:61
  138.1 3.4 copy-start.1
  141.5 15.7 %collective-permute-start.2 = (f32[8,4,1,1024]{3,0,2,1:T(8,128)S(1)}, f32[8,4,1,1024]{3,0,2,1:T(8,128)S(1)}, u32[]{:S(2)}, u32[]{:S(2)}) collective-permute-start(f32[8,4,1,1024]{3,0,2,1:T(8,128)S(1)} %get-tuple-element.18), channel_id=1, source_target_pairs={{1,0},{2,1},{3,2},{4,3},{5,4},{6,5},{7,6},{8,7},{9,8},{10,9},{11,1... | collective-permute-start | bytes 393224 | tf_op jit(solution)/shard_map/ppermute | solution.py:27
  141.6 15.6 %collective-permute-start.3 = (f32[8,4,1,1024]{3,0,2,1:T(8,128)S(1)}, f32[8,4,1,1024]{3,0,2,1:T(8,128)S(1)}, u32[]{:S(2)}, u32[]{:S(2)}) collective-permute-start(f32[8,4,1,1024]{3,0,2,1:T(8,128)S(1)} %get-tuple-element.19), channel_id=1, source_target_pairs={{0,1},{1,2},{2,3},{3,4},{4,5},{5,6},{6,7},{7,8},{8,9},{9,10},{10,1... | collective-permute-start | bytes 393224 | tf_op jit(solution)/shard_map/ppermute | solution.py:26
  142.1 201.9 %all-reduce.8.cloned.1.call-start = ((), (), s32[]{:S(2)}) async-start(), calls=%async_computation.6 | async-start | bytes 2097152 | tf_op jit(solution)/shard_map/psum | solution.py:61
  250.5 3.4 copy-start
  254.0 15.6 %collective-permute-start.4 = (f32[8,4,1,1024]{3,0,2,1:T(8,128)S(1)}, f32[8,4,1,1024]{3,0,2,1:T(8,128)S(1)}, u32[]{:S(2)}, u32[]{:S(2)}) collective-permute-start(f32[8,4,1,1024]{3,0,2,1:T(8,128)S(1)} %get-tuple-element.12), channel_id=1, source_target_pairs={{1,0},{2,1},{3,2},{4,3},{5,4},{6,5},{7,6},{8,7},{9,8},{10,9},{11,1... | collective-permute-start | bytes 393224 | tf_op jit(solution)/shard_map/ppermute | solution.py:27
  254.0 15.6 %collective-permute-start.5 = (f32[8,4,1,1024]{3,0,2,1:T(8,128)S(1)}, f32[8,4,1,1024]{3,0,2,1:T(8,128)S(1)}, u32[]{:S(2)}, u32[]{:S(2)}) collective-permute-start(f32[8,4,1,1024]{3,0,2,1:T(8,128)S(1)} %get-tuple-element.13), channel_id=1, source_target_pairs={{0,1},{1,2},{2,3},{3,4},{4,5},{5,6},{6,7},{7,8},{8,9},{9,10},{10,1... | collective-permute-start | bytes 393224 | tf_op jit(solution)/shard_map/ppermute | solution.py:26
  267.7 76.3 %copy-start.6 = (f32[8]{0:T(128)S(1)}, f32[8]{0:T(128)}, u32[]{:S(2)}) copy-start(f32[8]{0:T(128)} %param.4) | copy-start | bytes 100
  366.8 36.7 %all-to-all-start = ((f32[8,4,8,1024]{3,2,1,0:T(8,128)}), f32[8,4,8,1024]{3,2,1,0:T(8,128)S(1)}, u32[]{:S(2)}, u32[]{:S(2)}) async-start(f32[8,4,8,1024]{3,2,1,0:T(8,128)} %copy.54), calls=%async_computation | async-start | bytes 2097152 | tf_op jit(solution)/shard_map/all_to_all | solution.py:40
  387.1 1.9 copy-start.3
  387.1 3.2 copy-start.4
  426.0 21.2 %all-to-all-start.1 = ((f32[128,1,512]{2,1,0:T(1,128)}), f32[128,1,512]{2,1,0:T(1,128)S(1)}, u32[]{:S(2)}, u32[]{:S(2)}) async-start(f32[128,1,512]{2,1,0:T(1,128)} %reshape.82), calls=%async_computation.1 | async-start | bytes 524288 | tf_op jit(solution)/shard_map/all_to_all | solution.py:163
  667.4 21.5 %all-to-all-start.3 = ((f32[8,4,8,1024]{3,2,1,0:T(8,128)}), f32[8,4,8,1024]{3,2,1,0:T(8,128)S(1)}, u32[]{:S(2)}, u32[]{:S(2)}) async-start(f32[8,4,8,1024]{3,2,1,0:T(8,128)} %broadcast_in_dim.5), calls=%async_computation.3 | async-start | bytes 2097152 | tf_op jit(solution)/shard_map/all_to_all | solution.py:52
  689.0 4.7 copy-start.5
Sparse Core Ops, SparseCore 0:
  26.4 92.6 all-reduce.3
  142.3 89.2 all-reduce.5
  254.7 89.2 all-reduce.7
where the time goes:
time: 716 us; the launch traced here: 709 us
  waiting for transfers between devices  253 us (35%)
  matrix products  166 us (23%)
  local copies, waits for them, and re-layouts  137 us (19%)
  other arithmetic  99.4 us (14%)
  starting transfers between devices  23.1 us (3%)
  blocking collectives  15.5 us (2%)
  between operations  14.6 us (2%)
    psum x3, waiting for transfers between devices, advance(): totals = lax.psum(jnp.sum(center * center, axis=0), 'grain')  226 us
    dot_general x4, matrix products, forward_rows(): jnp.einsum('kq,pqc->pkc', matrix, values, precision=lax.Precision.HIGHEST...  76.4 us
    dot_general x4, matrix products, backward_rows(): jnp.einsum('kq,pkc->pqc', matrix, values, precision=lax.Precision.HIGHEST...  72.3 us
    reduce_sum x3, other arithmetic, advance(): totals = lax.psum(jnp.sum(center * center, axis=0), 'grain')  50 us
    unnamed x19, local copies, waits for them, and re-layouts  49.7 us
    slice x6, local copies, waits for them, and re-layouts, advance(): jnp.roll(center, 1, 3)  45.3 us
    reduce_sum x1, other arithmetic, local(): strain = jnp.sum(eigen_weight[:, None, None, None] * order * order, axis=0)  21.7 us
    all_to_all x1, waiting for transfers between devices, copy_for_each(): lax.all_to_all(jnp.broadcast_to(x[None], (devices, *x.shape)), axis, 0, 0...  17.6 us
  transfers between devices with their start and end apart: 12, of which 5 were waited for; matrix products, arithmetic and copies ran while one was open for 11% of the time, Pallas kernels for 0%

commit v1 on v0

v1 whole, which is shorter than its diff:
```python
import math

import jax
import jax.numpy as jnp
import numpy as np
from jax import lax
from jax.experimental import pallas as pl
from jax.experimental.pallas import tpu as pltpu
from jax.sharding import Mesh, PartitionSpec as P

GRAINS = 8
PLANES = 4
ROWS = 64
N = 1024
HALF = 32
STEPS = 3

DT = 0.1
ALPHA = 1.0
BETA = 1.0
GAMMA = 0.25
KAPPA = 1.0
ELASTIC = 2.0

C_ONE = 1.0 + DT * ALPHA - 4.0 * DT * KAPPA
C_TOTAL = 2.0 * DT * GAMMA
C_CUBE = DT * BETA - 2.0 * DT * GAMMA
C_NEAR = DT * KAPPA
FACTOR = DT * 2.0 * ELASTIC

ROW_AXES = ("y", "xl", "c")
HIGH = lax.Precision.HIGHEST
F32 = jnp.float32


def make_tables():
    two_pi = 2.0 * np.pi
    u = np.arange(128)
    low = np.arange(8).reshape(2, 4)
    place = 128 * np.arange(8)[:, None] + u[None, :]
    angle = two_pi * ((low[:, :, None, None] * place) % N) / N
    line = np.stack([np.cos(angle), np.sin(angle)], axis=1)
    high = np.arange(64)
    angle = two_pi * ((high[:, None] * u[None, :]) % 128) / 128
    plain = np.concatenate([np.cos(angle), np.sin(angle)], axis=1)
    special = plain.copy()
    special[0, 128:] = -((-1.0) ** u)
    fwd = np.stack([np.stack([special, plain]), np.stack([plain, plain])])
    scale = np.full((2, 2, 64, 1), 2.0)
    scale[0, 0, 0, 0] = 1.0
    bwd = fwd * scale / (N * N)
    r = np.arange(64)
    angle = two_pi * (np.arange(16)[:, None] * r[None, :]) / N
    sign = np.concatenate([-np.ones(64), np.ones(64)])
    cosine = np.tile(np.cos(angle), (1, 2))
    sine = np.tile(np.sin(angle), (1, 2)) * sign
    twiddle = np.stack([cosine, sine])
    angle = two_pi * ((r[:, None] * r[None, :]) % 64) / 64
    c, s = np.cos(angle), np.sin(angle)
    col = np.stack([np.block([[c, -s], [s, c]]), np.block([[c, s], [-s, c]])])
    return [x.astype(np.float32) for x in (line, fwd, bwd, twiddle, col)]


LINE, FWD, BWD, TWIDDLE, COL = make_tables()


def square_kernel(meta, eta, total, top, bottom):
    for rg in range(HALF // 8):
        acc = None
        for g in range(GRAINS):
            e = eta[g, 0, 8 * rg : 8 * rg + 8, :]
            acc = e * e if acc is None else acc + e * e
        total[0, 8 * rg : 8 * rg + 8, :] = acc
    for g in range(GRAINS):
        top[0, g : g + 1, :] = eta[g, 0, 0:1, :]
        bottom[0, g : g + 1, :] = eta[g, 0, HALF - 1 : HALF, :]


def step_body(load, weight, total, above, below, out, sums, edges):
    row = lax.broadcasted_iota(jnp.int32, (8, N), 0)
    for rg in range(HALF // 8):
        base = 8 * rg
        coef = C_ONE - C_TOTAL * total[0, base : base + 8, :]
        acc = jnp.zeros((8, N), F32)
        for g in range(GRAINS):
            e = load(g, base, 8)
            before = above[0, g : g + 1, :] if rg == 0 else load(g, base - 1, 1)
            after = below[0, g : g + 1, :] if base + 8 == HALF else load(g, base + 8, 1)
            up = jnp.where(row == 0, before, pltpu.roll(e, 1, 0))
            down = jnp.where(row == 7, after, pltpu.roll(e, 7, 0))
            near = (up + down) + (pltpu.roll(e, 1, 1) + pltpu.roll(e, N - 1, 1))
            new = e * (coef - C_CUBE * (e * e)) + C_NEAR * near
            out[0, g, base : base + 8, :] = new
            if edges is not None:
                top, bottom = edges
                if rg == 0:
                    top[0, g : g + 1, :] = new[0:1]
                if base + 8 == HALF:
                    bottom[0, g : g + 1, :] = new[7:8]
                acc = acc + new * new
            else:
                acc = acc + weight[g] * (new * new)
        sums[0, base : base + 8, :] = acc


def first_step_kernel(meta, eta, total, above, below, out, sums, top, bottom):
    step_body(lambda g, r, n: eta[g, 0, r : r + n, :], None, total, above, below, out, sums, (top, bottom))


def step_kernel(eta, total, above, below, out, sums, top, bottom):
    step_body(lambda g, r, n: eta[0, g, r : r + n, :], None, total, above, below, out, sums, (top, bottom))


def last_step_kernel(weight, eta, total, above, below, out, sums):
    step_body(lambda g, r, n: eta[0, g, r : r + n, :], weight, total, above, below, out, sums, None)


def final_body(weight, eta, pot, out, pot_out):
    for rg in range(HALF // 8):
        base = 8 * rg
        v = pot[0, base : base + 8, :]
        pot_out[0, base : base + 8, :] = v
        for g in range(GRAINS):
            e = eta[0, g, base : base + 8, :]
            out[g, 0, base : base + 8, :] = e - (FACTOR * weight[g]) * (e * v)


def final_first_kernel(meta, weight, eta, pot, out, pot_out):
    final_body(weight, eta, pot, out, pot_out)


def final_second_kernel(meta, weight, eta, pot, _out, _pot, out, pot_out):
    final_body(weight, eta, pot, out, pot_out)


def nt(a, b):
    return lax.dot_general(a, b, (((1,), (1,)), ((), ())), precision=HIGH, preferred_element_type=F32)


def nn(a, b):
    return lax.dot_general(a, b, (((1,), (0,)), ((), ())), precision=HIGH, preferred_element_type=F32)


def row_forward_kernel(meta, s0, s1, line, fwd, out):
    for l1 in range(4):
        real, imag = [], []
        for src in (s0, s1):
            a = b = None
            for t in range(8):
                x = src[:, 128 * t : 128 * t + 128]
                p = x * line[0, 0, l1, t : t + 1, :]
                q = x * line[0, 1, l1, t : t + 1, :]
                a = p if a is None else a + p
                b = q if b is None else b + q
            real.append(a)
            imag.append(-b)
        a = jnp.concatenate(real, axis=0)
        b = jnp.concatenate(imag, axis=0)
        pairs = jnp.concatenate([jnp.concatenate([a, b], axis=1), jnp.concatenate([b, -a], axis=1)], axis=0)
        y = nt(fwd[0, 0 if l1 == 0 else 1], pairs)
        j, p = divmod(l1, 2)
        out[8 * j : 8 * j + 8, 8 * p : 8 * p + 8, :] = y.reshape(8, 8, 128)


def dft16(z, turned, sign):
    plus = [None] + [z[t] + z[16 - t] for t in range(1, 8)]
    minus = [None] + [turned[t] - turned[16 - t] for t in range(1, 8)]
    out = [None] * 16
    for k in range(9):
        even = z[0] + z[8] if k % 2 == 0 else z[0] - z[8]
        for t in range(1, 8):
            c = math.cos(2.0 * math.pi * (k * t % 16) / 16)
            if abs(c) > 1e-9:
                even = even + c * plus[t]
        odd = None
        for t in range(1, 8):
            s = math.sin(2.0 * math.pi * (k * t % 16) / 16)
            if abs(s) > 1e-9:
                term = s * minus[t]
                odd = term if odd is None else odd + term
        if odd is None:
            out[k] = even
        else:
            out[k] = even + sign * odd
            out[16 - k] = even - sign * odd
    return out


def column_kernel(recv, masks, green, twiddle, col, out):
    sign = jnp.where(lax.broadcasted_iota(jnp.int32, (1, 128), 1) < 64, -1.0, 1.0).astype(F32)
    keep = masks[0:16, :]
    extra = masks[16:24, :]
    z = []
    for t in range(16):
        x = recv[t]
        z.append(jnp.concatenate([x * keep, x[0:8] * extra], axis=0))
    turned = [pltpu.roll(x, 64, 1) * sign for x in z]
    y = dft16(z, turned, -1.0)
    y = [v * twiddle[0, k : k + 1, :] - pltpu.roll(v, 64, 1) * twiddle[1, k : k + 1, :] for k, v in enumerate(y)]
    f = nn(jnp.concatenate(y, axis=0), col[0])
    g = []
    for k in range(16):
        v = f[24 * k : 24 * k + 24] * green[k]
        g.append(v[0:8] + v[16:24])
        g.append(v[8:16])
    f = nn(jnp.concatenate(g, axis=0), col[1])
    y = [f[16 * k : 16 * k + 16] for k in range(16)]
    y = [v * twiddle[0, k : k + 1, :] + pltpu.roll(v, 64, 1) * twiddle[1, k : k + 1, :] for k, v in enumerate(y)]
    turned = [pltpu.roll(x, 64, 1) * sign for x in y]
    y = dft16(y, turned, 1.0)
    for t in range(16):
        out[t] = y[t]


def row_backward_kernel(meta, recv, line, bwd, out0, out1):
    real, imag = [], []
    for l1 in range(4):
        j, p = divmod(l1, 2)
        v = recv[8 * j : 8 * j + 8, 8 * p : 8 * p + 8, :].reshape(64, 128)
        y = nn(v.T, bwd[0, 0 if l1 == 0 else 1])
        real.append(y[0:64, 0:128] - y[64:128, 128:256])
        imag.append(y[0:64, 128:256] + y[64:128, 0:128])
    for t in range(8):
        acc = None
        for l1 in range(4):
            v = real[l1] * line[0, 0, l1, t : t + 1, :] - imag[l1] * line[0, 1, l1, t : t + 1, :]
            acc = v if acc is None else acc + v
        out0[:, 128 * t : 128 * t + 128] = acc[0:HALF]
        out1[:, 128 * t : 128 * t + 128] = acc[HALF:ROWS]


def shape(*dims):
    return jax.ShapeDtypeStruct(dims, F32)


CHUNK = shape(PLANES, GRAINS, HALF, N)
EDGE = shape(PLANES, GRAINS, N)
SUMS = shape(PLANES, HALF, N)


def own(k, meta):
    return (meta[0] + k) % PLANES


def input_spec(c):
    return pl.BlockSpec((GRAINS, 1, HALF, N), lambda k, meta: (0, own(k, meta), c, 0))


CHUNK_SPEC = pl.BlockSpec((1, GRAINS, HALF, N), lambda k, *_: (k, 0, 0, 0))
EDGE_SPEC = pl.BlockSpec((1, GRAINS, N), lambda k, *_: (k, 0, 0))
SUMS_SPEC = pl.BlockSpec((1, HALF, N), lambda k, *_: (k, 0, 0))
SMEM_SPEC = pl.BlockSpec(memory_space=pltpu.SMEM)


def call(kernel, name, outs, out_specs, in_specs, args, meta=None, grid=(PLANES,), aliases=None):
    spec = pltpu.PrefetchScalarGridSpec(
        num_scalar_prefetch=0 if meta is None else 1, grid=grid, in_specs=in_specs, out_specs=out_specs
    )
    args = args if meta is None else (meta, *args)
    return pl.pallas_call(
        kernel, out_shape=outs, grid_spec=spec, name=name, input_output_aliases=aliases or {}
    )(*args)


def squares(order, c, meta):
    return call(
        square_kernel, f"squares{c}", (SUMS, EDGE, EDGE), (SUMS_SPEC, EDGE_SPEC, EDGE_SPEC),
        [input_spec(c)], (order,), meta,
    )


def advance(step, c, eta, total, above, below, weight, meta):
    specs = [SUMS_SPEC, EDGE_SPEC, EDGE_SPEC]
    outs, out_specs = (CHUNK, SUMS, EDGE, EDGE), (CHUNK_SPEC, SUMS_SPEC, EDGE_SPEC, EDGE_SPEC)
    args = (eta, total, above, below)
    name = f"step{step}_{c}"
    if step == 0:
        return call(first_step_kernel, name, outs, out_specs, [input_spec(c)] + specs, args, meta)
    if step < STEPS - 1:
        return call(step_kernel, name, outs, out_specs, [CHUNK_SPEC] + specs, args)
    out, sums = call(
        last_step_kernel, name, outs[:2], out_specs[:2], [SMEM_SPEC, CHUNK_SPEC] + specs, (weight, *args)
    )
    return out, sums, None, None


def final(c, eta, pot, weight, meta, previous):
    outs = (shape(GRAINS, PLANES, ROWS, N), shape(PLANES, ROWS, N))
    out_specs = (input_spec(c), pl.BlockSpec((1, HALF, N), lambda k, meta: (own(k, meta), c, 0)))
    in_specs = [SMEM_SPEC, CHUNK_SPEC, SUMS_SPEC]
    args = (weight, eta, pot)
    if previous is None:
        return call(final_first_kernel, f"final{c}", outs, out_specs, in_specs, args, meta)
    in_specs = in_specs + [pl.BlockSpec(memory_space=pl.ANY)] * 2
    return call(
        final_second_kernel, f"final{c}", outs, out_specs, in_specs, (*args, *previous), meta,
        aliases={4: 0, 5: 1},
    )


def whole(dims):
    return pl.BlockSpec(dims, lambda i, *_: (0,) * len(dims))


LINE_SPEC = pl.BlockSpec((1, 2, 4, 8, 128), lambda i, meta: (meta[1], 0, 0, 0, 0))
TABLE_SPEC = pl.BlockSpec((1, 2, 64, 256), lambda i, meta: (meta[1], 0, 0, 0))


def row_forward(s0, s1, meta):
    return call(
        row_forward_kernel, "row_forward", shape(16, 16, 128), whole((16, 16, 128)),
        [whole((HALF, N)), whole((HALF, N)), LINE_SPEC, TABLE_SPEC], (s0, s1, LINE, FWD), meta, (1,),
    )


def column(recv, masks, green):
    return call(
        column_kernel, "column", shape(16, 16, 128), whole((16, 16, 128)),
        [whole((16, 16, 128)), whole((24, 128)), whole((16, 24, 128)), whole((2, 16, 128)), whole((2, 128, 128))],
        (recv, masks, green, TWIDDLE, COL), None, (1,),
    )


def row_backward(recv, meta):
    return call(
        row_backward_kernel, "row_backward", (shape(HALF, N), shape(HALF, N)), (whole((HALF, N)), whole((HALF, N))),
        [whole((16, 16, 128)), LINE_SPEC, TABLE_SPEC], (recv, LINE, BWD), meta, (1,),
    )


def shift(k):
    return [(i, (i + k) % PLANES) for i in range(PLANES)]


def to_owner(sums):
    acc = sums[0]
    for part in [lax.ppermute(sums[k], "z", shift(k)) for k in (2, 1, 3)]:
        acc = acc + part
    return acc


def with_partner(x):
    return x + lax.ppermute(x, "xh", [(0, 1), (1, 0)])


def to_all(x):
    parts = {k: lax.ppermute(x, "z", shift(-k)) for k in (2, 1, 3)}
    return jnp.stack([x, parts[1], parts[2], parts[3]])


def own_green(green, xh, row):
    s = jnp.arange(16, dtype=jnp.int32)
    freq = 4 * xh + 2 * (row // 8) + s // 8 + 8 * (8 * (row % 8) + s % 8)
    freq = jnp.concatenate([freq, jnp.full((1,), N // 2, jnp.int32)])
    both = jnp.concatenate([freq, (N - freq) % N])
    pick = (both[:, None] == jnp.arange(N, dtype=jnp.int32)[None, :]).astype(F32)
    cols = nt(pick, green)
    mirrored = jnp.roll(jnp.flip(cols[17:], axis=1), 1, axis=1)
    cols = 0.5 * (cols[:17] + mirrored)
    cols = cols.reshape(17, 64, 16).transpose(2, 0, 1)
    cols = jnp.concatenate([cols, cols], axis=2)
    return jnp.pad(cols, ((0, 0), (0, 7), (0, 0)))


def own_masks(xh, row):
    special = jnp.logical_and(xh == 0, row == 0)
    line = lax.broadcasted_iota(jnp.int32, (24, 128), 0)
    imag = lax.broadcasted_iota(jnp.int32, (24, 128), 1) >= 64
    keep = jnp.where(jnp.logical_and(special, jnp.logical_and(line == 0, imag)), 0.0, 1.0)
    extra = jnp.where(jnp.logical_and(special, jnp.logical_and(line == 16, imag)), 1.0, 0.0)
    return jnp.where(line < 16, keep, extra).astype(F32)


def local(order_params, eigen_weight, green):
    xh = lax.axis_index("xh")
    row = lax.axis_index(ROW_AXES)
    meta = jnp.stack([lax.axis_index("z"), xh]).astype(jnp.int32)
    row_count = 16
    up = [(i, (i + 1) % row_count) for i in range(row_count)]
    down = [(j, i) for i, j in up]
    chunks = (0, 1)

    eta = [order_params, order_params]
    sums, top, bottom = [None] * 2, [None] * 2, [None] * 2
    for c in chunks:
        sums[c], top[c], bottom[c] = squares(order_params, c, meta)
    own_cols = own_green(green, xh, row)
    masks = own_masks(xh, row)
    for step in range(STEPS):
        before = lax.ppermute(bottom[1], ROW_AXES, up)
        after = lax.ppermute(top[0], ROW_AXES, down)
        above, below = (before, bottom[0]), (top[1], after)
        totals = [to_all(with_partner(to_owner(sums[c]))) for c in chunks]
        for c in chunks:
            eta[c], sums[c], top[c], bottom[c] = advance(
                step, c, eta[c], totals[c], above[c], below[c], eigen_weight, meta
            )
    strain = [with_partner(to_owner(sums[c])) for c in chunks]
    spectrum = row_forward(strain[0], strain[1], meta)
    spectrum = lax.all_to_all(spectrum, ROW_AXES, 0, 0, tiled=True)
    mixed = column(spectrum, masks, own_cols)
    mixed = lax.all_to_all(mixed, ROW_AXES, 0, 0, tiled=True)
    pots = row_backward(mixed, meta)
    pots = [to_all(with_partner(p)) for p in pots]
    result = None
    for c in chunks:
        result = final(c, eta[c], pots[c], eigen_weight, meta, result)
    return tuple(result)


def solution(mesh):
    fine = Mesh(mesh.devices.reshape(4, 2, 4, 2, 2), ("z", "xh", "y", "xl", "c"))
    field = P(("z", "xh"), None, ROW_AXES, None)
    return jax.shard_map(
        local,
        mesh=fine,
        in_specs=(field, P(("z", "xh")), P()),
        out_specs=(field, P(None, ROW_AXES, None)),
        check_vma=False,
    )
```

time: 716 us -> 251 us (0.35)
  waiting for transfers between devices: 253 us -> 38.1 us
  matrix products: 166 us -> 4.43 us
  local copies, waits for them, and re-layouts: 137 us -> 13.3 us
  other arithmetic: 99.4 us -> 19 us
  Pallas kernels: 0 us -> 69.7 us
  starting transfers between devices: 23.1 us -> 92.7 us
  between operations: 14.6 us -> 0.94 us
    psum x3 -> x0, waiting for transfers between devices: 226 us -> none  [advance(): totals = lax.psum(jnp.sum(center * center, axis=0), 'grain')]
    dot_general x10 -> x1, matrix products: 166 us -> 4.43 us  [nt(): lax.dot_general(a, b, (((1,), (1,)), ((), ())), precision=HIGH, preferred...]
    ppermute x6 -> x64, starting transfers between devices: 4.71 us -> 89.2 us  [the longest x24 36.2 us: to_owner(): lax.ppermute(sums[k], 'z', shift(k))]
    reduce_sum x5 -> x0, other arithmetic: 71.7 us -> none  [the longest x3 50 us: advance(): totals = lax.psum(jnp.sum(center * center, axis=0), 'grain')]
    pallas_call x0 -> x13, Pallas kernels: none -> 69.7 us  [call(): pl.pallas_call(kernel, out_shape=outs, grid_spec=spec, name=name, input_o...]
    slice x9 -> x2, local copies, waits for them, and re-layouts: 45.3 us -> 0.1 us  [own_green(): mirrored = jnp.roll(jnp.flip(cols[17:], axis=1), 1, axis=1)]
    unnamed x19 -> x22, local copies, waits for them, and re-layouts: 49.7 us -> 5.27 us
    ppermute x6 -> x64, waiting for transfers between devices: 0.02 us -> 33.4 us  [the longest x24 12.6 us: to_owner(): lax.ppermute(sums[k], 'z', shift(k))]
  transfers between devices with their start and end apart: 12 -> 65, of which waited for: 5 -> 20; matrix products, arithmetic and copies ran while one was open for 11% -> 12% of each run, Pallas kernels for 0% -> 20%
where the time goes in v1:
time: 251 us; the launch traced here: 249 us
  starting transfers between devices  92.7 us (37%)
  Pallas kernels  69.7 us (28%)
  waiting for transfers between devices  38.1 us (15%)
  other arithmetic  19 us (8%)
  local copies, waits for them, and re-layouts  13.3 us (5%)
  blocking collectives  10.9 us (4%)
  matrix products  4.43 us (2%)
    pallas_call x13, Pallas kernels, call(): pl.pallas_call(kernel, out_shape=outs, grid_spec=spec, name=name, input_o...  69.7 us
    ppermute x24, starting transfers between devices, to_owner(): lax.ppermute(sums[k], 'z', shift(k))  36.2 us
    ppermute x24, starting transfers between devices, to_all(): parts = {k: lax.ppermute(x, 'z', shift(-k)) for k in (2, 1, 3)}  30.3 us
    ppermute x10, starting transfers between devices, with_partner(): return x + lax.ppermute(x, 'xh', [(0, 1), (1, 0)])  18.2 us
    ppermute x24, waiting for transfers between devices, to_owner(): lax.ppermute(sums[k], 'z', shift(k))  12.6 us
    ppermute x10, waiting for transfers between devices, with_partner(): return x + lax.ppermute(x, 'xh', [(0, 1), (1, 0)])  11 us
    all_to_all x1, blocking collectives, local(): mixed = lax.all_to_all(mixed, ROW_AXES, 0, 0, tiled=True)  10.9 us
    ppermute x24, waiting for transfers between devices, to_all(): parts = {k: lax.ppermute(x, 'z', shift(-k)) for k in (2, 1, 3)}  9.79 us
  transfers between devices with their start and end apart: 65, of which 20 were waited for; matrix products, arithmetic and copies ran while one was open for 12% of the time, Pallas kernels for 20%

profile of v1, /device:TPU:0, one launch (start us, length us, event | category | flops | bytes accessed | tf_op | source)
XLA Modules:
  0.0 249.0 jit_solution(4322188973089684929)
XLA Ops:
  1.3 4.7 %squares0.1 = (f32[4,32,1024]{2,1,0:T(8,128)}, f32[4,8,1024]{2,1,0:T(8,128)}, f32[4,8,1024]{2,1,0:T(8,128)}) custom-call(s32[2]{0:T(128)} %pad_add_fusion.meta, f32[8,4,64,1024]{3,2,1,0:T(8,128)} %eta.7), custom_call_target="tpu_custom_call" | custom-call | tf_op jit(solution)/shard_map/squares0/pallas_call | solution.py:260
  6.0 3.5 %collective-permute-start.7 = (f32[4,8,1024]{2,1,0:T(8,128)}, f32[4,8,1024]{2,1,0:T(8,128)S(1)}, u32[]{:S(2)}, u32[]{:S(2)}) collective-permute-start(f32[4,8,1024]{2,1,0:T(8,128)} %get-tuple-element.34), channel_id=1, source_target_pairs={{1,0},{2,1},{3,2},{4,3},{5,4},{6,5},{7,6},{8,7},{9,8},{10,9},{11,1... | collective-permute-start | bytes 393224 | tf_op jit(solution)/shard_map/ppermute | solution.py:391
  9.5 4.7 %squares1.1 = (f32[4,32,1024]{2,1,0:T(8,128)}, f32[4,8,1024]{2,1,0:T(8,128)}, f32[4,8,1024]{2,1,0:T(8,128)}) custom-call(s32[2]{0:T(128)} %pad_add_fusion.meta, f32[8,4,64,1024]{3,2,1,0:T(8,128)} %eta.7), custom_call_target="tpu_custom_call" | custom-call | tf_op jit(solution)/shard_map/squares1/pallas_call | solution.py:260
  15.3 4.0 %collective-permute-start = (f32[32,1024]{1,0:T(8,128)S(1)}, f32[32,1024]{1,0:T(8,128)S(1)}, u32[]{:S(2)}, u32[]{:S(2)}) collective-permute-start(f32[32,1024]{1,0:T(8,128)S(1)} %get-tuple-element.83), channel_id=1, source_target_pairs={{0,64},{32,96},{64,0},{96,32},{1,65},{33,97},{65,1},{97,33},{2,66}... | collective-permute-start | bytes 393224 | tf_op jit(solution)/shard_map/ppermute | solution.py:337
  23.4 3.8 %collective-permute-start.17 = (f32[32,1024]{1,0:T(8,128)S(1)}, f32[32,1024]{1,0:T(8,128)S(1)}, u32[]{:S(2)}, u32[]{:S(2)}) collective-permute-start(f32[32,1024]{1,0:T(8,128)S(1)} %get-tuple-element.78), channel_id=1, source_target_pairs={{0,96},{32,0},{64,32},{96,64},{1,97},{33,1},{65,33},{97,65},{2,98}... | collective-permute-start | bytes 393224 | tf_op jit(solution)/shard_map/ppermute | solution.py:337
  29.3 2.9 %collective-permute-start.3 = (f32[32,1024]{1,0:T(8,128)S(1)}, f32[32,1024]{1,0:T(8,128)S(1)}, u32[]{:S(2)}, u32[]{:S(2)}) collective-permute-start(f32[32,1024]{1,0:T(8,128)S(1)} %fusion.16), channel_id=1, source_target_pairs={{0,16},{16,0},{1,17},{17,1},{2,18},{18,2},{3,19},{19,3},{4,20},{20... | collective-permute-start | bytes 393224 | tf_op jit(solution)/shard_map/ppermute | solution.py:343
  33.5 2.8 %collective-permute-start.18 = (f32[32,1024]{1,0:T(8,128)S(1)}, f32[32,1024]{1,0:T(8,128)S(1)}, u32[]{:S(2)}, u32[]{:S(2)}) collective-permute-start(f32[32,1024]{1,0:T(8,128)S(1)} %fusion.12), channel_id=1, source_target_pairs={{0,16},{16,0},{1,17},{17,1},{2,18},{18,2},{3,19},{19,3},{4,20},{20... | collective-permute-start | bytes 393224 | tf_op jit(solution)/shard_map/ppermute | solution.py:343
  36.4 3.1 %collective-permute-start.5 = (f32[32,1024]{1,0:T(8,128)S(1)}, f32[32,1024]{1,0:T(8,128)S(1)}, u32[]{:S(2)}, u32[]{:S(2)}) collective-permute-start(f32[32,1024]{1,0:T(8,128)S(1)} %add.152), channel_id=1, source_target_pairs={{0,64},{32,96},{64,0},{96,32},{1,65},{33,97},{65,1},{97,33},{2,66}... | collective-permute-start | bytes 393224 | tf_op jit(solution)/shard_map/ppermute | solution.py:347
  42.6 2.4 collective-permute-done.5
  45.0 2.4 collective-permute-start.20
  49.1 7.0 %step0_1.1 = (f32[4,8,32,1024]{3,2,1,0:T(8,128)}, f32[4,32,1024]{2,1,0:T(8,128)}, f32[4,8,1024]{2,1,0:T(8,128)}, f32[4,8,1024]{2,1,0:T(8,128)}) custom-call(s32[2]{0:T(128)} %pad_add_fusion.meta, f32[8,4,64,1024]{3,2,1,0:T(8,128)} %eta.7, f32[4,32,1024]{2,1,0:T(8,128)} %pad_maximum_fusion.total, f32[4,8,1024]{2,1,0:T(8,128)} %get-tuple-element.33.above, ...), custom_call_target="tpu_custom_call" | custom-call | tf_op jit(solution)/shard_map/step0_1/pallas_call | solution.py:260
  58.7 2.9 %collective-permute-start.10 = (f32[32,1024]{1,0:T(8,128)S(1)}, f32[32,1024]{1,0:T(8,128)S(1)}, u32[]{:S(2)}, u32[]{:S(2)}) collective-permute-start(f32[32,1024]{1,0:T(8,128)S(1)} %get-tuple-element.81), channel_id=1, source_target_pairs={{0,96},{32,0},{64,32},{96,64},{1,97},{33,1},{65,33},{97,65},{2,98}... | collective-permute-start | bytes 393224 | tf_op jit(solution)/shard_map/ppermute | solution.py:337
  63.1 7.0 %step0_0.1 = (f32[4,8,32,1024]{3,2,1,0:T(8,128)}, f32[4,32,1024]{2,1,0:T(8,128)}, f32[4,8,1024]{2,1,0:T(8,128)}, f32[4,8,1024]{2,1,0:T(8,128)}) custom-call(s32[2]{0:T(128)} %pad_add_fusion.meta, f32[8,4,64,1024]{3,2,1,0:T(8,128)} %eta.7, f32[4,32,1024]{2,1,0:T(8,128)} %pad_maximum_fusion.2.total, f32[4,8,1024]{2,1,0:T(8,128)} %copy-done.3, ...), custom_call_target="tpu_custom_call" | custom-call | tf_op jit(solution)/shard_map/step0_0/pallas_call | solution.py:260
  71.3 1.6 collective-permute-start.31
  72.9 1.8 collective-permute-start.33
  76.5 2.5 collective-permute-start.11
  79.2 3.0 %collective-permute-done.33 = f32[32,1024]{1,0:T(8,128)S(1)} collective-permute-done((f32[32,1024]{1,0:T(8,128)S(1)}, f32[32,1024]{1,0:T(8,128)S(1)}, u32[]{:S(2)}, u32[]{:S(2)}) %collective-permute-start.33) | collective-permute-done | bytes 131104 | tf_op jit(solution)/shard_map/ppermute | solution.py:337
  83.2 2.5 collective-permute-start.34
  85.9 3.6 %collective-permute-start.13 = (f32[32,1024]{1,0:T(8,128)S(1)}, f32[32,1024]{1,0:T(8,128)S(1)}, u32[]{:S(2)}, u32[]{:S(2)}) collective-permute-start(f32[32,1024]{1,0:T(8,128)S(1)} %add.156), channel_id=1, source_target_pairs={{0,64},{32,96},{64,0},{96,32},{1,65},{33,97},{65,1},{97,33},{2,66}... | collective-permute-start | bytes 393224 | tf_op jit(solution)/shard_map/ppermute | solution.py:347
  89.6 4.4 %fusion = f32[34,1024]{1,0:T(8,128)S(1)} fusion(f32[1024,1024]{1,0:T(8,128)} %param.10, s32[34]{0:T(128)S(1)} %pad_add_fusion.1), kind=kOutput, calls=%fused_computation.11 | convolution fusion | flops 427853824 | bytes 4333704 | tf_op jit(solution)/shard_map/dot_general | solution.py:137
  95.0 2.1 collective-permute-start.37
  97.4 2.5 %collective-permute-start.35 = (f32[32,1024]{1,0:T(8,128)S(1)}, f32[32,1024]{1,0:T(8,128)S(1)}, u32[]{:S(2)}, u32[]{:S(2)}) collective-permute-start(f32[32,1024]{1,0:T(8,128)S(1)} %add.168), channel_id=1, source_target_pairs={{0,96},{32,0},{64,32},{96,64},{1,97},{33,1},{65,33},{97,65},{2,98}... | collective-permute-start | bytes 393224 | tf_op jit(solution)/shard_map/ppermute | solution.py:347
  101.4 6.5 %step1_1.1 = (f32[4,8,32,1024]{3,2,1,0:T(8,128)}, f32[4,32,1024]{2,1,0:T(8,128)}, f32[4,8,1024]{2,1,0:T(8,128)}, f32[4,8,1024]{2,1,0:T(8,128)}) custom-call(f32[4,8,32,1024]{3,2,1,0:T(8,128)} %get-tuple-element.35.eta, f32[4,32,1024]{2,1,0:T(8,128)} %pad_maximum_fusion.1.total, f32[4,8,1024]{2,1,0:T(8,128)} %get-tuple-element.40.above, f32[4,8,1024]{2,1,0:T(8,128)} %copy-done.4), custom_call_target="tpu_custom_call" | custom-call | tf_op jit(solution)/shard_map/step1_1/pallas_call | solution.py:260
  113.9 6.5 %step1_0.1 = (f32[4,8,32,1024]{3,2,1,0:T(8,128)}, f32[4,32,1024]{2,1,0:T(8,128)}, f32[4,8,1024]{2,1,0:T(8,128)}, f32[4,8,1024]{2,1,0:T(8,128)}) custom-call(f32[4,8,32,1024]{3,2,1,0:T(8,128)} %get-tuple-element.44.eta, f32[4,32,1024]{2,1,0:T(8,128)} %pad_maximum_fusion.4.total, f32[4,8,1024]{2,1,0:T(8,128)} %copy-done.5, f32[4,8,1024]{2,1,0:T(8,128)} %get-tuple-element.47.below), custom_call_target="tpu_custom_call" | custom-call | tf_op jit(solution)/shard_map/step1_0/pallas_call | solution.py:260
  121.4 2.4 collective-permute-start.40
  128.8 2.3 collective-permute-done.41
  134.8 2.5 collective-permute-start.29
  139.3 3.1 %collective-permute-done.30 = f32[32,1024]{1,0:T(8,128)S(1)} collective-permute-done((f32[32,1024]{1,0:T(8,128)S(1)}, f32[32,1024]{1,0:T(8,128)S(1)}, u32[]{:S(2)}, u32[]{:S(2)}) %collective-permute-start.30) | collective-permute-done | bytes 131104 | tf_op jit(solution)/shard_map/ppermute | solution.py:347
  143.8 2.1 collective-permute-start.44
  147.4 6.5 %step2_1.1 = (f32[4,8,32,1024]{3,2,1,0:T(8,128)}, f32[4,32,1024]{2,1,0:T(8,128)}) custom-call(f32[8]{0:T(128)} %weight.7, f32[4,8,32,1024]{3,2,1,0:T(8,128)} %get-tuple-element.42.eta, f32[4,32,1024]{2,1,0:T(8,128)} %pad_maximum_fusion.3.total, f32[4,8,1024]{2,1,0:T(8,128)} %get-tuple-element.48.above, f32[4,8,1024]{2,1,0:T(8,128)} %copy-done.7), custom_call_target="tpu_custom_call" | custom-call | tf_op jit(solution)/shard_map/step2_1/pallas_call | solution.py:260
  155.0 2.7 %collective-permute-start.52 = (f32[32,1024]{1,0:T(8,128)S(1)}, f32[32,1024]{1,0:T(8,128)S(1)}, u32[]{:S(2)}, u32[]{:S(2)}) collective-permute-start(f32[32,1024]{1,0:T(8,128)S(1)} %get-tuple-element.62), channel_id=1, source_target_pairs={{0,64},{32,96},{64,0},{96,32},{1,65},{33,97},{65,1},{97,33},{2,66}... | collective-permute-start | bytes 393224 | tf_op jit(solution)/shard_map/ppermute | solution.py:337
  161.2 6.5 %step2_0.1 = (f32[4,8,32,1024]{3,2,1,0:T(8,128)}, f32[4,32,1024]{2,1,0:T(8,128)}) custom-call(f32[8]{0:T(128)} %weight.7, f32[4,8,32,1024]{3,2,1,0:T(8,128)} %get-tuple-element.51.eta, f32[4,32,1024]{2,1,0:T(8,128)} %pad_maximum_fusion.5.total, f32[4,8,1024]{2,1,0:T(8,128)} %copy-done.6, f32[4,8,1024]{2,1,0:T(8,128)} %get-tuple-element.54.below), custom_call_target="tpu_custom_call" | custom-call | tf_op jit(solution)/shard_map/step2_0/pallas_call | solution.py:260
  169.7 1.8 collective-permute-start.50
  175.8 1.8 collective-permute-done.49
  180.6 4.5 %collective-permute-done.51 = f32[32,1024]{1,0:T(8,128)S(1)} collective-permute-done((f32[32,1024]{1,0:T(8,128)S(1)}, f32[32,1024]{1,0:T(8,128)S(1)}, u32[]{:S(2)}, u32[]{:S(2)}) %collective-permute-start.51) | collective-permute-done | bytes 131104 | tf_op jit(solution)/shard_map/ppermute | solution.py:343
  185.8 3.1 %row_forward.1 = f32[16,16,128]{2,1,0:T(8,128)} custom-call(s32[2]{0:T(128)} %pad_add_fusion.meta, f32[32,1024]{1,0:T(8,128)} %add.176.s0, f32[32,1024]{1,0:T(8,128)} %add.180.s1, f32[2,2,4,8,128]{4,3,2,1,0:T(8,128)} %constant.110.clone.line, f32[2,2,64,256]{3,2,1,0:T(8,128)} %constant.111.clone.fwd), custom_call_target="tpu_custom_call" | custom-call | tf_op jit(solution)/shard_map/row_forward/pallas_call | solution.py:260
  188.9 3.5 %all-to-all-start = ((f32[16,16,128]{2,1,0:T(8,128)}), f32[16,16,128]{2,1,0:T(8,128)S(1)}, u32[]{:S(2)}, u32[]{:S(2)}) async-start(f32[16,16,128]{2,1,0:T(8,128)} %row_forward.1), calls=%async_computation | async-start | bytes 262144 | tf_op jit(solution)/shard_map/all_to_all | solution.py:400
  194.4 4.7 %all-to-all-done.recv = f32[16,16,128]{2,1,0:T(8,128)S(1)} async-done(((f32[16,16,128]{2,1,0:T(8,128)}), f32[16,16,128]{2,1,0:T(8,128)S(1)}, u32[]{:S(2)}, u32[]{:S(2)}) %all-to-all-start) | async-done | bytes 131104 | tf_op jit(solution)/shard_map/all_to_all | solution.py:400
  199.7 2.8 %column.1 = f32[16,16,128]{2,1,0:T(8,128)} custom-call(f32[16,16,128]{2,1,0:T(8,128)} %copy-done.1, f32[24,128]{1,0:T(8,128)} %select_select_fusion.masks, f32[16,24,128]{2,1,0:T(8,128)} %select_maximum_fusion.green, f32[2,16,128]{2,1,0:T(8,128)} %constant.112.clone.twiddle, f32[2,128,128]{2,1,0:T(8,128)} %constant.113.clone.col), custom_call_target="tpu_custom_call" | custom-call | tf_op jit(solution)/shard_map/column/pallas_call | solution.py:260
  202.5 10.9 %all_to_all.10.recv = f32[16,16,128]{2,1,0:T(8,128)} all-to-all(f32[16,16,128]{2,1,0:T(8,128)} %column.1), channel_id=1, replica_groups=mesh['z'=4,'xh'=2,'y'=4,'xl'=2,'c'=2] {'y','xl','c'}, dimensions={0} | all-to-all | bytes 262144 | tf_op jit(solution)/shard_map/all_to_all | solution.py:402
  213.4 3.0 %row_backward.1 = (f32[32,1024]{1,0:T(8,128)}, f32[32,1024]{1,0:T(8,128)}) custom-call(s32[2]{0:T(128)} %pad_add_fusion.meta, f32[16,16,128]{2,1,0:T(8,128)} %all_to_all.10.recv, f32[2,2,4,8,128]{4,3,2,1,0:T(8,128)} %constant.110.clone.line, f32[2,2,64,256]{3,2,1,0:T(8,128)} %constant.114.clone.bwd), custom_call_target="tpu_custom_call" | custom-call | tf_op jit(solution)/shard_map/row_backward/pallas_call | solution.py:260
  216.4 2.3 collective-permute-start.60
  219.9 4.2 %collective-permute-done.60 = f32[32,1024]{1,0:T(8,128)S(1)} collective-permute-done((f32[32,1024]{1,0:T(8,128)}, f32[32,1024]{1,0:T(8,128)S(1)}, u32[]{:S(2)}, u32[]{:S(2)}) %collective-permute-start.60) | collective-permute-done | bytes 131104 | tf_op jit(solution)/shard_map/ppermute | solution.py:343
  225.2 2.3 collective-permute-start.62
  230.5 1.9 collective-permute-start.58
  232.4 1.9 collective-permute-done.63
  236.7 5.7 %final0.1 = (f32[8,4,64,1024]{3,2,1,0:T(8,128)}, f32[4,64,1024]{2,1,0:T(8,128)}) custom-call(s32[2]{0:T(128)} %pad_add_fusion.meta, f32[8]{0:T(128)} %weight.7, f32[4,8,32,1024]{3,2,1,0:T(8,128)} %get-tuple-element.58.eta, f32[4,32,1024]{2,1,0:T(8,128)} %pad_maximum_fusion.7.pot), custom_call_target="tpu_custom_call" | custom-call | tf_op jit(solution)/shard_map/final0/pallas_call | solution.py:260
  243.2 5.7 %final1.1 = (f32[8,4,64,1024]{3,2,1,0:T(8,128)}, f32[4,64,1024]{2,1,0:T(8,128)}) custom-call(s32[2]{0:T(128)} %pad_add_fusion.meta, f32[8]{0:T(128)} %weight.7, f32[4,8,32,1024]{3,2,1,0:T(8,128)} %get-tuple-element.50.eta, f32[4,32,1024]{2,1,0:T(8,128)} %pad_maximum_fusion.6.pot, ...), custom_call_target="tpu_custom_call", output_to_operand_aliasing={{0}: (4, {}), {1}: (5, {})} | custom-call | tf_op jit(solution)/shard_map/final1/pallas_call | solution.py:260
  (167 shorter events, 71.6 us)
Async XLA Ops:
  6.0 42.5 %collective-permute-start.7 = (f32[4,8,1024]{2,1,0:T(8,128)}, f32[4,8,1024]{2,1,0:T(8,128)S(1)}, u32[]{:S(2)}, u32[]{:S(2)}) collective-permute-start(f32[4,8,1024]{2,1,0:T(8,128)} %get-tuple-element.34), channel_id=1, source_target_pairs={{1,0},{2,1},{3,2},{4,3},{5,4},{6,5},{7,6},{8,7},{9,8},{10,9},{11,1... | collective-permute-start | bytes 393224 | tf_op jit(solution)/shard_map/ppermute | solution.py:391
  15.3 8.2 %collective-permute-start = (f32[32,1024]{1,0:T(8,128)S(1)}, f32[32,1024]{1,0:T(8,128)S(1)}, u32[]{:S(2)}, u32[]{:S(2)}) collective-permute-start(f32[32,1024]{1,0:T(8,128)S(1)} %get-tuple-element.83), channel_id=1, source_target_pairs={{0,64},{32,96},{64,0},{96,32},{1,65},{33,97},{65,1},{97,33},{2,66}... | collective-permute-start | bytes 393224 | tf_op jit(solution)/shard_map/ppermute | solution.py:337
  19.2 8.0 %collective-permute-start.2 = (f32[32,1024]{1,0:T(8,128)S(1)}, f32[32,1024]{1,0:T(8,128)S(1)}, u32[]{:S(2)}, u32[]{:S(2)}) collective-permute-start(f32[32,1024]{1,0:T(8,128)S(1)} %get-tuple-element.84), channel_id=1, source_target_pairs={{0,96},{32,0},{64,32},{96,64},{1,97},{33,1},{65,33},{97,65},{2,98}... | collective-permute-start | bytes 393224 | tf_op jit(solution)/shard_map/ppermute | solution.py:337
  19.9 8.4 %collective-permute-start.1 = (f32[32,1024]{1,0:T(8,128)S(1)}, f32[32,1024]{1,0:T(8,128)S(1)}, u32[]{:S(2)}, u32[]{:S(2)}) collective-permute-start(f32[32,1024]{1,0:T(8,128)S(1)} %get-tuple-element.85), channel_id=1, source_target_pairs={{0,32},{32,64},{64,96},{96,0},{1,33},{33,65},{65,97},{97,1},{2,34}... | collective-permute-start | bytes 393224 | tf_op jit(solution)/shard_map/ppermute | solution.py:337
  21.3 10.9 %collective-permute-start.15 = (f32[32,1024]{1,0:T(8,128)S(1)}, f32[32,1024]{1,0:T(8,128)S(1)}, u32[]{:S(2)}, u32[]{:S(2)}) collective-permute-start(f32[32,1024]{1,0:T(8,128)S(1)} %get-tuple-element.77), channel_id=1, source_target_pairs={{0,64},{32,96},{64,0},{96,32},{1,65},{33,97},{65,1},{97,33},{2,66}... | collective-permute-start | bytes 393224 | tf_op jit(solution)/shard_map/ppermute | solution.py:337
  23.4 8.8 %collective-permute-start.17 = (f32[32,1024]{1,0:T(8,128)S(1)}, f32[32,1024]{1,0:T(8,128)S(1)}, u32[]{:S(2)}, u32[]{:S(2)}) collective-permute-start(f32[32,1024]{1,0:T(8,128)S(1)} %get-tuple-element.78), channel_id=1, source_target_pairs={{0,96},{32,0},{64,32},{96,64},{1,97},{33,1},{65,33},{97,65},{2,98}... | collective-permute-start | bytes 393224 | tf_op jit(solution)/shard_map/ppermute | solution.py:337
  36.4 8.5 %collective-permute-start.5 = (f32[32,1024]{1,0:T(8,128)S(1)}, f32[32,1024]{1,0:T(8,128)S(1)}, u32[]{:S(2)}, u32[]{:S(2)}) collective-permute-start(f32[32,1024]{1,0:T(8,128)S(1)} %add.152), channel_id=1, source_target_pairs={{0,64},{32,96},{64,0},{96,32},{1,65},{33,97},{65,1},{97,33},{2,66}... | collective-permute-start | bytes 393224 | tf_op jit(solution)/shard_map/ppermute | solution.py:347
  39.5 7.8 %collective-permute-start.4 = (f32[32,1024]{1,0:T(8,128)S(1)}, f32[32,1024]{1,0:T(8,128)S(1)}, u32[]{:S(2)}, u32[]{:S(2)}) collective-permute-start(f32[32,1024]{1,0:T(8,128)S(1)} %add.152), channel_id=1, source_target_pairs={{0,96},{32,0},{64,32},{96,64},{1,97},{33,1},{65,33},{97,65},{2,98}... | collective-permute-start | bytes 393224 | tf_op jit(solution)/shard_map/ppermute | solution.py:347
  41.0 21.4 %collective-permute-start.22 = (f32[4,8,1024]{2,1,0:T(8,128)}, f32[4,8,1024]{2,1,0:T(8,128)S(1)}, u32[]{:S(2)}, u32[]{:S(2)}) collective-permute-start(f32[4,8,1024]{2,1,0:T(8,128)} %get-tuple-element.38), channel_id=1, source_target_pairs={{0,1},{1,2},{2,3},{3,4},{4,5},{5,6},{6,7},{7,8},{8,9},{9,10},{10,1... | collective-permute-start | bytes 393224 | tf_op jit(solution)/shard_map/ppermute | solution.py:390
  42.6 16.1 %collective-permute-start.21 = (f32[32,1024]{1,0:T(8,128)S(1)}, f32[32,1024]{1,0:T(8,128)S(1)}, u32[]{:S(2)}, u32[]{:S(2)}) collective-permute-start(f32[32,1024]{1,0:T(8,128)S(1)} %add.160), channel_id=1, source_target_pairs={{0,32},{32,64},{64,96},{96,0},{1,33},{33,65},{65,97},{97,1},{2,34}... | collective-permute-start | bytes 393224 | tf_op jit(solution)/shard_map/ppermute | solution.py:347
  45.0 16.7 %collective-permute-start.20 = (f32[32,1024]{1,0:T(8,128)S(1)}, f32[32,1024]{1,0:T(8,128)S(1)}, u32[]{:S(2)}, u32[]{:S(2)}) collective-permute-start(f32[32,1024]{1,0:T(8,128)S(1)} %add.160), channel_id=1, source_target_pairs={{0,64},{32,96},{64,0},{96,32},{1,65},{33,97},{65,1},{97,33},{2,66}... | collective-permute-start | bytes 393224 | tf_op jit(solution)/shard_map/ppermute | solution.py:347
  47.3 14.3 %collective-permute-start.19 = (f32[32,1024]{1,0:T(8,128)S(1)}, f32[32,1024]{1,0:T(8,128)S(1)}, u32[]{:S(2)}, u32[]{:S(2)}) collective-permute-start(f32[32,1024]{1,0:T(8,128)S(1)} %add.160), channel_id=1, source_target_pairs={{0,96},{32,0},{64,32},{96,64},{1,97},{33,1},{65,33},{97,65},{2,98}... | collective-permute-start | bytes 393224 | tf_op jit(solution)/shard_map/ppermute | solution.py:347
  57.2 15.8 %collective-permute-start.8 = (f32[32,1024]{1,0:T(8,128)S(1)}, f32[32,1024]{1,0:T(8,128)S(1)}, u32[]{:S(2)}, u32[]{:S(2)}) collective-permute-start(f32[32,1024]{1,0:T(8,128)S(1)} %get-tuple-element.80), channel_id=1, source_target_pairs={{0,64},{32,96},{64,0},{96,32},{1,65},{33,97},{65,1},{97,33},{2,66}... | collective-permute-start | bytes 393224 | tf_op jit(solution)/shard_map/ppermute | solution.py:337
  58.7 16.0 %collective-permute-start.10 = (f32[32,1024]{1,0:T(8,128)S(1)}, f32[32,1024]{1,0:T(8,128)S(1)}, u32[]{:S(2)}, u32[]{:S(2)}) collective-permute-start(f32[32,1024]{1,0:T(8,128)S(1)} %get-tuple-element.81), channel_id=1, source_target_pairs={{0,96},{32,0},{64,32},{96,64},{1,97},{33,1},{65,33},{97,65},{2,98}... | collective-permute-start | bytes 393224 | tf_op jit(solution)/shard_map/ppermute | solution.py:337
  61.6 13.9 %collective-permute-start.9 = (f32[32,1024]{1,0:T(8,128)S(1)}, f32[32,1024]{1,0:T(8,128)S(1)}, u32[]{:S(2)}, u32[]{:S(2)}) collective-permute-start(f32[32,1024]{1,0:T(8,128)S(1)} %get-tuple-element.82), channel_id=1, source_target_pairs={{0,32},{32,64},{64,96},{96,0},{1,33},{33,65},{65,97},{97,1},{2,34}... | collective-permute-start | bytes 393224 | tf_op jit(solution)/shard_map/ppermute | solution.py:337
  70.2 30.6 %collective-permute-start.23 = (f32[4,8,1024]{2,1,0:T(8,128)}, f32[4,8,1024]{2,1,0:T(8,128)S(1)}, u32[]{:S(2)}, u32[]{:S(2)}) collective-permute-start(f32[4,8,1024]{2,1,0:T(8,128)} %get-tuple-element.41), channel_id=1, source_target_pairs={{1,0},{2,1},{3,2},{4,3},{5,4},{6,5},{7,6},{8,7},{9,8},{10,9},{11,1... | collective-permute-start | bytes 393224 | tf_op jit(solution)/shard_map/ppermute | solution.py:391
  71.3 7.9 %collective-permute-start.31 = (f32[32,1024]{1,0:T(8,128)S(1)}, f32[32,1024]{1,0:T(8,128)S(1)}, u32[]{:S(2)}, u32[]{:S(2)}) collective-permute-start(f32[32,1024]{1,0:T(8,128)S(1)} %get-tuple-element.71), channel_id=1, source_target_pairs={{0,64},{32,96},{64,0},{96,32},{1,65},{33,97},{65,1},{97,33},{2,66}... | collective-permute-start | bytes 393224 | tf_op jit(solution)/shard_map/ppermute | solution.py:337
  72.9 9.3 %collective-permute-start.33 = (f32[32,1024]{1,0:T(8,128)S(1)}, f32[32,1024]{1,0:T(8,128)S(1)}, u32[]{:S(2)}, u32[]{:S(2)}) collective-permute-start(f32[32,1024]{1,0:T(8,128)S(1)} %get-tuple-element.72), channel_id=1, source_target_pairs={{0,96},{32,0},{64,32},{96,64},{1,97},{33,1},{65,33},{97,65},{2,98}... | collective-permute-start | bytes 393224 | tf_op jit(solution)/shard_map/ppermute | solution.py:337
  76.5 9.1 %collective-permute-start.11 = (f32[32,1024]{1,0:T(8,128)S(1)}, f32[32,1024]{1,0:T(8,128)S(1)}, u32[]{:S(2)}, u32[]{:S(2)}) collective-permute-start(f32[32,1024]{1,0:T(8,128)S(1)} %fusion.14), channel_id=1, source_target_pairs={{0,16},{16,0},{1,17},{17,1},{2,18},{18,2},{3,19},{19,3},{4,20},{20... | collective-permute-start | bytes 393224 | tf_op jit(solution)/shard_map/ppermute | solution.py:343
  83.2 11.7 %collective-permute-start.34 = (f32[32,1024]{1,0:T(8,128)S(1)}, f32[32,1024]{1,0:T(8,128)S(1)}, u32[]{:S(2)}, u32[]{:S(2)}) collective-permute-start(f32[32,1024]{1,0:T(8,128)S(1)} %fusion.8), channel_id=1, source_target_pairs={{0,16},{16,0},{1,17},{17,1},{2,18},{18,2},{3,19},{19,3},{4,20},{20... | collective-permute-start | bytes 393224 | tf_op jit(solution)/shard_map/ppermute | solution.py:343
  85.6 9.3 %collective-permute-start.14 = (f32[32,1024]{1,0:T(8,128)S(1)}, f32[32,1024]{1,0:T(8,128)S(1)}, u32[]{:S(2)}, u32[]{:S(2)}) collective-permute-start(f32[32,1024]{1,0:T(8,128)S(1)} %add.156), channel_id=1, source_target_pairs={{0,32},{32,64},{64,96},{96,0},{1,33},{33,65},{65,97},{97,1},{2,34}... | collective-permute-start | bytes 393224 | tf_op jit(solution)/shard_map/ppermute | solution.py:347
  85.9 11.1 %collective-permute-start.13 = (f32[32,1024]{1,0:T(8,128)S(1)}, f32[32,1024]{1,0:T(8,128)S(1)}, u32[]{:S(2)}, u32[]{:S(2)}) collective-permute-start(f32[32,1024]{1,0:T(8,128)S(1)} %add.156), channel_id=1, source_target_pairs={{0,64},{32,96},{64,0},{96,32},{1,65},{33,97},{65,1},{97,33},{2,66}... | collective-permute-start | bytes 393224 | tf_op jit(solution)/shard_map/ppermute | solution.py:347
  89.6 7.8 %collective-permute-start.12 = (f32[32,1024]{1,0:T(8,128)S(1)}, f32[32,1024]{1,0:T(8,128)S(1)}, u32[]{:S(2)}, u32[]{:S(2)}) collective-permute-start(f32[32,1024]{1,0:T(8,128)S(1)} %add.156), channel_id=1, source_target_pairs={{0,96},{32,0},{64,32},{96,64},{1,97},{33,1},{65,33},{97,65},{2,98}... | collective-permute-start | bytes 393224 | tf_op jit(solution)/shard_map/ppermute | solution.py:347
  94.9 18.4 %collective-permute-start.38 = (f32[4,8,1024]{2,1,0:T(8,128)S(1)}, f32[4,8,1024]{2,1,0:T(8,128)S(1)}, u32[]{:S(2)}, u32[]{:S(2)}) collective-permute-start(f32[4,8,1024]{2,1,0:T(8,128)S(1)} %copy-done.8), channel_id=1, source_target_pairs={{0,1},{1,2},{2,3},{3,4},{4,5},{5,6},{6,7},{7,8},{8,9},{9,10},{10,1... | collective-permute-start | bytes 393224 | tf_op jit(solution)/shard_map/ppermute | solution.py:390
  95.0 15.4 %collective-permute-start.37 = (f32[32,1024]{1,0:T(8,128)S(1)}, f32[32,1024]{1,0:T(8,128)S(1)}, u32[]{:S(2)}, u32[]{:S(2)}) collective-permute-start(f32[32,1024]{1,0:T(8,128)S(1)} %add.168), channel_id=1, source_target_pairs={{0,32},{32,64},{64,96},{96,0},{1,33},{33,65},{65,97},{97,1},{2,34}... | collective-permute-start | bytes 393224 | tf_op jit(solution)/shard_map/ppermute | solution.py:347
  97.1 14.2 %collective-permute-start.36 = (f32[32,1024]{1,0:T(8,128)S(1)}, f32[32,1024]{1,0:T(8,128)S(1)}, u32[]{:S(2)}, u32[]{:S(2)}) collective-permute-start(f32[32,1024]{1,0:T(8,128)S(1)} %add.168), channel_id=1, source_target_pairs={{0,64},{32,96},{64,0},{96,32},{1,65},{33,97},{65,1},{97,33},{2,66}... | collective-permute-start | bytes 393224 | tf_op jit(solution)/shard_map/ppermute | solution.py:347
  97.4 15.0 %collective-permute-start.35 = (f32[32,1024]{1,0:T(8,128)S(1)}, f32[32,1024]{1,0:T(8,128)S(1)}, u32[]{:S(2)}, u32[]{:S(2)}) collective-permute-start(f32[32,1024]{1,0:T(8,128)S(1)} %add.168), channel_id=1, source_target_pairs={{0,96},{32,0},{64,32},{96,64},{1,97},{33,1},{65,33},{97,65},{2,98}... | collective-permute-start | bytes 393224 | tf_op jit(solution)/shard_map/ppermute | solution.py:347
  109.1 16.0 %collective-permute-start.24 = (f32[32,1024]{1,0:T(8,128)S(1)}, f32[32,1024]{1,0:T(8,128)S(1)}, u32[]{:S(2)}, u32[]{:S(2)}) collective-permute-start(f32[32,1024]{1,0:T(8,128)S(1)} %get-tuple-element.74), channel_id=1, source_target_pairs={{0,64},{32,96},{64,0},{96,32},{1,65},{33,97},{65,1},{97,33},{2,66}... | collective-permute-start | bytes 393224 | tf_op jit(solution)/shard_map/ppermute | solution.py:337
  110.4 15.4 %collective-permute-start.26 = (f32[32,1024]{1,0:T(8,128)S(1)}, f32[32,1024]{1,0:T(8,128)S(1)}, u32[]{:S(2)}, u32[]{:S(2)}) collective-permute-start(f32[32,1024]{1,0:T(8,128)S(1)} %get-tuple-element.75), channel_id=1, source_target_pairs={{0,96},{32,0},{64,32},{96,64},{1,97},{33,1},{65,33},{97,65},{2,98}... | collective-permute-start | bytes 393224 | tf_op jit(solution)/shard_map/ppermute | solution.py:337
  111.3 14.5 %collective-permute-start.25 = (f32[32,1024]{1,0:T(8,128)S(1)}, f32[32,1024]{1,0:T(8,128)S(1)}, u32[]{:S(2)}, u32[]{:S(2)}) collective-permute-start(f32[32,1024]{1,0:T(8,128)S(1)} %get-tuple-element.76), channel_id=1, source_target_pairs={{0,32},{32,64},{64,96},{96,0},{1,33},{33,65},{65,97},{97,1},{2,34}... | collective-permute-start | bytes 393224 | tf_op jit(solution)/shard_map/ppermute | solution.py:337
  126.8 7.9 %collective-permute-start.27 = (f32[32,1024]{1,0:T(8,128)S(1)}, f32[32,1024]{1,0:T(8,128)S(1)}, u32[]{:S(2)}, u32[]{:S(2)}) collective-permute-start(f32[32,1024]{1,0:T(8,128)S(1)} %fusion.10), channel_id=1, source_target_pairs={{0,16},{16,0},{1,17},{17,1},{2,18},{18,2},{3,19},{19,3},{4,20},{20... | collective-permute-start | bytes 393224 | tf_op jit(solution)/shard_map/ppermute | solution.py:343
  138.4 8.3 %collective-permute-start.39 = (f32[4,8,1024]{2,1,0:T(8,128)}, f32[4,8,1024]{2,1,0:T(8,128)S(1)}, u32[]{:S(2)}, u32[]{:S(2)}) collective-permute-start(f32[4,8,1024]{2,1,0:T(8,128)} %get-tuple-element.49), channel_id=1, source_target_pairs={{1,0},{2,1},{3,2},{4,3},{5,4},{6,5},{7,6},{8,7},{9,8},{10,9},{11,1... | collective-permute-start | bytes 393224 | tf_op jit(solution)/shard_map/ppermute | solution.py:391
  139.2 21.3 %collective-permute-start.47 = (f32[4,8,1024]{2,1,0:T(8,128)S(1)}, f32[4,8,1024]{2,1,0:T(8,128)S(1)}, u32[]{:S(2)}, u32[]{:S(2)}) collective-permute-start(f32[4,8,1024]{2,1,0:T(8,128)S(1)} %copy-done.9), channel_id=1, source_target_pairs={{0,1},{1,2},{2,3},{3,4},{4,5},{5,6},{6,7},{7,8},{8,9},{9,10},{10,1... | collective-permute-start | bytes 393224 | tf_op jit(solution)/shard_map/ppermute | solution.py:390
  142.4 15.3 %collective-permute-start.46 = (f32[32,1024]{1,0:T(8,128)S(1)}, f32[32,1024]{1,0:T(8,128)S(1)}, u32[]{:S(2)}, u32[]{:S(2)}) collective-permute-start(f32[32,1024]{1,0:T(8,128)S(1)} %add.172), channel_id=1, source_target_pairs={{0,32},{32,64},{64,96},{96,0},{1,33},{33,65},{65,97},{97,1},{2,34}... | collective-permute-start | bytes 393224 | tf_op jit(solution)/shard_map/ppermute | solution.py:347
  142.4 15.9 %collective-permute-start.45 = (f32[32,1024]{1,0:T(8,128)S(1)}, f32[32,1024]{1,0:T(8,128)S(1)}, u32[]{:S(2)}, u32[]{:S(2)}) collective-permute-start(f32[32,1024]{1,0:T(8,128)S(1)} %add.172), channel_id=1, source_target_pairs={{0,64},{32,96},{64,0},{96,32},{1,65},{33,97},{65,1},{97,33},{2,66}... | collective-permute-start | bytes 393224 | tf_op jit(solution)/shard_map/ppermute | solution.py:347
  143.8 15.9 %collective-permute-start.44 = (f32[32,1024]{1,0:T(8,128)S(1)}, f32[32,1024]{1,0:T(8,128)S(1)}, u32[]{:S(2)}, u32[]{:S(2)}) collective-permute-start(f32[32,1024]{1,0:T(8,128)S(1)} %add.172), channel_id=1, source_target_pairs={{0,96},{32,0},{64,32},{96,64},{1,97},{33,1},{65,33},{97,65},{2,98}... | collective-permute-start | bytes 393224 | tf_op jit(solution)/shard_map/ppermute | solution.py:347
  155.0 16.5 %collective-permute-start.52 = (f32[32,1024]{1,0:T(8,128)S(1)}, f32[32,1024]{1,0:T(8,128)S(1)}, u32[]{:S(2)}, u32[]{:S(2)}) collective-permute-start(f32[32,1024]{1,0:T(8,128)S(1)} %get-tuple-element.62), channel_id=1, source_target_pairs={{0,64},{32,96},{64,0},{96,32},{1,65},{33,97},{65,1},{97,33},{2,66}... | collective-permute-start | bytes 393224 | tf_op jit(solution)/shard_map/ppermute | solution.py:337
  157.7 14.0 %collective-permute-start.54 = (f32[32,1024]{1,0:T(8,128)S(1)}, f32[32,1024]{1,0:T(8,128)S(1)}, u32[]{:S(2)}, u32[]{:S(2)}) collective-permute-start(f32[32,1024]{1,0:T(8,128)S(1)} %get-tuple-element.63), channel_id=1, source_target_pairs={{0,96},{32,0},{64,32},{96,64},{1,97},{33,1},{65,33},{97,65},{2,98}... | collective-permute-start | bytes 393224 | tf_op jit(solution)/shard_map/ppermute | solution.py:337
  158.3 13.4 %collective-permute-start.53 = (f32[32,1024]{1,0:T(8,128)S(1)}, f32[32,1024]{1,0:T(8,128)S(1)}, u32[]{:S(2)}, u32[]{:S(2)}) collective-permute-start(f32[32,1024]{1,0:T(8,128)S(1)} %get-tuple-element.64), channel_id=1, source_target_pairs={{0,32},{32,64},{64,96},{96,0},{1,33},{33,65},{65,97},{97,1},{2,34}... | collective-permute-start | bytes 393224 | tf_op jit(solution)/shard_map/ppermute | solution.py:337
  188.9 10.2 %all-to-all-start = ((f32[16,16,128]{2,1,0:T(8,128)}), f32[16,16,128]{2,1,0:T(8,128)S(1)}, u32[]{:S(2)}, u32[]{:S(2)}) async-start(f32[16,16,128]{2,1,0:T(8,128)} %row_forward.1), calls=%async_computation | async-start | bytes 262144 | tf_op jit(solution)/shard_map/all_to_all | solution.py:400
  216.4 7.8 %collective-permute-start.60 = (f32[32,1024]{1,0:T(8,128)}, f32[32,1024]{1,0:T(8,128)S(1)}, u32[]{:S(2)}, u32[]{:S(2)}) collective-permute-start(f32[32,1024]{1,0:T(8,128)} %get-tuple-element.59), channel_id=1, source_target_pairs={{0,16},{16,0},{1,17},{17,1},{2,18},{18,2},{3,19},{19,3},{4,20},{20... | collective-permute-start | bytes 393224 | tf_op jit(solution)/shard_map/ppermute | solution.py:343
  218.6 9.8 %collective-permute-start.56 = (f32[32,1024]{1,0:T(8,128)}, f32[32,1024]{1,0:T(8,128)S(1)}, u32[]{:S(2)}, u32[]{:S(2)}) collective-permute-start(f32[32,1024]{1,0:T(8,128)} %get-tuple-element.57), channel_id=1, source_target_pairs={{0,16},{16,0},{1,17},{17,1},{2,18},{18,2},{3,19},{19,3},{4,20},{20... | collective-permute-start | bytes 393224 | tf_op jit(solution)/shard_map/ppermute | solution.py:343
  225.1 9.2 %collective-permute-start.63 = (f32[32,1024]{1,0:T(8,128)S(1)}, f32[32,1024]{1,0:T(8,128)S(1)}, u32[]{:S(2)}, u32[]{:S(2)}) collective-permute-start(f32[32,1024]{1,0:T(8,128)S(1)} %add.194), channel_id=1, source_target_pairs={{0,32},{32,64},{64,96},{96,0},{1,33},{33,65},{65,97},{97,1},{2,34}... | collective-permute-start | bytes 393224 | tf_op jit(solution)/shard_map/ppermute | solution.py:347
  225.2 9.8 %collective-permute-start.62 = (f32[32,1024]{1,0:T(8,128)S(1)}, f32[32,1024]{1,0:T(8,128)S(1)}, u32[]{:S(2)}, u32[]{:S(2)}) collective-permute-start(f32[32,1024]{1,0:T(8,128)S(1)} %add.194), channel_id=1, source_target_pairs={{0,64},{32,96},{64,0},{96,32},{1,65},{33,97},{65,1},{97,33},{2,66}... | collective-permute-start | bytes 393224 | tf_op jit(solution)/shard_map/ppermute | solution.py:347
  227.5 8.4 %collective-permute-start.61 = (f32[32,1024]{1,0:T(8,128)S(1)}, f32[32,1024]{1,0:T(8,128)S(1)}, u32[]{:S(2)}, u32[]{:S(2)}) collective-permute-start(f32[32,1024]{1,0:T(8,128)S(1)} %add.194), channel_id=1, source_target_pairs={{0,96},{32,0},{64,32},{96,64},{1,97},{33,1},{65,33},{97,65},{2,98}... | collective-permute-start | bytes 393224 | tf_op jit(solution)/shard_map/ppermute | solution.py:347
  229.3 13.1 %collective-permute-start.59 = (f32[32,1024]{1,0:T(8,128)S(1)}, f32[32,1024]{1,0:T(8,128)S(1)}, u32[]{:S(2)}, u32[]{:S(2)}) collective-permute-start(f32[32,1024]{1,0:T(8,128)S(1)} %add.193), channel_id=1, source_target_pairs={{0,32},{32,64},{64,96},{96,0},{1,33},{33,65},{65,97},{97,1},{2,34}... | collective-permute-start | bytes 393224 | tf_op jit(solution)/shard_map/ppermute | solution.py:347
  230.5 11.9 %collective-permute-start.58 = (f32[32,1024]{1,0:T(8,128)S(1)}, f32[32,1024]{1,0:T(8,128)S(1)}, u32[]{:S(2)}, u32[]{:S(2)}) collective-permute-start(f32[32,1024]{1,0:T(8,128)S(1)} %add.193), channel_id=1, source_target_pairs={{0,64},{32,96},{64,0},{96,32},{1,65},{33,97},{65,1},{97,33},{2,66}... | collective-permute-start | bytes 393224 | tf_op jit(solution)/shard_map/ppermute | solution.py:347
  234.3 8.1 %collective-permute-start.57 = (f32[32,1024]{1,0:T(8,128)S(1)}, f32[32,1024]{1,0:T(8,128)S(1)}, u32[]{:S(2)}, u32[]{:S(2)}) collective-permute-start(f32[32,1024]{1,0:T(8,128)S(1)} %add.193), channel_id=1, source_target_pairs={{0,96},{32,0},{64,32},{96,64},{1,97},{33,1},{65,33},{97,65},{2,98}... | collective-permute-start | bytes 393224 | tf_op jit(solution)/shard_map/ppermute | solution.py:347
  (27 other events, 185.1 us)

commit v2 on v1

v2 whole, which is shorter than its diff:
```python
import functools
import math

import jax
import jax.numpy as jnp
import numpy as np
from jax import lax
from jax.experimental import pallas as pl
from jax.experimental.pallas import tpu as pltpu
from jax.sharding import Mesh, PartitionSpec as P

GRAINS = 8
PLANES = 4
ROWS = 64
N = 1024
HALF = 32
STEPS = 3

DT = 0.1
ALPHA = 1.0
BETA = 1.0
GAMMA = 0.25
KAPPA = 1.0
ELASTIC = 2.0

C_ONE = 1.0 + DT * ALPHA - 4.0 * DT * KAPPA
C_TOTAL = 2.0 * DT * GAMMA
C_CUBE = DT * BETA - 2.0 * DT * GAMMA
C_NEAR = DT * KAPPA
FACTOR = DT * 2.0 * ELASTIC

ROW_AXES = ("y", "xl", "c")
HIGH = lax.Precision.HIGHEST
F32 = jnp.float32


def make_tables():
    two_pi = 2.0 * np.pi
    u = np.arange(128)
    low = np.arange(8).reshape(2, 4)
    place = 128 * np.arange(8)[:, None] + u[None, :]
    angle = two_pi * ((low[:, :, None, None] * place) % N) / N
    line = np.stack([np.cos(angle), np.sin(angle)], axis=1)
    high = np.arange(64)
    angle = two_pi * ((high[:, None] * u[None, :]) % 128) / 128
    plain = np.concatenate([np.cos(angle), np.sin(angle)], axis=1)
    special = plain.copy()
    special[0, 128:] = -((-1.0) ** u)
    fwd = np.stack([np.stack([special, plain]), np.stack([plain, plain])])
    scale = np.full((2, 2, 64, 1), 2.0)
    scale[0, 0, 0, 0] = 1.0
    bwd = fwd * scale / (N * N)
    r = np.arange(64)
    angle = two_pi * (np.arange(16)[:, None] * r[None, :]) / N
    sign = np.concatenate([-np.ones(64), np.ones(64)])
    cosine = np.tile(np.cos(angle), (1, 2))
    sine = np.tile(np.sin(angle), (1, 2)) * sign
    twiddle = np.stack([cosine, sine])
    angle = two_pi * ((r[:, None] * r[None, :]) % 64) / 64
    c, s = np.cos(angle), np.sin(angle)
    col = np.stack([np.block([[c, -s], [s, c]]), np.block([[c, s], [-s, c]])])
    return [x.astype(np.float32) for x in (line, fwd, bwd, twiddle, col)]


LINE, FWD, BWD, TWIDDLE, COL = make_tables()


def square_kernel(c, meta, order, eta, s0, s1, s2, s3, top, bottom, sems):
    copies = []
    for k in range(PLANES):
        source = order.at[:, own(k, meta), HALF * c : HALF * c + HALF, :]
        copies.append(pltpu.make_async_copy(source, eta.at[k], sems.at[k]))
        copies[k].start()
    for k, total in enumerate((s0, s1, s2, s3)):
        copies[k].wait()
        for rg in range(HALF // 8):
            acc = None
            for g in range(GRAINS):
                e = eta[k, g, 8 * rg : 8 * rg + 8, :]
                acc = e * e if acc is None else acc + e * e
            total[8 * rg : 8 * rg + 8, :] = acc
        for g in range(GRAINS):
            top[k, g : g + 1, :] = eta[k, g, 0:1, :]
            bottom[k, g : g + 1, :] = eta[k, g, HALF - 1 : HALF, :]


def step_kernel(last, extras, *refs):
    refs = list(refs[extras:])
    weight = refs.pop(0) if last else None
    eta, t0, t1, t2, t3, above, below, out, s0, s1, s2, s3 = refs[:12]
    total, sums = refs[-2:]
    row = lax.broadcasted_iota(jnp.int32, (8, N), 0)
    for k, t in enumerate((t0, t1, t2, t3)):
        total[k] = C_ONE - C_TOTAL * t[...]

    def plane(k, carry):
        for rg in range(HALF // 8):
            base = 8 * rg
            coef = total[k, base : base + 8, :]
            acc = jnp.zeros((8, N), F32)
            for g in range(GRAINS):
                e = eta[k, g, base : base + 8, :]
                before = above[k, g : g + 1, :] if rg == 0 else eta[k, g, base - 1 : base, :]
                after = below[k, g : g + 1, :] if base + 8 == HALF else eta[k, g, base + 8 : base + 9, :]
                up = jnp.where(row == 0, before, pltpu.roll(e, 1, 0))
                down = jnp.where(row == 7, after, pltpu.roll(e, 7, 0))
                near = (up + down) + (pltpu.roll(e, 1, 1) + pltpu.roll(e, N - 1, 1))
                new = e * (coef - C_CUBE * (e * e)) + C_NEAR * near
                out[k, g, base : base + 8, :] = new
                if last:
                    acc = acc + weight[g] * (new * new)
                else:
                    top, bottom = refs[12:14]
                    if rg == 0:
                        top[k, g : g + 1, :] = new[0:1]
                    if base + 8 == HALF:
                        bottom[k, g : g + 1, :] = new[7:8]
                    acc = acc + new * new
            sums[k, base : base + 8, :] = acc
        return carry

    lax.fori_loop(0, PLANES, plane, 0)
    for k, s in enumerate((s0, s1, s2, s3)):
        s[...] = sums[k]


def final_kernel(c, meta, weight, eta, p0, p1, p2, p3, *refs):
    out, pot_out, field, pot, sems, pot_sems = refs[-6:]
    copies = []
    for k, p in enumerate((p0, p1, p2, p3)):
        for rg in range(HALF // 8):
            base = 8 * rg
            v = p[base : base + 8, :]
            pot[k, base : base + 8, :] = v
            for g in range(GRAINS):
                e = eta[k, g, base : base + 8, :]
                field[k, g, base : base + 8, :] = e - (FACTOR * weight[g]) * (e * v)
        plane, rows = own(k, meta), slice(HALF * c, HALF * c + HALF)
        copies.append(pltpu.make_async_copy(field.at[k], out.at[:, plane, rows, :], sems.at[k]))
        copies.append(pltpu.make_async_copy(pot.at[k], pot_out.at[plane, rows, :], pot_sems.at[k]))
        copies[-2].start()
        copies[-1].start()
    for copy in copies:
        copy.wait()


def nt(a, b):
    return lax.dot_general(a, b, (((1,), (1,)), ((), ())), precision=HIGH, preferred_element_type=F32)


def nn(a, b):
    return lax.dot_general(a, b, (((1,), (0,)), ((), ())), precision=HIGH, preferred_element_type=F32)


def row_forward_kernel(meta, s0, s1, line, fwd, out):
    for l1 in range(4):
        real, imag = [], []
        for src in (s0, s1):
            a = b = None
            for t in range(8):
                x = src[:, 128 * t : 128 * t + 128]
                p = x * line[0, 0, l1, t : t + 1, :]
                q = x * line[0, 1, l1, t : t + 1, :]
                a = p if a is None else a + p
                b = q if b is None else b + q
            real.append(a)
            imag.append(-b)
        a = jnp.concatenate(real, axis=0)
        b = jnp.concatenate(imag, axis=0)
        pairs = jnp.concatenate([jnp.concatenate([a, b], axis=1), jnp.concatenate([b, -a], axis=1)], axis=0)
        y = nt(fwd[0, 0 if l1 == 0 else 1], pairs)
        j, p = divmod(l1, 2)
        out[8 * j : 8 * j + 8, 8 * p : 8 * p + 8, :] = y.reshape(8, 8, 128)


def green_kernel(meta, green, out, cols):
    q = lax.broadcasted_iota(jnp.int32, (128, N), 0)
    s = q & 31
    freq = jnp.where(s == 16, N // 2, meta[2] + (s >> 3) + 8 * (s & 7))
    freq = jnp.where(q >= 32, (N - freq) & (N - 1), freq)
    hit = (lax.broadcasted_iota(jnp.int32, (128, N), 1) == freq) & (s < 17) & (q < 64)
    cols[...] = nt(green[...], jnp.where(hit, 0.5, 0.0).astype(F32))
    line = lax.broadcasted_iota(jnp.int32, (64, 128), 0)
    place = lax.broadcasted_iota(jnp.int32, (64, 128), 1) & 63

    def both(back):
        table = jnp.concatenate([place == line, place == back], axis=0)
        return jnp.where(table, 1.0, 0.0).astype(F32)

    rows = []
    for k in range(16):
        same = cols[pl.ds(k, 64, stride=16), :].T
        mirrored = cols[pl.ds((16 - k) % 16, 64, stride=16), :].T
        rows.append(jnp.concatenate([same[0:24], mirrored[32:56]], axis=1))
    out[0] = nn(rows[0], both((64 - line) & 63))
    rest = nn(jnp.concatenate(rows[1:], axis=0), both(63 - line))
    for k in range(1, 16):
        out[k] = rest[24 * k - 24 : 24 * k]


def dft16(z, turned, sign):
    plus = [None] + [z[t] + z[16 - t] for t in range(1, 8)]
    minus = [None] + [turned[t] - turned[16 - t] for t in range(1, 8)]
    out = [None] * 16
    for k in range(9):
        even = z[0] + z[8] if k % 2 == 0 else z[0] - z[8]
        for t in range(1, 8):
            c = math.cos(2.0 * math.pi * (k * t % 16) / 16)
            if abs(c) > 1e-9:
                even = even + c * plus[t]
        odd = None
        for t in range(1, 8):
            s = math.sin(2.0 * math.pi * (k * t % 16) / 16)
            if abs(s) > 1e-9:
                term = s * minus[t]
                odd = term if odd is None else odd + term
        if odd is None:
            out[k] = even
        else:
            out[k] = even + sign * odd
            out[16 - k] = even - sign * odd
    return out


def column_kernel(meta, recv, green, twiddle, col, out):
    sign = jnp.where(lax.broadcasted_iota(jnp.int32, (1, 128), 1) < 64, -1.0, 1.0).astype(F32)
    imag = lax.broadcasted_iota(jnp.int32, (16, 128), 1) >= 64
    packed = imag & (lax.broadcasted_iota(jnp.int32, (16, 128), 0) == 0) & (meta[2] == 0)
    extra = jnp.where(packed, 1.0, 0.0).astype(F32)
    keep = 1.0 - extra
    extra = extra[0:8]
    z = []
    for t in range(16):
        x = recv[t]
        z.append(jnp.concatenate([x * keep, x[0:8] * extra], axis=0))
    turned = [pltpu.roll(x, 64, 1) * sign for x in z]
    y = dft16(z, turned, -1.0)
    y = [v * twiddle[0, k : k + 1, :] - pltpu.roll(v, 64, 1) * twiddle[1, k : k + 1, :] for k, v in enumerate(y)]
    f = nn(jnp.concatenate(y, axis=0), col[0])
    g = []
    for k in range(16):
        v = f[24 * k : 24 * k + 24] * green[k]
        g.append(v[0:8] + v[16:24])
        g.append(v[8:16])
    f = nn(jnp.concatenate(g, axis=0), col[1])
    y = [f[16 * k : 16 * k + 16] for k in range(16)]
    y = [v * twiddle[0, k : k + 1, :] + pltpu.roll(v, 64, 1) * twiddle[1, k : k + 1, :] for k, v in enumerate(y)]
    turned = [pltpu.roll(x, 64, 1) * sign for x in y]
    y = dft16(y, turned, 1.0)
    for t in range(16):
        out[t] = y[t]


def row_backward_kernel(meta, recv, line, bwd, out0, out1):
    real, imag = [], []
    for l1 in range(4):
        j, p = divmod(l1, 2)
        v = recv[8 * j : 8 * j + 8, 8 * p : 8 * p + 8, :].reshape(64, 128)
        y = nn(v.T, bwd[0, 0 if l1 == 0 else 1])
        real.append(y[0:64, 0:128] - y[64:128, 128:256])
        imag.append(y[0:64, 128:256] + y[64:128, 0:128])
    for t in range(8):
        acc = None
        for l1 in range(4):
            v = real[l1] * line[0, 0, l1, t : t + 1, :] - imag[l1] * line[0, 1, l1, t : t + 1, :]
            acc = v if acc is None else acc + v
        out0[:, 128 * t : 128 * t + 128] = acc[0:HALF]
        out1[:, 128 * t : 128 * t + 128] = acc[HALF:ROWS]


def shape(*dims):
    return jax.ShapeDtypeStruct(dims, F32)


def own(k, meta):
    return (meta[0] + k) % PLANES


CHUNK = pltpu.VMEM((PLANES, GRAINS, HALF, N), F32)
EDGE = pltpu.VMEM((PLANES, GRAINS, N), F32)
SUMS = pltpu.VMEM((HALF, N), F32)
VMEM_SPEC = pl.BlockSpec(memory_space=pltpu.VMEM)
SMEM_SPEC = pl.BlockSpec(memory_space=pltpu.SMEM)
ANY_SPEC = pl.BlockSpec(memory_space=pl.ANY)
HBM_SPEC = pl.BlockSpec(memory_space=pltpu.HBM)
STACKED = pltpu.VMEM((PLANES, HALF, N), F32)


def limit(mib):
    return pltpu.CompilerParams(vmem_limit_bytes=mib << 20)


def near(x):
    return pltpu.with_memory_space_constraint(x, pltpu.VMEM)


def squares(order, c, meta):
    outs = (CHUNK, SUMS, SUMS, SUMS, SUMS, EDGE, EDGE)
    out = pl.pallas_call(
        functools.partial(square_kernel, c), out_shape=outs, in_specs=[SMEM_SPEC, HBM_SPEC],
        out_specs=(VMEM_SPEC,) * 7, scratch_shapes=[pltpu.SemaphoreType.DMA((PLANES,))], name=f"squares{c}", compiler_params=limit(2),
    )(meta, order)
    return out[0], out[1:5], out[5], out[6]


def advance(step, c, eta, totals, above, below, weight, ready):
    last = step == STEPS - 1
    args = [near(x) for x in (eta, *totals, above, below)]
    outs = (CHUNK, SUMS, SUMS, SUMS, SUMS) + (() if last else (EDGE, EDGE))
    out = pl.pallas_call(
        functools.partial(step_kernel, last, len(ready)), out_shape=outs,
        in_specs=[ANY_SPEC] * len(ready) + ([SMEM_SPEC] if last else []) + [VMEM_SPEC] * 7, out_specs=(VMEM_SPEC,) * len(outs),
        scratch_shapes=[STACKED, STACKED], name=f"step{step}_{c}", compiler_params=limit(4),
    )(*ready, *([weight] if last else []), *args)
    return out[0], out[1:5], *((None, None) if last else out[5:7])


def final(c, eta, pots, weight, meta, previous):
    args = [meta, weight] + [near(x) for x in (eta, *pots)] + list(previous or ())
    return pl.pallas_call(
        functools.partial(final_kernel, c),
        out_shape=(shape(GRAINS, PLANES, ROWS, N), shape(PLANES, ROWS, N)),
        in_specs=[SMEM_SPEC, SMEM_SPEC] + [VMEM_SPEC] * 5 + [ANY_SPEC] * len(previous or ()),
        out_specs=(ANY_SPEC, ANY_SPEC),
        scratch_shapes=[CHUNK, STACKED] + [pltpu.SemaphoreType.DMA((PLANES,))] * 2,
        input_output_aliases={7: 0, 8: 1} if previous else {}, name=f"final{c}", compiler_params=limit(8),
    )(*args)


def call(kernel, name, outs, out_specs, in_specs, args, meta=None, grid=(1,)):
    spec = pltpu.PrefetchScalarGridSpec(
        num_scalar_prefetch=0 if meta is None else 1, grid=grid, in_specs=in_specs, out_specs=out_specs
    )
    args = args if meta is None else (meta, *args)
    return pl.pallas_call(kernel, out_shape=outs, grid_spec=spec, name=name, compiler_params=limit(8))(*args)


def whole(dims):
    return pl.BlockSpec(dims, lambda i, *_: (0,) * len(dims))


LINE_SPEC = pl.BlockSpec((1, 2, 4, 8, 128), lambda i, meta: (meta[1], 0, 0, 0, 0))
TABLE_SPEC = pl.BlockSpec((1, 2, 64, 256), lambda i, meta: (meta[1], 0, 0, 0))


def row_forward(s0, s1, meta):
    return call(
        row_forward_kernel, "row_forward", shape(16, 16, 128), whole((16, 16, 128)),
        [whole((HALF, N)), whole((HALF, N)), LINE_SPEC, TABLE_SPEC], (s0, s1, LINE, FWD), meta,
    )


def own_green(green, meta):
    return pl.pallas_call(
        green_kernel, out_shape=pltpu.VMEM((16, 24, 128), F32), in_specs=[SMEM_SPEC, VMEM_SPEC], out_specs=VMEM_SPEC,
        scratch_shapes=[pltpu.VMEM((N, 128), F32)], name="own_green", compiler_params=limit(16),
    )(meta, near(green))


def column(recv, green, meta):
    return call(
        column_kernel, "column", shape(16, 16, 128), whole((16, 16, 128)),
        [whole((16, 16, 128)), whole((16, 24, 128)), whole((2, 16, 128)), whole((2, 128, 128))],
        (recv, green, TWIDDLE, COL), meta,
    )


def row_backward(recv, meta):
    return call(
        row_backward_kernel, "row_backward", (shape(HALF, N), shape(HALF, N)), (whole((HALF, N)), whole((HALF, N))),
        [whole((16, 16, 128)), LINE_SPEC, TABLE_SPEC], (recv, LINE, BWD), meta,
    )


def shift(k):
    return [(i, (i + k) % PLANES) for i in range(PLANES)]


def to_owner(sums):
    acc = sums[0]
    for part in [lax.ppermute(sums[k], "z", shift(k)) for k in (2, 1, 3)]:
        acc = acc + part
    return acc


def with_partner(x):
    return x + lax.ppermute(x, "xh", [(0, 1), (1, 0)])


def to_all(x):
    parts = {k: lax.ppermute(x, "z", shift(-k)) for k in (2, 1, 3)}
    return [x, parts[1], parts[2], parts[3]]


def local(order_params, eigen_weight, green):
    xh = lax.axis_index("xh")
    row = lax.axis_index(ROW_AXES)
    base = 4 * xh + 2 * (row >> 3) + 64 * (row & 7)
    meta = jnp.stack([lax.axis_index("z"), xh, base]).astype(jnp.int32)
    row_count = 16
    up = [(i, (i + 1) % row_count) for i in range(row_count)]
    down = [(j, i) for i, j in up]
    chunks = (0, 1)

    eta, sums, top, bottom = [None] * 2, [None] * 2, [None] * 2, [None] * 2
    for c in chunks:
        eta[c], sums[c], top[c], bottom[c] = squares(order_params, c, meta)
    own_cols = own_green(green, meta)
    for step in range(STEPS):
        before = lax.ppermute(bottom[1], ROW_AXES, up)
        after = lax.ppermute(top[0], ROW_AXES, down)
        above, below = (before, bottom[0]), (top[1], after)
        totals = [to_all(with_partner(to_owner(sums[c]))) for c in chunks]
        for c in chunks:
            eta[c], sums[c], top[c], bottom[c] = advance(
                step, c, eta[c], totals[c], above[c], below[c], eigen_weight,
                [own_cols] if step == 1 else [],
            )
    strain = [with_partner(to_owner(sums[c])) for c in chunks]
    spectrum = row_forward(strain[0], strain[1], meta)
    spectrum = lax.all_to_all(spectrum, ROW_AXES, 0, 0, tiled=True)
    mixed = column(spectrum, own_cols, meta)
    mixed = lax.all_to_all(mixed, ROW_AXES, 0, 0, tiled=True)
    pots = row_backward(mixed, meta)
    pots = [to_all(with_partner(p)) for p in pots]
    result = None
    for c in chunks:
        result = final(c, eta[c], pots[c], eigen_weight, meta, result)
    return tuple(result)


def solution(mesh):
    fine = Mesh(mesh.devices.reshape(4, 2, 4, 2, 2), ("z", "xh", "y", "xl", "c"))
    field = P(("z", "xh"), None, ROW_AXES, None)
    return jax.shard_map(
        local,
        mesh=fine,
        in_specs=(field, P(("z", "xh")), P()),
        out_specs=(field, P(None, ROW_AXES, None)),
        check_vma=False,
    )
```

time: 251 us -> 186 us (0.74)
  Pallas kernels: 69.7 us -> 36.9 us
  other arithmetic: 19 us -> 0.53 us
  waiting for transfers between devices: 38.1 us -> 27.3 us
  local copies, waits for them, and re-layouts: 13.3 us -> 3.43 us
  blocking collectives: 10.9 us -> 19.5 us
  matrix products: 4.43 us -> 0 us
  starting transfers between devices: 92.7 us -> 95.7 us
    pallas_call x13 -> x14, Pallas kernels: 69.7 us -> 36.9 us  [the longest x6 19.2 us: advance(): pl.pallas_call(functools.partial(step_kernel, last, len(ready)), out_shap...]
    all_to_all x0 -> x1, blocking collectives: none -> 10.2 us  [local(): spectrum = lax.all_to_all(spectrum, ROW_AXES, 0, 0, tiled=True)]
    squeeze x8 -> x0, local copies, waits for them, and re-layouts: 7.42 us -> none  [to_owner(): sums[k]]
    another operation x9 -> x1, other arithmetic: 7.31 us -> 0.08 us  [local(): meta = jnp.stack([lax.axis_index('z'), xh, base]).astype(jnp.int32)]
    add x8, other arithmetic: 6.61 us -> 0.27 us  [to_owner(): acc = acc + part]
    ppermute x10, starting transfers between devices: 18.2 us -> 24.5 us  [with_partner(): return x + lax.ppermute(x, 'xh', [(0, 1), (1, 0)])]
    ppermute x24, waiting for transfers between devices: 12.6 us -> 6.35 us  [to_owner(): lax.ppermute(sums[k], 'z', shift(k))]
    all_to_all x1 -> x0, waiting for transfers between devices: 4.69 us -> none  [local(): spectrum = lax.all_to_all(spectrum, ROW_AXES, 0, 0, tiled=True)]
  transfers between devices with their start and end apart: 65 -> 64, of which waited for: 20 -> 18; matrix products, arithmetic and copies ran while one was open for 12% -> 0% of each run, Pallas kernels for 20% -> 16%
where the time goes in v2:
time: 186 us; the launch traced here: 184 us
  starting transfers between devices  95.7 us (51%)
  Pallas kernels  36.9 us (20%)
  waiting for transfers between devices  27.3 us (15%)
  blocking collectives  19.5 us (10%)
  local copies, waits for them, and re-layouts  3.43 us (2%)
    ppermute x24, starting transfers between devices, to_owner(): lax.ppermute(sums[k], 'z', shift(k))  38 us
    ppermute x24, starting transfers between devices, to_all(): parts = {k: lax.ppermute(x, 'z', shift(-k)) for k in (2, 1, 3)}  28.9 us
    ppermute x10, starting transfers between devices, with_partner(): return x + lax.ppermute(x, 'xh', [(0, 1), (1, 0)])  24.5 us
    pallas_call x6, Pallas kernels, advance(): pl.pallas_call(functools.partial(step_kernel, last, len(ready)), out_shap...  19.2 us
    ppermute x24, waiting for transfers between devices, to_all(): parts = {k: lax.ppermute(x, 'z', shift(-k)) for k in (2, 1, 3)}  12.2 us
    all_to_all x1, blocking collectives, local(): spectrum = lax.all_to_all(spectrum, ROW_AXES, 0, 0, tiled=True)  10.2 us
    all_to_all x1, blocking collectives, local(): mixed = lax.all_to_all(mixed, ROW_AXES, 0, 0, tiled=True)  9.29 us
    ppermute x10, waiting for transfers between devices, with_partner(): return x + lax.ppermute(x, 'xh', [(0, 1), (1, 0)])  8.76 us
  transfers between devices with their start and end apart: 64, of which 18 were waited for; matrix products, arithmetic and copies ran while one was open for 0% of the time, Pallas kernels for 16%

profile of v2, /device:TPU:0, one launch (start us, length us, event | category | flops | bytes accessed | tf_op | source)
XLA Modules:
  0.0 184.4 jit_solution(7656404731022226981)
XLA Ops:
  0.7 3.4 %copy-done = f32[8,4,64,1024]{3,2,1,0:T(8,128)S(1)} copy-done((f32[8,4,64,1024]{3,2,1,0:T(8,128)S(1)}, f32[8,4,64,1024]{3,2,1,0:T(8,128)}, u32[]{:S(2)}) %copy-start) | copy-done | bytes 8388632
  5.3 4.1 %collective-permute-start = (f32[32,1024]{1,0:T(8,128)S(1)}, f32[32,1024]{1,0:T(8,128)S(1)}, u32[]{:S(2)}, u32[]{:S(2)}) collective-permute-start(f32[32,1024]{1,0:T(8,128)S(1)} %get-tuple-element.60), channel_id=1, source_target_pairs={{0,64},{32,96},{64,0},{96,32},{1,65},{33,97},{65,1},{97,33},{2,66}... | collective-permute-start | bytes 393224 | tf_op jit(solution)/shard_map/ppermute | solution.py:381
  10.4 2.2 %collective-permute-start.2 = (f32[32,1024]{1,0:T(8,128)S(1)}, f32[32,1024]{1,0:T(8,128)S(1)}, u32[]{:S(2)}, u32[]{:S(2)}) collective-permute-start(f32[32,1024]{1,0:T(8,128)S(1)} %get-tuple-element.62), channel_id=1, source_target_pairs={{0,96},{32,0},{64,32},{96,64},{1,97},{33,1},{65,33},{97,65},{2,98}... | collective-permute-start | bytes 393224 | tf_op jit(solution)/shard_map/ppermute | solution.py:381
  14.8 2.6 %collective-permute-start.17 = (f32[32,1024]{1,0:T(8,128)S(1)}, f32[32,1024]{1,0:T(8,128)S(1)}, u32[]{:S(2)}, u32[]{:S(2)}) collective-permute-start(f32[32,1024]{1,0:T(8,128)S(1)} %get-tuple-element.74), channel_id=1, source_target_pairs={{0,96},{32,0},{64,32},{96,64},{1,97},{33,1},{65,33},{97,65},{2,98}... | collective-permute-start | bytes 393224 | tf_op jit(solution)/shard_map/ppermute | solution.py:381
  18.2 3.1 %collective-permute-start.3 = (f32[32,1024]{1,0:T(8,128)S(1)}, f32[32,1024]{1,0:T(8,128)S(1)}, u32[]{:S(2)}, u32[]{:S(2)}) collective-permute-start(f32[32,1024]{1,0:T(8,128)S(1)} %add_add_fusion.7), channel_id=1, source_target_pairs={{0,16},{16,0},{1,17},{17,1},{2,18},{18,2},{3,19},{19,3},{4,20},{20... | collective-permute-start | bytes 393224 | tf_op jit(solution)/shard_map/ppermute | solution.py:387
  22.4 3.1 %collective-permute-start.18 = (f32[32,1024]{1,0:T(8,128)S(1)}, f32[32,1024]{1,0:T(8,128)S(1)}, u32[]{:S(2)}, u32[]{:S(2)}) collective-permute-start(f32[32,1024]{1,0:T(8,128)S(1)} %add_add_fusion.5), channel_id=1, source_target_pairs={{0,16},{16,0},{1,17},{17,1},{2,18},{18,2},{3,19},{19,3},{4,20},{20... | collective-permute-start | bytes 393224 | tf_op jit(solution)/shard_map/ppermute | solution.py:387
  25.6 1.9 %collective-permute-start.7 = (f32[4,8,1024]{2,1,0:T(8,128)S(1)}, f32[4,8,1024]{2,1,0:T(8,128)S(1)}, u32[]{:S(2)}, u32[]{:S(2)}) collective-permute-start(f32[4,8,1024]{2,1,0:T(8,128)S(1)} %get-tuple-element.64), channel_id=1, source_target_pairs={{1,0},{2,1},{3,2},{4,3},{5,4},{6,5},{7,6},{8,7},{9,8},{10,9},{11,1... | collective-permute-start | bytes 393224 | tf_op jit(solution)/shard_map/ppermute | solution.py:411
  27.7 3.9 %collective-permute-start.5 = (f32[32,1024]{1,0:T(8,128)S(1)}, f32[32,1024]{1,0:T(8,128)S(1)}, u32[]{:S(2)}, u32[]{:S(2)}) collective-permute-start(f32[32,1024]{1,0:T(8,128)S(1)} %add.121.refs_1_), channel_id=1, source_target_pairs={{0,64},{32,96},{64,0},{96,32},{1,65},{33,97},{65,1},{97,33},{2,66}... | collective-permute-start | bytes 393224 | tf_op jit(solution)/shard_map/ppermute | solution.py:391
  31.9 1.9 %collective-permute-start.21 = (f32[32,1024]{1,0:T(8,128)S(1)}, f32[32,1024]{1,0:T(8,128)S(1)}, u32[]{:S(2)}, u32[]{:S(2)}) collective-permute-start(f32[32,1024]{1,0:T(8,128)S(1)} %add.129.refs_1_), channel_id=1, source_target_pairs={{0,32},{32,64},{64,96},{96,0},{1,33},{33,65},{65,97},{97,1},{2,34}... | collective-permute-start | bytes 393224 | tf_op jit(solution)/shard_map/ppermute | solution.py:391
  35.0 2.3 %collective-permute-done.5.refs_3_ = f32[32,1024]{1,0:T(8,128)S(1)} collective-permute-done((f32[32,1024]{1,0:T(8,128)S(1)}, f32[32,1024]{1,0:T(8,128)S(1)}, u32[]{:S(2)}, u32[]{:S(2)}) %collective-permute-start.5) | collective-permute-done | bytes 131104 | tf_op jit(solution)/shard_map/ppermute | solution.py:391
  37.8 3.0 %step0_1.1 = (f32[4,8,32,1024]{3,2,1,0:T(8,128)S(1)}, f32[32,1024]{1,0:T(8,128)S(1)}, f32[32,1024]{1,0:T(8,128)S(1)}, f32[32,1024]{1,0:T(8,128)S(1)}, f32[32,102...) custom-call(f32[4,8,32,1024]{3,2,1,0:T(8,128)S(1)} %get-tuple-element.58.refs_0_, ...), custom_call_target="tpu_custom_call" | custom-call | tf_op jit(solution)/shard_map/step0_1/pallas_call | solution.py:310
  43.1 2.1 %collective-permute-start.10 = (f32[32,1024]{1,0:T(8,128)S(1)}, f32[32,1024]{1,0:T(8,128)S(1)}, u32[]{:S(2)}, u32[]{:S(2)}) collective-permute-start(f32[32,1024]{1,0:T(8,128)S(1)} %get-tuple-element.69), channel_id=1, source_target_pairs={{0,96},{32,0},{64,32},{96,64},{1,97},{33,1},{65,33},{97,65},{2,98}... | collective-permute-start | bytes 393224 | tf_op jit(solution)/shard_map/ppermute | solution.py:381
  45.2 3.0 %step0_0.1 = (f32[4,8,32,1024]{3,2,1,0:T(8,128)S(1)}, f32[32,1024]{1,0:T(8,128)S(1)}, f32[32,1024]{1,0:T(8,128)S(1)}, f32[32,1024]{1,0:T(8,128)S(1)}, f32[32,102...) custom-call(f32[4,8,32,1024]{3,2,1,0:T(8,128)S(1)} %get-tuple-element.70.refs_0_, ...), custom_call_target="tpu_custom_call" | custom-call | tf_op jit(solution)/shard_map/step0_0/pallas_call | solution.py:310
  51.1 1.8 collective-permute-start.33
  53.0 1.5 collective-permute-start.11
  56.2 2.6 %collective-permute-start.34 = (f32[32,1024]{1,0:T(8,128)S(1)}, f32[32,1024]{1,0:T(8,128)S(1)}, u32[]{:S(2)}, u32[]{:S(2)}) collective-permute-start(f32[32,1024]{1,0:T(8,128)S(1)} %add_add_fusion.3), channel_id=1, source_target_pairs={{0,16},{16,0},{1,17},{17,1},{2,18},{18,2},{3,19},{19,3},{4,20},{20... | collective-permute-start | bytes 393224 | tf_op jit(solution)/shard_map/ppermute | solution.py:387
  61.1 1.7 collective-permute-start.13
  65.0 5.4 %own_green.1.refs_0_.green = f32[16,24,128]{2,1,0:T(8,128)S(1)} custom-call(s32[3]{0:T(128)S(1)} %pad_add_fusion.meta, f32[1024,1024]{1,0:T(8,128)S(1)} %copy-done.1), custom_call_target="tpu_custom_call" | custom-call | tf_op jit(solution)/shard_map/own_green/pallas_call | solution.py:354
  70.4 2.4 %collective-permute-start.36 = (f32[32,1024]{1,0:T(8,128)S(1)}, f32[32,1024]{1,0:T(8,128)S(1)}, u32[]{:S(2)}, u32[]{:S(2)}) collective-permute-start(f32[32,1024]{1,0:T(8,128)S(1)} %add.137.refs_2_), channel_id=1, source_target_pairs={{0,64},{32,96},{64,0},{96,32},{1,65},{33,97},{65,1},{97,33},{2,66}... | collective-permute-start | bytes 393224 | tf_op jit(solution)/shard_map/ppermute | solution.py:391
  72.8 1.8 collective-permute-start.35
  74.6 3.0 %step1_1.1 = (f32[4,8,32,1024]{3,2,1,0:T(8,128)S(1)}, f32[32,1024]{1,0:T(8,128)S(1)}, f32[32,1024]{1,0:T(8,128)S(1)}, f32[32,1024]{1,0:T(8,128)S(1)}, f32[32,102...) custom-call(f32[16,24,128]{2,1,0:T(8,128)S(1)} %own_green.1.refs_0_.green, ...), custom_call_target="tpu_custom_call" | custom-call | tf_op jit(solution)/shard_map/step1_1/pallas_call | solution.py:310
  79.0 3.2 %collective-permute-start.26 = (f32[32,1024]{1,0:T(8,128)S(1)}, f32[32,1024]{1,0:T(8,128)S(1)}, u32[]{:S(2)}, u32[]{:S(2)}) collective-permute-start(f32[32,1024]{1,0:T(8,128)S(1)} %get-tuple-element.83), channel_id=1, source_target_pairs={{0,96},{32,0},{64,32},{96,64},{1,97},{33,1},{65,33},{97,65},{2,98}... | collective-permute-start | bytes 393224 | tf_op jit(solution)/shard_map/ppermute | solution.py:381
  82.2 3.0 %step1_0.1 = (f32[4,8,32,1024]{3,2,1,0:T(8,128)S(1)}, f32[32,1024]{1,0:T(8,128)S(1)}, f32[32,1024]{1,0:T(8,128)S(1)}, f32[32,1024]{1,0:T(8,128)S(1)}, f32[32,102...) custom-call(f32[16,24,128]{2,1,0:T(8,128)S(1)} %own_green.1.refs_0_.green, ...), custom_call_target="tpu_custom_call" | custom-call | tf_op jit(solution)/shard_map/step1_0/pallas_call | solution.py:310
  87.6 2.0 %collective-permute-start.42 = (f32[32,1024]{1,0:T(8,128)S(1)}, f32[32,1024]{1,0:T(8,128)S(1)}, u32[]{:S(2)}, u32[]{:S(2)}) collective-permute-start(f32[32,1024]{1,0:T(8,128)S(1)} %get-tuple-element.98), channel_id=1, source_target_pairs={{0,96},{32,0},{64,32},{96,64},{1,97},{33,1},{65,33},{97,65},{2,98}... | collective-permute-start | bytes 393224 | tf_op jit(solution)/shard_map/ppermute | solution.py:381
  89.7 2.5 %collective-permute-start.27 = (f32[32,1024]{1,0:T(8,128)S(1)}, f32[32,1024]{1,0:T(8,128)S(1)}, u32[]{:S(2)}, u32[]{:S(2)}) collective-permute-start(f32[32,1024]{1,0:T(8,128)S(1)} %add_add_fusion.4), channel_id=1, source_target_pairs={{0,16},{16,0},{1,17},{17,1},{2,18},{18,2},{3,19},{19,3},{4,20},{20... | collective-permute-start | bytes 393224 | tf_op jit(solution)/shard_map/ppermute | solution.py:387
  93.9 3.0 %collective-permute-start.43 = (f32[32,1024]{1,0:T(8,128)S(1)}, f32[32,1024]{1,0:T(8,128)S(1)}, u32[]{:S(2)}, u32[]{:S(2)}) collective-permute-start(f32[32,1024]{1,0:T(8,128)S(1)} %add_add_fusion.2), channel_id=1, source_target_pairs={{0,16},{16,0},{1,17},{17,1},{2,18},{18,2},{3,19},{19,3},{4,20},{20... | collective-permute-start | bytes 393224 | tf_op jit(solution)/shard_map/ppermute | solution.py:387
  96.9 1.7 collective-permute-start.39
  98.7 2.6 %collective-permute-start.29 = (f32[32,1024]{1,0:T(8,128)S(1)}, f32[32,1024]{1,0:T(8,128)S(1)}, u32[]{:S(2)}, u32[]{:S(2)}) collective-permute-start(f32[32,1024]{1,0:T(8,128)S(1)} %add.133.refs_2_), channel_id=1, source_target_pairs={{0,64},{32,96},{64,0},{96,32},{1,65},{33,97},{65,1},{97,33},{2,66}... | collective-permute-start | bytes 393224 | tf_op jit(solution)/shard_map/ppermute | solution.py:391
  103.4 4.0 %collective-permute-done.30.refs_5_ = f32[32,1024]{1,0:T(8,128)S(1)} collective-permute-done((f32[32,1024]{1,0:T(8,128)S(1)}, f32[32,1024]{1,0:T(8,128)S(1)}, u32[]{:S(2)}, u32[]{:S(2)}) %collective-permute-start.30) | collective-permute-done | bytes 131104 | tf_op jit(solution)/shard_map/ppermute | solution.py:391
  108.8 3.6 %step2_1.1 = (f32[4,8,32,1024]{3,2,1,0:T(8,128)S(1)}, f32[32,1024]{1,0:T(8,128)S(1)}, f32[32,1024]{1,0:T(8,128)S(1)}, f32[32,1024]{1,0:T(8,128)S(1)}, f32[32,1024]{1,0:T(8,128)S(1)}) custom-call(f32[8]{0:T(128)S(1)} %copy-done.7, f32[4,8,32,1024]{3,2,1,0:T(8,128)S(1)} %get-tuple-element.79.refs_1_, f32[32,1024]{1,0:T(8,128)S(1)} %add.133.refs_2_, ...), custom_call_target="tpu_custom_call" | custom-call | tf_op jit(solution)/shard_map/step2_1/pallas_call | solution.py:310
  112.5 2.3 %collective-permute-start.52 = (f32[32,1024]{1,0:T(8,128)S(1)}, f32[32,1024]{1,0:T(8,128)S(1)}, u32[]{:S(2)}, u32[]{:S(2)}) collective-permute-start(f32[32,1024]{1,0:T(8,128)S(1)} %get-tuple-element.106), channel_id=1, source_target_pairs={{0,64},{32,96},{64,0},{96,32},{1,65},{33,97},{65,1},{97,33},{2,66}... | collective-permute-start | bytes 393224 | tf_op jit(solution)/shard_map/ppermute | solution.py:381
  116.1 1.8 collective-permute-start.54
  118.0 3.6 %step2_0.1 = (f32[4,8,32,1024]{3,2,1,0:T(8,128)S(1)}, f32[32,1024]{1,0:T(8,128)S(1)}, f32[32,1024]{1,0:T(8,128)S(1)}, f32[32,1024]{1,0:T(8,128)S(1)}, f32[32,1024]{1,0:T(8,128)S(1)}) custom-call(f32[8]{0:T(128)S(1)} %copy-done.7, f32[4,8,32,1024]{3,2,1,0:T(8,128)S(1)} %get-tuple-element.94.refs_1_, f32[32,1024]{1,0:T(8,128)S(1)} %add.141.refs_2_, ...), custom_call_target="tpu_custom_call" | custom-call | tf_op jit(solution)/shard_map/step2_0/pallas_call | solution.py:310
  122.5 2.7 %collective-permute-start.50 = (f32[32,1024]{1,0:T(8,128)S(1)}, f32[32,1024]{1,0:T(8,128)S(1)}, u32[]{:S(2)}, u32[]{:S(2)}) collective-permute-start(f32[32,1024]{1,0:T(8,128)S(1)} %get-tuple-element.104), channel_id=1, source_target_pairs={{0,96},{32,0},{64,32},{96,64},{1,97},{33,1},{65,33},{97,65},{2,98}... | collective-permute-start | bytes 393224 | tf_op jit(solution)/shard_map/ppermute | solution.py:381
  125.3 3.2 %collective-permute-start.55 = (f32[32,1024]{1,0:T(8,128)S(1)}, f32[32,1024]{1,0:T(8,128)S(1)}, u32[]{:S(2)}, u32[]{:S(2)}) collective-permute-start(f32[32,1024]{1,0:T(8,128)S(1)} %add_add_fusion), channel_id=1, source_target_pairs={{0,16},{16,0},{1,17},{17,1},{2,18},{18,2},{3,19},{19,3},{4,20},{20... | collective-permute-start | bytes 393224 | tf_op jit(solution)/shard_map/ppermute | solution.py:387
  129.6 1.8 collective-permute-start.51
  131.8 4.3 %collective-permute-done.51 = f32[32,1024]{1,0:T(8,128)S(1)} collective-permute-done((f32[32,1024]{1,0:T(8,128)S(1)}, f32[32,1024]{1,0:T(8,128)S(1)}, u32[]{:S(2)}, u32[]{:S(2)}) %collective-permute-start.51) | collective-permute-done | bytes 131104 | tf_op jit(solution)/shard_map/ppermute | solution.py:387
  137.4 10.2 %all_to_all.10.recv = f32[16,16,128]{2,1,0:T(8,128)S(1)} all-to-all(f32[16,16,128]{2,1,0:T(8,128)S(1)} %row_forward.1), channel_id=1, replica_groups=mesh['z'=4,'xh'=2,'y'=4,'xl'=2,'c'=2] {'y','xl','c'}, dimensions={0} | all-to-all | bytes 262144 | tf_op jit(solution)/shard_map/all_to_all | solution.py:421
  147.6 1.6 column.1
  149.2 9.3 %all_to_all.11.recv = f32[16,16,128]{2,1,0:T(8,128)S(1)} all-to-all(f32[16,16,128]{2,1,0:T(8,128)S(1)} %column.1), channel_id=1, replica_groups=mesh['z'=4,'xh'=2,'y'=4,'xl'=2,'c'=2] {'y','xl','c'}, dimensions={0} | all-to-all | bytes 262144 | tf_op jit(solution)/shard_map/all_to_all | solution.py:423
  159.7 2.8 %collective-permute-start.60 = (f32[32,1024]{1,0:T(8,128)S(1)}, f32[32,1024]{1,0:T(8,128)S(1)}, u32[]{:S(2)}, u32[]{:S(2)}) collective-permute-start(f32[32,1024]{1,0:T(8,128)S(1)} %get-tuple-element.111), channel_id=1, source_target_pairs={{0,16},{16,0},{1,17},{17,1},{2,18},{18,2},{3,19},{19,3},{4,20},{20... | collective-permute-start | bytes 393224 | tf_op jit(solution)/shard_map/ppermute | solution.py:387
  163.3 3.5 %collective-permute-done.60 = f32[32,1024]{1,0:T(8,128)S(1)} collective-permute-done((f32[32,1024]{1,0:T(8,128)S(1)}, f32[32,1024]{1,0:T(8,128)S(1)}, u32[]{:S(2)}, u32[]{:S(2)}) %collective-permute-start.60) | collective-permute-done | bytes 131104 | tf_op jit(solution)/shard_map/ppermute | solution.py:387
  167.0 3.6 %collective-permute-start.62 = (f32[32,1024]{1,0:T(8,128)S(1)}, f32[32,1024]{1,0:T(8,128)S(1)}, u32[]{:S(2)}, u32[]{:S(2)}) collective-permute-start(f32[32,1024]{1,0:T(8,128)S(1)} %add.151.p0), channel_id=1, source_target_pairs={{0,64},{32,96},{64,0},{96,32},{1,65},{33,97},{65,1},{97,33},{2,66}... | collective-permute-start | bytes 393224 | tf_op jit(solution)/shard_map/ppermute | solution.py:391
  170.6 2.1 %collective-permute-start.59 = (f32[32,1024]{1,0:T(8,128)S(1)}, f32[32,1024]{1,0:T(8,128)S(1)}, u32[]{:S(2)}, u32[]{:S(2)}) collective-permute-start(f32[32,1024]{1,0:T(8,128)S(1)} %add.150.p0), channel_id=1, source_target_pairs={{0,32},{32,64},{64,96},{96,0},{1,33},{33,65},{65,97},{97,1},{2,34}... | collective-permute-start | bytes 393224 | tf_op jit(solution)/shard_map/ppermute | solution.py:391
  173.3 2.0 %collective-permute-done.63.p3 = f32[32,1024]{1,0:T(8,128)S(1)} collective-permute-done((f32[32,1024]{1,0:T(8,128)S(1)}, f32[32,1024]{1,0:T(8,128)S(1)}, u32[]{:S(2)}, u32[]{:S(2)}) %collective-permute-start.63) | collective-permute-done | bytes 131104 | tf_op jit(solution)/shard_map/ppermute | solution.py:391
  175.9 1.8 collective-permute-done.62.p2
  178.3 2.9 %final0.1 = (f32[8,4,64,1024]{3,2,1,0:T(8,128)}, f32[4,64,1024]{2,1,0:T(8,128)}) custom-call(s32[3]{0:T(128)S(1)} %pad_add_fusion.meta, f32[8]{0:T(128)S(1)} %copy-done.7, f32[4,8,32,1024]{3,2,1,0:T(8,128)S(1)} %get-tuple-element.110.eta, f32[32,1024]{1,0:T(8,128)S(1)} %add.151.p0, f32[32,1024]{1,0:T(8,128)S(1)} %collective-permute-done.61.p1, ...), custom_call_target="tpu_custom_call" | custom-call | tf_op jit(solution)/shard_map/final0/pallas_call | solution.py:320
  181.4 2.9 %final1.1 = (f32[8,4,64,1024]{3,2,1,0:T(8,128)}, f32[4,64,1024]{2,1,0:T(8,128)}) custom-call(s32[3]{0:T(128)S(1)} %pad_add_fusion.meta, f32[8]{0:T(128)S(1)} %copy-done.7, f32[4,8,32,1024]{3,2,1,0:T(8,128)S(1)} %get-tuple-element.93.eta, f32[32,1024]{1,0:T(8,128)S(1)} %add.150.p0, ...), custom_call_target="tpu_custom_call", output_to_operand_aliasing={{0}: (7, {}), {1}: (8, {})} | custom-call | tf_op jit(solution)/shard_map/final1/pallas_call | solution.py:320
  (131 shorter events, 38.3 us)
Async XLA Ops:
  5.3 9.5 %collective-permute-start = (f32[32,1024]{1,0:T(8,128)S(1)}, f32[32,1024]{1,0:T(8,128)S(1)}, u32[]{:S(2)}, u32[]{:S(2)}) collective-permute-start(f32[32,1024]{1,0:T(8,128)S(1)} %get-tuple-element.60), channel_id=1, source_target_pairs={{0,64},{32,96},{64,0},{96,32},{1,65},{33,97},{65,1},{97,33},{2,66}... | collective-permute-start | bytes 393224 | tf_op jit(solution)/shard_map/ppermute | solution.py:381
  9.4 8.0 %collective-permute-start.1 = (f32[32,1024]{1,0:T(8,128)S(1)}, f32[32,1024]{1,0:T(8,128)S(1)}, u32[]{:S(2)}, u32[]{:S(2)}) collective-permute-start(f32[32,1024]{1,0:T(8,128)S(1)} %get-tuple-element.61), channel_id=1, source_target_pairs={{0,32},{32,64},{64,96},{96,0},{1,33},{33,65},{65,97},{97,1},{2,34}... | collective-permute-start | bytes 393224 | tf_op jit(solution)/shard_map/ppermute | solution.py:381
  10.4 7.7 %collective-permute-start.2 = (f32[32,1024]{1,0:T(8,128)S(1)}, f32[32,1024]{1,0:T(8,128)S(1)}, u32[]{:S(2)}, u32[]{:S(2)}) collective-permute-start(f32[32,1024]{1,0:T(8,128)S(1)} %get-tuple-element.62), channel_id=1, source_target_pairs={{0,96},{32,0},{64,32},{96,64},{1,97},{33,1},{65,33},{97,65},{2,98}... | collective-permute-start | bytes 393224 | tf_op jit(solution)/shard_map/ppermute | solution.py:381
  13.8 7.5 %collective-permute-start.15 = (f32[32,1024]{1,0:T(8,128)S(1)}, f32[32,1024]{1,0:T(8,128)S(1)}, u32[]{:S(2)}, u32[]{:S(2)}) collective-permute-start(f32[32,1024]{1,0:T(8,128)S(1)} %get-tuple-element.72), channel_id=1, source_target_pairs={{0,64},{32,96},{64,0},{96,32},{1,65},{33,97},{65,1},{97,33},{2,66}... | collective-permute-start | bytes 393224 | tf_op jit(solution)/shard_map/ppermute | solution.py:381
  13.9 8.5 %collective-permute-start.16 = (f32[32,1024]{1,0:T(8,128)S(1)}, f32[32,1024]{1,0:T(8,128)S(1)}, u32[]{:S(2)}, u32[]{:S(2)}) collective-permute-start(f32[32,1024]{1,0:T(8,128)S(1)} %get-tuple-element.73), channel_id=1, source_target_pairs={{0,32},{32,64},{64,96},{96,0},{1,33},{33,65},{65,97},{97,1},{2,34}... | collective-permute-start | bytes 393224 | tf_op jit(solution)/shard_map/ppermute | solution.py:381
  14.8 7.6 %collective-permute-start.17 = (f32[32,1024]{1,0:T(8,128)S(1)}, f32[32,1024]{1,0:T(8,128)S(1)}, u32[]{:S(2)}, u32[]{:S(2)}) collective-permute-start(f32[32,1024]{1,0:T(8,128)S(1)} %get-tuple-element.74), channel_id=1, source_target_pairs={{0,96},{32,0},{64,32},{96,64},{1,97},{33,1},{65,33},{97,65},{2,98}... | collective-permute-start | bytes 393224 | tf_op jit(solution)/shard_map/ppermute | solution.py:381
  18.2 9.3 %collective-permute-start.3 = (f32[32,1024]{1,0:T(8,128)S(1)}, f32[32,1024]{1,0:T(8,128)S(1)}, u32[]{:S(2)}, u32[]{:S(2)}) collective-permute-start(f32[32,1024]{1,0:T(8,128)S(1)} %add_add_fusion.7), channel_id=1, source_target_pairs={{0,16},{16,0},{1,17},{17,1},{2,18},{18,2},{3,19},{19,3},{4,20},{20... | collective-permute-start | bytes 393224 | tf_op jit(solution)/shard_map/ppermute | solution.py:387
  22.4 9.4 %collective-permute-start.18 = (f32[32,1024]{1,0:T(8,128)S(1)}, f32[32,1024]{1,0:T(8,128)S(1)}, u32[]{:S(2)}, u32[]{:S(2)}) collective-permute-start(f32[32,1024]{1,0:T(8,128)S(1)} %add_add_fusion.5), channel_id=1, source_target_pairs={{0,16},{16,0},{1,17},{17,1},{2,18},{18,2},{3,19},{19,3},{4,20},{20... | collective-permute-start | bytes 393224 | tf_op jit(solution)/shard_map/ppermute | solution.py:387
  27.5 7.5 %collective-permute-start.6 = (f32[32,1024]{1,0:T(8,128)S(1)}, f32[32,1024]{1,0:T(8,128)S(1)}, u32[]{:S(2)}, u32[]{:S(2)}) collective-permute-start(f32[32,1024]{1,0:T(8,128)S(1)} %add.121.refs_1_), channel_id=1, source_target_pairs={{0,32},{32,64},{64,96},{96,0},{1,33},{33,65},{65,97},{97,1},{2,34}... | collective-permute-start | bytes 393224 | tf_op jit(solution)/shard_map/ppermute | solution.py:391
  27.7 9.6 %collective-permute-start.5 = (f32[32,1024]{1,0:T(8,128)S(1)}, f32[32,1024]{1,0:T(8,128)S(1)}, u32[]{:S(2)}, u32[]{:S(2)}) collective-permute-start(f32[32,1024]{1,0:T(8,128)S(1)} %add.121.refs_1_), channel_id=1, source_target_pairs={{0,64},{32,96},{64,0},{96,32},{1,65},{33,97},{65,1},{97,33},{2,66}... | collective-permute-start | bytes 393224 | tf_op jit(solution)/shard_map/ppermute | solution.py:391
  31.8 9.8 %collective-permute-start.22 = (f32[4,8,1024]{2,1,0:T(8,128)S(1)}, f32[4,8,1024]{2,1,0:T(8,128)S(1)}, u32[]{:S(2)}, u32[]{:S(2)}) collective-permute-start(f32[4,8,1024]{2,1,0:T(8,128)S(1)} %get-tuple-element.75), channel_id=1, source_target_pairs={{0,1},{1,2},{2,3},{3,4},{4,5},{5,6},{6,7},{7,8},{8,9},{9,10},{10,1... | collective-permute-start | bytes 393224 | tf_op jit(solution)/shard_map/ppermute | solution.py:410
  31.9 11.2 %collective-permute-start.21 = (f32[32,1024]{1,0:T(8,128)S(1)}, f32[32,1024]{1,0:T(8,128)S(1)}, u32[]{:S(2)}, u32[]{:S(2)}) collective-permute-start(f32[32,1024]{1,0:T(8,128)S(1)} %add.129.refs_1_), channel_id=1, source_target_pairs={{0,32},{32,64},{64,96},{96,0},{1,33},{33,65},{65,97},{97,1},{2,34}... | collective-permute-start | bytes 393224 | tf_op jit(solution)/shard_map/ppermute | solution.py:391
  35.0 10.2 %collective-permute-start.20 = (f32[32,1024]{1,0:T(8,128)S(1)}, f32[32,1024]{1,0:T(8,128)S(1)}, u32[]{:S(2)}, u32[]{:S(2)}) collective-permute-start(f32[32,1024]{1,0:T(8,128)S(1)} %add.129.refs_1_), channel_id=1, source_target_pairs={{0,64},{32,96},{64,0},{96,32},{1,65},{33,97},{65,1},{97,33},{2,66}... | collective-permute-start | bytes 393224 | tf_op jit(solution)/shard_map/ppermute | solution.py:391
  37.3 7.9 %collective-permute-start.19 = (f32[32,1024]{1,0:T(8,128)S(1)}, f32[32,1024]{1,0:T(8,128)S(1)}, u32[]{:S(2)}, u32[]{:S(2)}) collective-permute-start(f32[32,1024]{1,0:T(8,128)S(1)} %add.129.refs_1_), channel_id=1, source_target_pairs={{0,96},{32,0},{64,32},{96,64},{1,97},{33,1},{65,33},{97,65},{2,98}... | collective-permute-start | bytes 393224 | tf_op jit(solution)/shard_map/ppermute | solution.py:391
  40.8 10.3 %collective-permute-start.8 = (f32[32,1024]{1,0:T(8,128)S(1)}, f32[32,1024]{1,0:T(8,128)S(1)}, u32[]{:S(2)}, u32[]{:S(2)}) collective-permute-start(f32[32,1024]{1,0:T(8,128)S(1)} %get-tuple-element.67), channel_id=1, source_target_pairs={{0,64},{32,96},{64,0},{96,32},{1,65},{33,97},{65,1},{97,33},{2,66}... | collective-permute-start | bytes 393224 | tf_op jit(solution)/shard_map/ppermute | solution.py:381
  41.6 11.3 %collective-permute-start.9 = (f32[32,1024]{1,0:T(8,128)S(1)}, f32[32,1024]{1,0:T(8,128)S(1)}, u32[]{:S(2)}, u32[]{:S(2)}) collective-permute-start(f32[32,1024]{1,0:T(8,128)S(1)} %get-tuple-element.68), channel_id=1, source_target_pairs={{0,32},{32,64},{64,96},{96,0},{1,33},{33,65},{65,97},{97,1},{2,34}... | collective-permute-start | bytes 393224 | tf_op jit(solution)/shard_map/ppermute | solution.py:381
  43.1 9.9 %collective-permute-start.10 = (f32[32,1024]{1,0:T(8,128)S(1)}, f32[32,1024]{1,0:T(8,128)S(1)}, u32[]{:S(2)}, u32[]{:S(2)}) collective-permute-start(f32[32,1024]{1,0:T(8,128)S(1)} %get-tuple-element.69), channel_id=1, source_target_pairs={{0,96},{32,0},{64,32},{96,64},{1,97},{33,1},{65,33},{97,65},{2,98}... | collective-permute-start | bytes 393224 | tf_op jit(solution)/shard_map/ppermute | solution.py:381
  56.2 7.9 %collective-permute-start.34 = (f32[32,1024]{1,0:T(8,128)S(1)}, f32[32,1024]{1,0:T(8,128)S(1)}, u32[]{:S(2)}, u32[]{:S(2)}) collective-permute-start(f32[32,1024]{1,0:T(8,128)S(1)} %add_add_fusion.3), channel_id=1, source_target_pairs={{0,16},{16,0},{1,17},{17,1},{2,18},{18,2},{3,19},{19,3},{4,20},{20... | collective-permute-start | bytes 393224 | tf_op jit(solution)/shard_map/ppermute | solution.py:387
  60.1 10.3 %collective-permute-start.14 = (f32[32,1024]{1,0:T(8,128)S(1)}, f32[32,1024]{1,0:T(8,128)S(1)}, u32[]{:S(2)}, u32[]{:S(2)}) collective-permute-start(f32[32,1024]{1,0:T(8,128)S(1)} %add.125.refs_2_), channel_id=1, source_target_pairs={{0,32},{32,64},{64,96},{96,0},{1,33},{33,65},{65,97},{97,1},{2,34}... | collective-permute-start | bytes 393224 | tf_op jit(solution)/shard_map/ppermute | solution.py:391
  61.1 11.7 %collective-permute-start.13 = (f32[32,1024]{1,0:T(8,128)S(1)}, f32[32,1024]{1,0:T(8,128)S(1)}, u32[]{:S(2)}, u32[]{:S(2)}) collective-permute-start(f32[32,1024]{1,0:T(8,128)S(1)} %add.125.refs_2_), channel_id=1, source_target_pairs={{0,64},{32,96},{64,0},{96,32},{1,65},{33,97},{65,1},{97,33},{2,66}... | collective-permute-start | bytes 393224 | tf_op jit(solution)/shard_map/ppermute | solution.py:391
  62.8 11.7 %collective-permute-start.12 = (f32[32,1024]{1,0:T(8,128)S(1)}, f32[32,1024]{1,0:T(8,128)S(1)}, u32[]{:S(2)}, u32[]{:S(2)}) collective-permute-start(f32[32,1024]{1,0:T(8,128)S(1)} %add.125.refs_2_), channel_id=1, source_target_pairs={{0,96},{32,0},{64,32},{96,64},{1,97},{33,1},{65,33},{97,65},{2,98}... | collective-permute-start | bytes 393224 | tf_op jit(solution)/shard_map/ppermute | solution.py:391
  64.1 14.9 %collective-permute-start.38 = (f32[4,8,1024]{2,1,0:T(8,128)S(1)}, f32[4,8,1024]{2,1,0:T(8,128)S(1)}, u32[]{:S(2)}, u32[]{:S(2)}) collective-permute-start(f32[4,8,1024]{2,1,0:T(8,128)S(1)} %get-tuple-element.89), channel_id=1, source_target_pairs={{0,1},{1,2},{2,3},{3,4},{4,5},{5,6},{6,7},{7,8},{8,9},{9,10},{10,1... | collective-permute-start | bytes 393224 | tf_op jit(solution)/shard_map/ppermute | solution.py:410
  64.1 14.9 %collective-permute-start.37 = (f32[32,1024]{1,0:T(8,128)S(1)}, f32[32,1024]{1,0:T(8,128)S(1)}, u32[]{:S(2)}, u32[]{:S(2)}) collective-permute-start(f32[32,1024]{1,0:T(8,128)S(1)} %add.137.refs_2_), channel_id=1, source_target_pairs={{0,32},{32,64},{64,96},{96,0},{1,33},{33,65},{65,97},{97,1},{2,34}... | collective-permute-start | bytes 393224 | tf_op jit(solution)/shard_map/ppermute | solution.py:391
  70.4 11.8 %collective-permute-start.36 = (f32[32,1024]{1,0:T(8,128)S(1)}, f32[32,1024]{1,0:T(8,128)S(1)}, u32[]{:S(2)}, u32[]{:S(2)}) collective-permute-start(f32[32,1024]{1,0:T(8,128)S(1)} %add.137.refs_2_), channel_id=1, source_target_pairs={{0,64},{32,96},{64,0},{96,32},{1,65},{33,97},{65,1},{97,33},{2,66}... | collective-permute-start | bytes 393224 | tf_op jit(solution)/shard_map/ppermute | solution.py:391
  72.8 9.4 %collective-permute-start.35 = (f32[32,1024]{1,0:T(8,128)S(1)}, f32[32,1024]{1,0:T(8,128)S(1)}, u32[]{:S(2)}, u32[]{:S(2)}) collective-permute-start(f32[32,1024]{1,0:T(8,128)S(1)} %add.137.refs_2_), channel_id=1, source_target_pairs={{0,96},{32,0},{64,32},{96,64},{1,97},{33,1},{65,33},{97,65},{2,98}... | collective-permute-start | bytes 393224 | tf_op jit(solution)/shard_map/ppermute | solution.py:391
  77.6 9.9 %collective-permute-start.24 = (f32[32,1024]{1,0:T(8,128)S(1)}, f32[32,1024]{1,0:T(8,128)S(1)}, u32[]{:S(2)}, u32[]{:S(2)}) collective-permute-start(f32[32,1024]{1,0:T(8,128)S(1)} %get-tuple-element.81), channel_id=1, source_target_pairs={{0,64},{32,96},{64,0},{96,32},{1,65},{33,97},{65,1},{97,33},{2,66}... | collective-permute-start | bytes 393224 | tf_op jit(solution)/shard_map/ppermute | solution.py:381
  79.0 10.7 %collective-permute-start.25 = (f32[32,1024]{1,0:T(8,128)S(1)}, f32[32,1024]{1,0:T(8,128)S(1)}, u32[]{:S(2)}, u32[]{:S(2)}) collective-permute-start(f32[32,1024]{1,0:T(8,128)S(1)} %get-tuple-element.82), channel_id=1, source_target_pairs={{0,32},{32,64},{64,96},{96,0},{1,33},{33,65},{65,97},{97,1},{2,34}... | collective-permute-start | bytes 393224 | tf_op jit(solution)/shard_map/ppermute | solution.py:381
  79.0 10.6 %collective-permute-start.26 = (f32[32,1024]{1,0:T(8,128)S(1)}, f32[32,1024]{1,0:T(8,128)S(1)}, u32[]{:S(2)}, u32[]{:S(2)}) collective-permute-start(f32[32,1024]{1,0:T(8,128)S(1)} %get-tuple-element.83), channel_id=1, source_target_pairs={{0,96},{32,0},{64,32},{96,64},{1,97},{33,1},{65,33},{97,65},{2,98}... | collective-permute-start | bytes 393224 | tf_op jit(solution)/shard_map/ppermute | solution.py:381
  86.4 7.5 %collective-permute-start.41 = (f32[32,1024]{1,0:T(8,128)S(1)}, f32[32,1024]{1,0:T(8,128)S(1)}, u32[]{:S(2)}, u32[]{:S(2)}) collective-permute-start(f32[32,1024]{1,0:T(8,128)S(1)} %get-tuple-element.97), channel_id=1, source_target_pairs={{0,32},{32,64},{64,96},{96,0},{1,33},{33,65},{65,97},{97,1},{2,34}... | collective-permute-start | bytes 393224 | tf_op jit(solution)/shard_map/ppermute | solution.py:381
  89.7 8.9 %collective-permute-start.27 = (f32[32,1024]{1,0:T(8,128)S(1)}, f32[32,1024]{1,0:T(8,128)S(1)}, u32[]{:S(2)}, u32[]{:S(2)}) collective-permute-start(f32[32,1024]{1,0:T(8,128)S(1)} %add_add_fusion.4), channel_id=1, source_target_pairs={{0,16},{16,0},{1,17},{17,1},{2,18},{18,2},{3,19},{19,3},{4,20},{20... | collective-permute-start | bytes 393224 | tf_op jit(solution)/shard_map/ppermute | solution.py:387
  93.9 8.8 %collective-permute-start.43 = (f32[32,1024]{1,0:T(8,128)S(1)}, f32[32,1024]{1,0:T(8,128)S(1)}, u32[]{:S(2)}, u32[]{:S(2)}) collective-permute-start(f32[32,1024]{1,0:T(8,128)S(1)} %add_add_fusion.2), channel_id=1, source_target_pairs={{0,16},{16,0},{1,17},{17,1},{2,18},{18,2},{3,19},{19,3},{4,20},{20... | collective-permute-start | bytes 393224 | tf_op jit(solution)/shard_map/ppermute | solution.py:387
  98.6 8.9 %collective-permute-start.30 = (f32[32,1024]{1,0:T(8,128)S(1)}, f32[32,1024]{1,0:T(8,128)S(1)}, u32[]{:S(2)}, u32[]{:S(2)}) collective-permute-start(f32[32,1024]{1,0:T(8,128)S(1)} %add.133.refs_2_), channel_id=1, source_target_pairs={{0,32},{32,64},{64,96},{96,0},{1,33},{33,65},{65,97},{97,1},{2,34}... | collective-permute-start | bytes 393224 | tf_op jit(solution)/shard_map/ppermute | solution.py:391
  98.7 8.8 %collective-permute-start.29 = (f32[32,1024]{1,0:T(8,128)S(1)}, f32[32,1024]{1,0:T(8,128)S(1)}, u32[]{:S(2)}, u32[]{:S(2)}) collective-permute-start(f32[32,1024]{1,0:T(8,128)S(1)} %add.133.refs_2_), channel_id=1, source_target_pairs={{0,64},{32,96},{64,0},{96,32},{1,65},{33,97},{65,1},{97,33},{2,66}... | collective-permute-start | bytes 393224 | tf_op jit(solution)/shard_map/ppermute | solution.py:391
  101.3 7.5 %collective-permute-start.28 = (f32[32,1024]{1,0:T(8,128)S(1)}, f32[32,1024]{1,0:T(8,128)S(1)}, u32[]{:S(2)}, u32[]{:S(2)}) collective-permute-start(f32[32,1024]{1,0:T(8,128)S(1)} %add.133.refs_2_), channel_id=1, source_target_pairs={{0,96},{32,0},{64,32},{96,64},{1,97},{33,1},{65,33},{97,65},{2,98}... | collective-permute-start | bytes 393224 | tf_op jit(solution)/shard_map/ppermute | solution.py:391
  102.7 12.1 %collective-permute-start.47 = (f32[4,8,1024]{2,1,0:T(8,128)S(1)}, f32[4,8,1024]{2,1,0:T(8,128)S(1)}, u32[]{:S(2)}, u32[]{:S(2)}) collective-permute-start(f32[4,8,1024]{2,1,0:T(8,128)S(1)} %get-tuple-element.99), channel_id=1, source_target_pairs={{0,1},{1,2},{2,3},{3,4},{4,5},{5,6},{6,7},{7,8},{8,9},{9,10},{10,1... | collective-permute-start | bytes 393224 | tf_op jit(solution)/shard_map/ppermute | solution.py:410
  102.7 13.4 %collective-permute-start.46 = (f32[32,1024]{1,0:T(8,128)S(1)}, f32[32,1024]{1,0:T(8,128)S(1)}, u32[]{:S(2)}, u32[]{:S(2)}) collective-permute-start(f32[32,1024]{1,0:T(8,128)S(1)} %add.141.refs_2_), channel_id=1, source_target_pairs={{0,32},{32,64},{64,96},{96,0},{1,33},{33,65},{65,97},{97,1},{2,34}... | collective-permute-start | bytes 393224 | tf_op jit(solution)/shard_map/ppermute | solution.py:391
  107.5 10.5 %collective-permute-start.45 = (f32[32,1024]{1,0:T(8,128)S(1)}, f32[32,1024]{1,0:T(8,128)S(1)}, u32[]{:S(2)}, u32[]{:S(2)}) collective-permute-start(f32[32,1024]{1,0:T(8,128)S(1)} %add.141.refs_2_), channel_id=1, source_target_pairs={{0,64},{32,96},{64,0},{96,32},{1,65},{33,97},{65,1},{97,33},{2,66}... | collective-permute-start | bytes 393224 | tf_op jit(solution)/shard_map/ppermute | solution.py:391
  107.5 10.5 %collective-permute-start.44 = (f32[32,1024]{1,0:T(8,128)S(1)}, f32[32,1024]{1,0:T(8,128)S(1)}, u32[]{:S(2)}, u32[]{:S(2)}) collective-permute-start(f32[32,1024]{1,0:T(8,128)S(1)} %add.141.refs_2_), channel_id=1, source_target_pairs={{0,96},{32,0},{64,32},{96,64},{1,97},{33,1},{65,33},{97,65},{2,98}... | collective-permute-start | bytes 393224 | tf_op jit(solution)/shard_map/ppermute | solution.py:391
  112.5 10.1 %collective-permute-start.52 = (f32[32,1024]{1,0:T(8,128)S(1)}, f32[32,1024]{1,0:T(8,128)S(1)}, u32[]{:S(2)}, u32[]{:S(2)}) collective-permute-start(f32[32,1024]{1,0:T(8,128)S(1)} %get-tuple-element.106), channel_id=1, source_target_pairs={{0,64},{32,96},{64,0},{96,32},{1,65},{33,97},{65,1},{97,33},{2,66}... | collective-permute-start | bytes 393224 | tf_op jit(solution)/shard_map/ppermute | solution.py:381
  114.7 10.5 %collective-permute-start.53 = (f32[32,1024]{1,0:T(8,128)S(1)}, f32[32,1024]{1,0:T(8,128)S(1)}, u32[]{:S(2)}, u32[]{:S(2)}) collective-permute-start(f32[32,1024]{1,0:T(8,128)S(1)} %get-tuple-element.107), channel_id=1, source_target_pairs={{0,32},{32,64},{64,96},{96,0},{1,33},{33,65},{65,97},{97,1},{2,34}... | collective-permute-start | bytes 393224 | tf_op jit(solution)/shard_map/ppermute | solution.py:381
  116.1 9.1 %collective-permute-start.54 = (f32[32,1024]{1,0:T(8,128)S(1)}, f32[32,1024]{1,0:T(8,128)S(1)}, u32[]{:S(2)}, u32[]{:S(2)}) collective-permute-start(f32[32,1024]{1,0:T(8,128)S(1)} %get-tuple-element.108), channel_id=1, source_target_pairs={{0,96},{32,0},{64,32},{96,64},{1,97},{33,1},{65,33},{97,65},{2,98}... | collective-permute-start | bytes 393224 | tf_op jit(solution)/shard_map/ppermute | solution.py:381
  122.0 7.6 %collective-permute-start.49 = (f32[32,1024]{1,0:T(8,128)S(1)}, f32[32,1024]{1,0:T(8,128)S(1)}, u32[]{:S(2)}, u32[]{:S(2)}) collective-permute-start(f32[32,1024]{1,0:T(8,128)S(1)} %get-tuple-element.103), channel_id=1, source_target_pairs={{0,32},{32,64},{64,96},{96,0},{1,33},{33,65},{65,97},{97,1},{2,34}... | collective-permute-start | bytes 393224 | tf_op jit(solution)/shard_map/ppermute | solution.py:381
  162.6 8.0 %collective-permute-start.56 = (f32[32,1024]{1,0:T(8,128)S(1)}, f32[32,1024]{1,0:T(8,128)S(1)}, u32[]{:S(2)}, u32[]{:S(2)}) collective-permute-start(f32[32,1024]{1,0:T(8,128)S(1)} %get-tuple-element.109), channel_id=1, source_target_pairs={{0,16},{16,0},{1,17},{17,1},{2,18},{18,2},{3,19},{19,3},{4,20},{20... | collective-permute-start | bytes 393224 | tf_op jit(solution)/shard_map/ppermute | solution.py:387
  166.9 8.4 %collective-permute-start.63 = (f32[32,1024]{1,0:T(8,128)S(1)}, f32[32,1024]{1,0:T(8,128)S(1)}, u32[]{:S(2)}, u32[]{:S(2)}) collective-permute-start(f32[32,1024]{1,0:T(8,128)S(1)} %add.151.p0), channel_id=1, source_target_pairs={{0,32},{32,64},{64,96},{96,0},{1,33},{33,65},{65,97},{97,1},{2,34}... | collective-permute-start | bytes 393224 | tf_op jit(solution)/shard_map/ppermute | solution.py:391
  167.0 10.6 %collective-permute-start.62 = (f32[32,1024]{1,0:T(8,128)S(1)}, f32[32,1024]{1,0:T(8,128)S(1)}, u32[]{:S(2)}, u32[]{:S(2)}) collective-permute-start(f32[32,1024]{1,0:T(8,128)S(1)} %add.151.p0), channel_id=1, source_target_pairs={{0,64},{32,96},{64,0},{96,32},{1,65},{33,97},{65,1},{97,33},{2,66}... | collective-permute-start | bytes 393224 | tf_op jit(solution)/shard_map/ppermute | solution.py:391
  170.6 7.7 %collective-permute-start.61 = (f32[32,1024]{1,0:T(8,128)S(1)}, f32[32,1024]{1,0:T(8,128)S(1)}, u32[]{:S(2)}, u32[]{:S(2)}) collective-permute-start(f32[32,1024]{1,0:T(8,128)S(1)} %add.151.p0), channel_id=1, source_target_pairs={{0,96},{32,0},{64,32},{96,64},{1,97},{33,1},{65,33},{97,65},{2,98}... | collective-permute-start | bytes 393224 | tf_op jit(solution)/shard_map/ppermute | solution.py:391
  170.6 10.5 %collective-permute-start.59 = (f32[32,1024]{1,0:T(8,128)S(1)}, f32[32,1024]{1,0:T(8,128)S(1)}, u32[]{:S(2)}, u32[]{:S(2)}) collective-permute-start(f32[32,1024]{1,0:T(8,128)S(1)} %add.150.p0), channel_id=1, source_target_pairs={{0,32},{32,64},{64,96},{96,0},{1,33},{33,65},{65,97},{97,1},{2,34}... | collective-permute-start | bytes 393224 | tf_op jit(solution)/shard_map/ppermute | solution.py:391
  172.7 8.4 %collective-permute-start.58 = (f32[32,1024]{1,0:T(8,128)S(1)}, f32[32,1024]{1,0:T(8,128)S(1)}, u32[]{:S(2)}, u32[]{:S(2)}) collective-permute-start(f32[32,1024]{1,0:T(8,128)S(1)} %add.150.p0), channel_id=1, source_target_pairs={{0,64},{32,96},{64,0},{96,32},{1,65},{33,97},{65,1},{97,33},{2,66}... | collective-permute-start | bytes 393224 | tf_op jit(solution)/shard_map/ppermute | solution.py:391
  (24 other events, 319.5 us)

commit v3 on v2

--- a/solution.py
+++ b/solution.py
@@ -179,7 +179,13 @@
     freq = jnp.where(s == 16, N // 2, meta[2] + (s >> 3) + 8 * (s & 7))
     freq = jnp.where(q >= 32, (N - freq) & (N - 1), freq)
     hit = (lax.broadcasted_iota(jnp.int32, (128, N), 1) == freq) & (s < 17) & (q < 64)
-    cols[...] = nt(green[...], jnp.where(hit, 0.5, 0.0).astype(F32))
+    pick = jnp.where(hit, 0.5, 0.0).astype(jnp.bfloat16)
+    rest, parts = green[...], []
+    for _ in range(3):
+        parts.append(rest.astype(jnp.bfloat16))
+        rest = rest - parts[-1].astype(F32)
+    dims = (((1,), (1,)), ((), ()))
+    cols[...] = sum(lax.dot_general(p, pick, dims, preferred_element_type=F32) for p in parts)
     line = lax.broadcasted_iota(jnp.int32, (64, 128), 0)
     place = lax.broadcasted_iota(jnp.int32, (64, 128), 1) & 63
 
@@ -299,7 +305,7 @@
     out = pl.pallas_call(
         functools.partial(square_kernel, c), out_shape=outs, in_specs=[SMEM_SPEC, HBM_SPEC],
         out_specs=(VMEM_SPEC,) * 7, scratch_shapes=[pltpu.SemaphoreType.DMA((PLANES,))], name=f"squares{c}", compiler_params=limit(2),
-    )(meta, order)
+    )(meta, pltpu.with_memory_space_constraint(order, pltpu.HBM))
     return out[0], out[1:5], out[5], out[6]
 
 

time: 186 us -> 183 us (0.984)
  local copies, waits for them, and re-layouts: 3.43 us -> 0.04 us
  starting transfers between devices: 95.7 us -> 93.1 us
    unnamed x16 -> x14, local copies, waits for them, and re-layouts: 3.43 us -> 0.04 us
    pallas_call x2, Pallas kernels: 2.4 us -> 5.67 us  [squares(): pl.pallas_call(functools.partial(square_kernel, c), out_shape=outs, in_sp...]
    ppermute x10, starting transfers between devices: 24.5 us -> 21.3 us  [with_partner(): return x + lax.ppermute(x, 'xh', [(0, 1), (1, 0)])]
    ppermute x24, waiting for transfers between devices: 6.35 us -> 9.09 us  [to_owner(): lax.ppermute(sums[k], 'z', shift(k))]
  transfers between devices with their start and end apart: 64 -> 64, of which waited for: 18 -> 16; matrix products, arithmetic and copies ran while one was open for 0% -> 0% of each run, Pallas kernels for 16% -> 16%
where the time goes in v3:
time: 183 us; the launch traced here: 182 us
  starting transfers between devices  93.1 us (51%)
  Pallas kernels  38.4 us (21%)
  waiting for transfers between devices  28.9 us (16%)
  blocking collectives  20.3 us (11%)
    ppermute x24, starting transfers between devices, to_owner(): lax.ppermute(sums[k], 'z', shift(k))  37.9 us
    ppermute x24, starting transfers between devices, to_all(): parts = {k: lax.ppermute(x, 'z', shift(-k)) for k in (2, 1, 3)}  29.3 us
    ppermute x10, starting transfers between devices, with_partner(): return x + lax.ppermute(x, 'xh', [(0, 1), (1, 0)])  21.3 us
    pallas_call x6, Pallas kernels, advance(): pl.pallas_call(functools.partial(step_kernel, last, len(ready)), out_shap...  19.2 us
    ppermute x24, waiting for transfers between devices, to_all(): parts = {k: lax.ppermute(x, 'z', shift(-k)) for k in (2, 1, 3)}  12 us
    all_to_all x1, blocking collectives, local(): spectrum = lax.all_to_all(spectrum, ROW_AXES, 0, 0, tiled=True)  11 us
    all_to_all x1, blocking collectives, local(): mixed = lax.all_to_all(mixed, ROW_AXES, 0, 0, tiled=True)  9.29 us
    ppermute x24, waiting for transfers between devices, to_owner(): lax.ppermute(sums[k], 'z', shift(k))  9.09 us
  transfers between devices with their start and end apart: 64, of which 16 were waited for; matrix products, arithmetic and copies ran while one was open for 0% of the time, Pallas kernels for 16%

profile of v3, /device:TPU:0, one launch (start us, length us, event | category | flops | bytes accessed | tf_op | source)
XLA Modules:
  0.0 182.5 jit_solution(7189272884375810416)
XLA Ops:
  0.7 2.8 %squares1.1 = (f32[4,8,32,1024]{3,2,1,0:T(8,128)S(1)}, f32[32,1024]{1,0:T(8,128)S(1)}, f32[32,1024]{1,0:T(8,128)S(1)}, f32[32,1024]{1,0:T(8,128)S(1)}, f32[32,10...) custom-call(s32[3]{0:T(128)S(1)} %pad_add_fusion.meta, f32[8,4,64,1024]{3,2,1,0:T(8,128)} %order.3), custom_call_target="tpu_custom_call" | custom-call | tf_op jit(solution)/shard_map/squares1/pallas_call | solution.py:305
  3.6 4.1 %collective-permute-start = (f32[32,1024]{1,0:T(8,128)S(1)}, f32[32,1024]{1,0:T(8,128)S(1)}, u32[]{:S(2)}, u32[]{:S(2)}) collective-permute-start(f32[32,1024]{1,0:T(8,128)S(1)} %get-tuple-element.60), channel_id=1, source_target_pairs={{0,64},{32,96},{64,0},{96,32},{1,65},{33,97},{65,1},{97,33},{2,66}... | collective-permute-start | bytes 393224 | tf_op jit(solution)/shard_map/ppermute | solution.py:387
  8.6 2.2 %collective-permute-start.2 = (f32[32,1024]{1,0:T(8,128)S(1)}, f32[32,1024]{1,0:T(8,128)S(1)}, u32[]{:S(2)}, u32[]{:S(2)}) collective-permute-start(f32[32,1024]{1,0:T(8,128)S(1)} %get-tuple-element.62), channel_id=1, source_target_pairs={{0,96},{32,0},{64,32},{96,64},{1,97},{33,1},{65,33},{97,65},{2,98}... | collective-permute-start | bytes 393224 | tf_op jit(solution)/shard_map/ppermute | solution.py:387
  10.9 2.8 %squares0.1 = (f32[4,8,32,1024]{3,2,1,0:T(8,128)S(1)}, f32[32,1024]{1,0:T(8,128)S(1)}, f32[32,1024]{1,0:T(8,128)S(1)}, f32[32,1024]{1,0:T(8,128)S(1)}, f32[32,10...) custom-call(s32[3]{0:T(128)S(1)} %pad_add_fusion.meta, f32[8,4,64,1024]{3,2,1,0:T(8,128)} %order.3), custom_call_target="tpu_custom_call" | custom-call | tf_op jit(solution)/shard_map/squares0/pallas_call | solution.py:305
  14.7 2.5 %collective-permute-start.17 = (f32[32,1024]{1,0:T(8,128)S(1)}, f32[32,1024]{1,0:T(8,128)S(1)}, u32[]{:S(2)}, u32[]{:S(2)}) collective-permute-start(f32[32,1024]{1,0:T(8,128)S(1)} %get-tuple-element.74), channel_id=1, source_target_pairs={{0,96},{32,0},{64,32},{96,64},{1,97},{33,1},{65,33},{97,65},{2,98}... | collective-permute-start | bytes 393224 | tf_op jit(solution)/shard_map/ppermute | solution.py:387
  17.2 3.1 %collective-permute-start.3 = (f32[32,1024]{1,0:T(8,128)S(1)}, f32[32,1024]{1,0:T(8,128)S(1)}, u32[]{:S(2)}, u32[]{:S(2)}) collective-permute-start(f32[32,1024]{1,0:T(8,128)S(1)} %add_add_fusion.7), channel_id=1, source_target_pairs={{0,16},{16,0},{1,17},{17,1},{2,18},{18,2},{3,19},{19,3},{4,20},{20... | collective-permute-start | bytes 393224 | tf_op jit(solution)/shard_map/ppermute | solution.py:393
  22.3 3.1 %collective-permute-start.18 = (f32[32,1024]{1,0:T(8,128)S(1)}, f32[32,1024]{1,0:T(8,128)S(1)}, u32[]{:S(2)}, u32[]{:S(2)}) collective-permute-start(f32[32,1024]{1,0:T(8,128)S(1)} %add_add_fusion.5), channel_id=1, source_target_pairs={{0,16},{16,0},{1,17},{17,1},{2,18},{18,2},{3,19},{19,3},{4,20},{20... | collective-permute-start | bytes 393224 | tf_op jit(solution)/shard_map/ppermute | solution.py:393
  25.4 1.9 %collective-permute-start.7 = (f32[4,8,1024]{2,1,0:T(8,128)S(1)}, f32[4,8,1024]{2,1,0:T(8,128)S(1)}, u32[]{:S(2)}, u32[]{:S(2)}) collective-permute-start(f32[4,8,1024]{2,1,0:T(8,128)S(1)} %get-tuple-element.64), channel_id=1, source_target_pairs={{1,0},{2,1},{3,2},{4,3},{5,4},{6,5},{7,6},{8,7},{9,8},{10,9},{11,1... | collective-permute-start | bytes 393224 | tf_op jit(solution)/shard_map/ppermute | solution.py:417
  28.7 1.9 %collective-permute-start.4 = (f32[32,1024]{1,0:T(8,128)S(1)}, f32[32,1024]{1,0:T(8,128)S(1)}, u32[]{:S(2)}, u32[]{:S(2)}) collective-permute-start(f32[32,1024]{1,0:T(8,128)S(1)} %add.121.refs_1_), channel_id=1, source_target_pairs={{0,96},{32,0},{64,32},{96,64},{1,97},{33,1},{65,33},{97,65},{2,98}... | collective-permute-start | bytes 393224 | tf_op jit(solution)/shard_map/ppermute | solution.py:397
  31.6 4.6 %collective-permute-done.6.refs_4_ = f32[32,1024]{1,0:T(8,128)S(1)} collective-permute-done((f32[32,1024]{1,0:T(8,128)S(1)}, f32[32,1024]{1,0:T(8,128)S(1)}, u32[]{:S(2)}, u32[]{:S(2)}) %collective-permute-start.6) | collective-permute-done | bytes 131104 | tf_op jit(solution)/shard_map/ppermute | solution.py:397
  37.5 3.0 %step0_1.1 = (f32[4,8,32,1024]{3,2,1,0:T(8,128)S(1)}, f32[32,1024]{1,0:T(8,128)S(1)}, f32[32,1024]{1,0:T(8,128)S(1)}, f32[32,1024]{1,0:T(8,128)S(1)}, f32[32,102...) custom-call(f32[4,8,32,1024]{3,2,1,0:T(8,128)S(1)} %get-tuple-element.58.refs_0_, ...), custom_call_target="tpu_custom_call" | custom-call | tf_op jit(solution)/shard_map/step0_1/pallas_call | solution.py:316
  40.5 2.4 %collective-permute-start.8 = (f32[32,1024]{1,0:T(8,128)S(1)}, f32[32,1024]{1,0:T(8,128)S(1)}, u32[]{:S(2)}, u32[]{:S(2)}) collective-permute-start(f32[32,1024]{1,0:T(8,128)S(1)} %get-tuple-element.67), channel_id=1, source_target_pairs={{0,64},{32,96},{64,0},{96,32},{1,65},{33,97},{65,1},{97,33},{2,66}... | collective-permute-start | bytes 393224 | tf_op jit(solution)/shard_map/ppermute | solution.py:387
  44.3 1.8 collective-permute-start.10
  46.1 3.0 %step0_0.1 = (f32[4,8,32,1024]{3,2,1,0:T(8,128)S(1)}, f32[32,1024]{1,0:T(8,128)S(1)}, f32[32,1024]{1,0:T(8,128)S(1)}, f32[32,1024]{1,0:T(8,128)S(1)}, f32[32,102...) custom-call(f32[4,8,32,1024]{3,2,1,0:T(8,128)S(1)} %get-tuple-element.70.refs_0_, ...), custom_call_target="tpu_custom_call" | custom-call | tf_op jit(solution)/shard_map/step0_0/pallas_call | solution.py:316
  50.1 2.7 %collective-permute-start.33 = (f32[32,1024]{1,0:T(8,128)S(1)}, f32[32,1024]{1,0:T(8,128)S(1)}, u32[]{:S(2)}, u32[]{:S(2)}) collective-permute-start(f32[32,1024]{1,0:T(8,128)S(1)} %get-tuple-element.88), channel_id=1, source_target_pairs={{0,96},{32,0},{64,32},{96,64},{1,97},{33,1},{65,33},{97,65},{2,98}... | collective-permute-start | bytes 393224 | tf_op jit(solution)/shard_map/ppermute | solution.py:387
  52.8 1.6 collective-permute-start.11
  58.0 1.6 collective-permute-start.23
  59.7 3.3 %collective-permute-start.13 = (f32[32,1024]{1,0:T(8,128)S(1)}, f32[32,1024]{1,0:T(8,128)S(1)}, u32[]{:S(2)}, u32[]{:S(2)}) collective-permute-start(f32[32,1024]{1,0:T(8,128)S(1)} %add.125.refs_2_), channel_id=1, source_target_pairs={{0,64},{32,96},{64,0},{96,32},{1,65},{33,97},{65,1},{97,33},{2,66}... | collective-permute-start | bytes 393224 | tf_op jit(solution)/shard_map/ppermute | solution.py:397
  65.1 3.8 %own_green.1.refs_0_.green = f32[16,24,128]{2,1,0:T(8,128)S(1)} custom-call(s32[3]{0:T(128)S(1)} %pad_add_fusion.meta, f32[1024,1024]{1,0:T(8,128)S(1)} %copy-done), custom_call_target="tpu_custom_call" | custom-call | tf_op jit(solution)/shard_map/own_green/pallas_call | solution.py:360
  68.9 2.0 %collective-permute-start.36 = (f32[32,1024]{1,0:T(8,128)S(1)}, f32[32,1024]{1,0:T(8,128)S(1)}, u32[]{:S(2)}, u32[]{:S(2)}) collective-permute-start(f32[32,1024]{1,0:T(8,128)S(1)} %add.137.refs_2_), channel_id=1, source_target_pairs={{0,64},{32,96},{64,0},{96,32},{1,65},{33,97},{65,1},{97,33},{2,66}... | collective-permute-start | bytes 393224 | tf_op jit(solution)/shard_map/ppermute | solution.py:397
  72.5 3.0 %step1_1.1 = (f32[4,8,32,1024]{3,2,1,0:T(8,128)S(1)}, f32[32,1024]{1,0:T(8,128)S(1)}, f32[32,1024]{1,0:T(8,128)S(1)}, f32[32,1024]{1,0:T(8,128)S(1)}, f32[32,102...) custom-call(f32[16,24,128]{2,1,0:T(8,128)S(1)} %own_green.1.refs_0_.green, ...), custom_call_target="tpu_custom_call" | custom-call | tf_op jit(solution)/shard_map/step1_1/pallas_call | solution.py:316
  75.5 1.8 collective-permute-start.24
  77.3 3.2 %collective-permute-start.26 = (f32[32,1024]{1,0:T(8,128)S(1)}, f32[32,1024]{1,0:T(8,128)S(1)}, u32[]{:S(2)}, u32[]{:S(2)}) collective-permute-start(f32[32,1024]{1,0:T(8,128)S(1)} %get-tuple-element.83), channel_id=1, source_target_pairs={{0,96},{32,0},{64,32},{96,64},{1,97},{33,1},{65,33},{97,65},{2,98}... | collective-permute-start | bytes 393224 | tf_op jit(solution)/shard_map/ppermute | solution.py:387
  80.6 3.0 %step1_0.1 = (f32[4,8,32,1024]{3,2,1,0:T(8,128)S(1)}, f32[32,1024]{1,0:T(8,128)S(1)}, f32[32,1024]{1,0:T(8,128)S(1)}, f32[32,1024]{1,0:T(8,128)S(1)}, f32[32,102...) custom-call(f32[16,24,128]{2,1,0:T(8,128)S(1)} %own_green.1.refs_0_.green, ...), custom_call_target="tpu_custom_call" | custom-call | tf_op jit(solution)/shard_map/step1_0/pallas_call | solution.py:316
  84.3 1.6 collective-permute-start.41
  85.9 1.7 collective-permute-start.42
  88.8 2.1 %collective-permute-done.40 = f32[32,1024]{1,0:T(8,128)S(1)} collective-permute-done((f32[32,1024]{1,0:T(8,128)S(1)}, f32[32,1024]{1,0:T(8,128)S(1)}, u32[]{:S(2)}, u32[]{:S(2)}) %collective-permute-start.40) | collective-permute-done | bytes 131104 | tf_op jit(solution)/shard_map/ppermute | solution.py:387
  92.2 2.6 %collective-permute-start.43 = (f32[32,1024]{1,0:T(8,128)S(1)}, f32[32,1024]{1,0:T(8,128)S(1)}, u32[]{:S(2)}, u32[]{:S(2)}) collective-permute-start(f32[32,1024]{1,0:T(8,128)S(1)} %add_add_fusion.2), channel_id=1, source_target_pairs={{0,16},{16,0},{1,17},{17,1},{2,18},{18,2},{3,19},{19,3},{4,20},{20... | collective-permute-start | bytes 393224 | tf_op jit(solution)/shard_map/ppermute | solution.py:393
  95.9 3.3 %collective-permute-start.29 = (f32[32,1024]{1,0:T(8,128)S(1)}, f32[32,1024]{1,0:T(8,128)S(1)}, u32[]{:S(2)}, u32[]{:S(2)}) collective-permute-start(f32[32,1024]{1,0:T(8,128)S(1)} %add.133.refs_2_), channel_id=1, source_target_pairs={{0,64},{32,96},{64,0},{96,32},{1,65},{33,97},{65,1},{97,33},{2,66}... | collective-permute-start | bytes 393224 | tf_op jit(solution)/shard_map/ppermute | solution.py:397
  99.3 2.1 %collective-permute-start.46 = (f32[32,1024]{1,0:T(8,128)S(1)}, f32[32,1024]{1,0:T(8,128)S(1)}, u32[]{:S(2)}, u32[]{:S(2)}) collective-permute-start(f32[32,1024]{1,0:T(8,128)S(1)} %add.141.refs_2_), channel_id=1, source_target_pairs={{0,32},{32,64},{64,96},{96,0},{1,33},{33,65},{65,97},{97,1},{2,34}... | collective-permute-start | bytes 393224 | tf_op jit(solution)/shard_map/ppermute | solution.py:397
  101.4 3.4 %collective-permute-done.30.refs_5_ = f32[32,1024]{1,0:T(8,128)S(1)} collective-permute-done((f32[32,1024]{1,0:T(8,128)S(1)}, f32[32,1024]{1,0:T(8,128)S(1)}, u32[]{:S(2)}, u32[]{:S(2)}) %collective-permute-start.30) | collective-permute-done | bytes 131104 | tf_op jit(solution)/shard_map/ppermute | solution.py:397
  104.8 1.9 %collective-permute-start.44 = (f32[32,1024]{1,0:T(8,128)S(1)}, f32[32,1024]{1,0:T(8,128)S(1)}, u32[]{:S(2)}, u32[]{:S(2)}) collective-permute-start(f32[32,1024]{1,0:T(8,128)S(1)} %add.141.refs_2_), channel_id=1, source_target_pairs={{0,96},{32,0},{64,32},{96,64},{1,97},{33,1},{65,33},{97,65},{2,98}... | collective-permute-start | bytes 393224 | tf_op jit(solution)/shard_map/ppermute | solution.py:397
  106.7 3.6 %step2_1.1 = (f32[4,8,32,1024]{3,2,1,0:T(8,128)S(1)}, f32[32,1024]{1,0:T(8,128)S(1)}, f32[32,1024]{1,0:T(8,128)S(1)}, f32[32,1024]{1,0:T(8,128)S(1)}, f32[32,1024]{1,0:T(8,128)S(1)}) custom-call(f32[8]{0:T(128)S(1)} %copy-done.6, f32[4,8,32,1024]{3,2,1,0:T(8,128)S(1)} %get-tuple-element.79.refs_1_, f32[32,1024]{1,0:T(8,128)S(1)} %add.133.refs_2_, ...), custom_call_target="tpu_custom_call" | custom-call | tf_op jit(solution)/shard_map/step2_1/pallas_call | solution.py:316
  110.3 1.7 collective-permute-start.52
  113.4 1.8 %collective-permute-start.54 = (f32[32,1024]{1,0:T(8,128)S(1)}, f32[32,1024]{1,0:T(8,128)S(1)}, u32[]{:S(2)}, u32[]{:S(2)}) collective-permute-start(f32[32,1024]{1,0:T(8,128)S(1)} %get-tuple-element.108), channel_id=1, source_target_pairs={{0,96},{32,0},{64,32},{96,64},{1,97},{33,1},{65,33},{97,65},{2,98}... | collective-permute-start | bytes 393224 | tf_op jit(solution)/shard_map/ppermute | solution.py:387
  115.3 3.6 %step2_0.1 = (f32[4,8,32,1024]{3,2,1,0:T(8,128)S(1)}, f32[32,1024]{1,0:T(8,128)S(1)}, f32[32,1024]{1,0:T(8,128)S(1)}, f32[32,1024]{1,0:T(8,128)S(1)}, f32[32,1024]{1,0:T(8,128)S(1)}) custom-call(f32[8]{0:T(128)S(1)} %copy-done.6, f32[4,8,32,1024]{3,2,1,0:T(8,128)S(1)} %get-tuple-element.94.refs_1_, f32[32,1024]{1,0:T(8,128)S(1)} %add.141.refs_2_, ...), custom_call_target="tpu_custom_call" | custom-call | tf_op jit(solution)/shard_map/step2_0/pallas_call | solution.py:316
  119.8 3.0 %collective-permute-start.50 = (f32[32,1024]{1,0:T(8,128)S(1)}, f32[32,1024]{1,0:T(8,128)S(1)}, u32[]{:S(2)}, u32[]{:S(2)}) collective-permute-start(f32[32,1024]{1,0:T(8,128)S(1)} %get-tuple-element.104), channel_id=1, source_target_pairs={{0,96},{32,0},{64,32},{96,64},{1,97},{33,1},{65,33},{97,65},{2,98}... | collective-permute-start | bytes 393224 | tf_op jit(solution)/shard_map/ppermute | solution.py:387
  122.9 2.9 %collective-permute-start.55 = (f32[32,1024]{1,0:T(8,128)S(1)}, f32[32,1024]{1,0:T(8,128)S(1)}, u32[]{:S(2)}, u32[]{:S(2)}) collective-permute-start(f32[32,1024]{1,0:T(8,128)S(1)} %add_add_fusion), channel_id=1, source_target_pairs={{0,16},{16,0},{1,17},{17,1},{2,18},{18,2},{3,19},{19,3},{4,20},{20... | collective-permute-start | bytes 393224 | tf_op jit(solution)/shard_map/ppermute | solution.py:393
  126.9 2.3 %collective-permute-start.51 = (f32[32,1024]{1,0:T(8,128)S(1)}, f32[32,1024]{1,0:T(8,128)S(1)}, u32[]{:S(2)}, u32[]{:S(2)}) collective-permute-start(f32[32,1024]{1,0:T(8,128)S(1)} %add_add_fusion.1), channel_id=1, source_target_pairs={{0,16},{16,0},{1,17},{17,1},{2,18},{18,2},{3,19},{19,3},{4,20},{20... | collective-permute-start | bytes 393224 | tf_op jit(solution)/shard_map/ppermute | solution.py:393
  130.6 2.9 %collective-permute-done.51 = f32[32,1024]{1,0:T(8,128)S(1)} collective-permute-done((f32[32,1024]{1,0:T(8,128)S(1)}, f32[32,1024]{1,0:T(8,128)S(1)}, u32[]{:S(2)}, u32[]{:S(2)}) %collective-permute-start.51) | collective-permute-done | bytes 131104 | tf_op jit(solution)/shard_map/ppermute | solution.py:393
  134.7 11.0 %all_to_all.10.recv = f32[16,16,128]{2,1,0:T(8,128)S(1)} all-to-all(f32[16,16,128]{2,1,0:T(8,128)S(1)} %row_forward.1), channel_id=1, replica_groups=mesh['z'=4,'xh'=2,'y'=4,'xl'=2,'c'=2] {'y','xl','c'}, dimensions={0} | all-to-all | bytes 262144 | tf_op jit(solution)/shard_map/all_to_all | solution.py:427
  147.3 9.3 %all_to_all.11.recv = f32[16,16,128]{2,1,0:T(8,128)S(1)} all-to-all(f32[16,16,128]{2,1,0:T(8,128)S(1)} %column.1), channel_id=1, replica_groups=mesh['z'=4,'xh'=2,'y'=4,'xl'=2,'c'=2] {'y','xl','c'}, dimensions={0} | all-to-all | bytes 262144 | tf_op jit(solution)/shard_map/all_to_all | solution.py:429
  157.9 3.3 %collective-permute-start.60 = (f32[32,1024]{1,0:T(8,128)S(1)}, f32[32,1024]{1,0:T(8,128)S(1)}, u32[]{:S(2)}, u32[]{:S(2)}) collective-permute-start(f32[32,1024]{1,0:T(8,128)S(1)} %get-tuple-element.111), channel_id=1, source_target_pairs={{0,16},{16,0},{1,17},{17,1},{2,18},{18,2},{3,19},{19,3},{4,20},{20... | collective-permute-start | bytes 393224 | tf_op jit(solution)/shard_map/ppermute | solution.py:393
  161.5 3.5 %collective-permute-done.60 = f32[32,1024]{1,0:T(8,128)S(1)} collective-permute-done((f32[32,1024]{1,0:T(8,128)S(1)}, f32[32,1024]{1,0:T(8,128)S(1)}, u32[]{:S(2)}, u32[]{:S(2)}) %collective-permute-start.60) | collective-permute-done | bytes 131104 | tf_op jit(solution)/shard_map/ppermute | solution.py:393
  165.7 2.7 %collective-permute-start.62 = (f32[32,1024]{1,0:T(8,128)S(1)}, f32[32,1024]{1,0:T(8,128)S(1)}, u32[]{:S(2)}, u32[]{:S(2)}) collective-permute-start(f32[32,1024]{1,0:T(8,128)S(1)} %add.151.p0), channel_id=1, source_target_pairs={{0,64},{32,96},{64,0},{96,32},{1,65},{33,97},{65,1},{97,33},{2,66}... | collective-permute-start | bytes 393224 | tf_op jit(solution)/shard_map/ppermute | solution.py:397
  174.0 1.7 collective-permute-done.62.p2
  176.1 2.9 %final0.1 = (f32[8,4,64,1024]{3,2,1,0:T(8,128)}, f32[4,64,1024]{2,1,0:T(8,128)}) custom-call(s32[3]{0:T(128)S(1)} %pad_add_fusion.meta, f32[8]{0:T(128)S(1)} %copy-done.6, f32[4,8,32,1024]{3,2,1,0:T(8,128)S(1)} %get-tuple-element.110.eta, f32[32,1024]{1,0:T(8,128)S(1)} %add.151.p0, f32[32,1024]{1,0:T(8,128)S(1)} %collective-permute-done.61.p1, ...), custom_call_target="tpu_custom_call" | custom-call | tf_op jit(solution)/shard_map/final0/pallas_call | solution.py:326
  179.4 2.9 %final1.1 = (f32[8,4,64,1024]{3,2,1,0:T(8,128)}, f32[4,64,1024]{2,1,0:T(8,128)}) custom-call(s32[3]{0:T(128)S(1)} %pad_add_fusion.meta, f32[8]{0:T(128)S(1)} %copy-done.6, f32[4,8,32,1024]{3,2,1,0:T(8,128)S(1)} %get-tuple-element.93.eta, f32[32,1024]{1,0:T(8,128)S(1)} %add.150.p0, ...), custom_call_target="tpu_custom_call", output_to_operand_aliasing={{0}: (7, {}), {1}: (8, {})} | custom-call | tf_op jit(solution)/shard_map/final1/pallas_call | solution.py:326
  (129 shorter events, 38.3 us)
Async XLA Ops:
  3.6 11.1 %collective-permute-start = (f32[32,1024]{1,0:T(8,128)S(1)}, f32[32,1024]{1,0:T(8,128)S(1)}, u32[]{:S(2)}, u32[]{:S(2)}) collective-permute-start(f32[32,1024]{1,0:T(8,128)S(1)} %get-tuple-element.60), channel_id=1, source_target_pairs={{0,64},{32,96},{64,0},{96,32},{1,65},{33,97},{65,1},{97,33},{2,66}... | collective-permute-start | bytes 393224 | tf_op jit(solution)/shard_map/ppermute | solution.py:387
  7.6 9.5 %collective-permute-start.1 = (f32[32,1024]{1,0:T(8,128)S(1)}, f32[32,1024]{1,0:T(8,128)S(1)}, u32[]{:S(2)}, u32[]{:S(2)}) collective-permute-start(f32[32,1024]{1,0:T(8,128)S(1)} %get-tuple-element.61), channel_id=1, source_target_pairs={{0,32},{32,64},{64,96},{96,0},{1,33},{33,65},{65,97},{97,1},{2,34}... | collective-permute-start | bytes 393224 | tf_op jit(solution)/shard_map/ppermute | solution.py:387
  8.6 8.5 %collective-permute-start.2 = (f32[32,1024]{1,0:T(8,128)S(1)}, f32[32,1024]{1,0:T(8,128)S(1)}, u32[]{:S(2)}, u32[]{:S(2)}) collective-permute-start(f32[32,1024]{1,0:T(8,128)S(1)} %get-tuple-element.62), channel_id=1, source_target_pairs={{0,96},{32,0},{64,32},{96,64},{1,97},{33,1},{65,33},{97,65},{2,98}... | collective-permute-start | bytes 393224 | tf_op jit(solution)/shard_map/ppermute | solution.py:387
  13.7 7.4 %collective-permute-start.15 = (f32[32,1024]{1,0:T(8,128)S(1)}, f32[32,1024]{1,0:T(8,128)S(1)}, u32[]{:S(2)}, u32[]{:S(2)}) collective-permute-start(f32[32,1024]{1,0:T(8,128)S(1)} %get-tuple-element.72), channel_id=1, source_target_pairs={{0,64},{32,96},{64,0},{96,32},{1,65},{33,97},{65,1},{97,33},{2,66}... | collective-permute-start | bytes 393224 | tf_op jit(solution)/shard_map/ppermute | solution.py:387
  13.8 8.5 %collective-permute-start.16 = (f32[32,1024]{1,0:T(8,128)S(1)}, f32[32,1024]{1,0:T(8,128)S(1)}, u32[]{:S(2)}, u32[]{:S(2)}) collective-permute-start(f32[32,1024]{1,0:T(8,128)S(1)} %get-tuple-element.73), channel_id=1, source_target_pairs={{0,32},{32,64},{64,96},{96,0},{1,33},{33,65},{65,97},{97,1},{2,34}... | collective-permute-start | bytes 393224 | tf_op jit(solution)/shard_map/ppermute | solution.py:387
  14.7 7.6 %collective-permute-start.17 = (f32[32,1024]{1,0:T(8,128)S(1)}, f32[32,1024]{1,0:T(8,128)S(1)}, u32[]{:S(2)}, u32[]{:S(2)}) collective-permute-start(f32[32,1024]{1,0:T(8,128)S(1)} %get-tuple-element.74), channel_id=1, source_target_pairs={{0,96},{32,0},{64,32},{96,64},{1,97},{33,1},{65,33},{97,65},{2,98}... | collective-permute-start | bytes 393224 | tf_op jit(solution)/shard_map/ppermute | solution.py:387
  17.2 10.2 %collective-permute-start.3 = (f32[32,1024]{1,0:T(8,128)S(1)}, f32[32,1024]{1,0:T(8,128)S(1)}, u32[]{:S(2)}, u32[]{:S(2)}) collective-permute-start(f32[32,1024]{1,0:T(8,128)S(1)} %add_add_fusion.7), channel_id=1, source_target_pairs={{0,16},{16,0},{1,17},{17,1},{2,18},{18,2},{3,19},{19,3},{4,20},{20... | collective-permute-start | bytes 393224 | tf_op jit(solution)/shard_map/ppermute | solution.py:393
  22.3 8.3 %collective-permute-start.18 = (f32[32,1024]{1,0:T(8,128)S(1)}, f32[32,1024]{1,0:T(8,128)S(1)}, u32[]{:S(2)}, u32[]{:S(2)}) collective-permute-start(f32[32,1024]{1,0:T(8,128)S(1)} %add_add_fusion.5), channel_id=1, source_target_pairs={{0,16},{16,0},{1,17},{17,1},{2,18},{18,2},{3,19},{19,3},{4,20},{20... | collective-permute-start | bytes 393224 | tf_op jit(solution)/shard_map/ppermute | solution.py:393
  27.4 8.9 %collective-permute-start.6 = (f32[32,1024]{1,0:T(8,128)S(1)}, f32[32,1024]{1,0:T(8,128)S(1)}, u32[]{:S(2)}, u32[]{:S(2)}) collective-permute-start(f32[32,1024]{1,0:T(8,128)S(1)} %add.121.refs_1_), channel_id=1, source_target_pairs={{0,32},{32,64},{64,96},{96,0},{1,33},{33,65},{65,97},{97,1},{2,34}... | collective-permute-start | bytes 393224 | tf_op jit(solution)/shard_map/ppermute | solution.py:397
  27.4 8.8 %collective-permute-start.5 = (f32[32,1024]{1,0:T(8,128)S(1)}, f32[32,1024]{1,0:T(8,128)S(1)}, u32[]{:S(2)}, u32[]{:S(2)}) collective-permute-start(f32[32,1024]{1,0:T(8,128)S(1)} %add.121.refs_1_), channel_id=1, source_target_pairs={{0,64},{32,96},{64,0},{96,32},{1,65},{33,97},{65,1},{97,33},{2,66}... | collective-permute-start | bytes 393224 | tf_op jit(solution)/shard_map/ppermute | solution.py:397
  28.7 8.7 %collective-permute-start.4 = (f32[32,1024]{1,0:T(8,128)S(1)}, f32[32,1024]{1,0:T(8,128)S(1)}, u32[]{:S(2)}, u32[]{:S(2)}) collective-permute-start(f32[32,1024]{1,0:T(8,128)S(1)} %add.121.refs_1_), channel_id=1, source_target_pairs={{0,96},{32,0},{64,32},{96,64},{1,97},{33,1},{65,33},{97,65},{2,98}... | collective-permute-start | bytes 393224 | tf_op jit(solution)/shard_map/ppermute | solution.py:397
  30.7 12.2 %collective-permute-start.22 = (f32[4,8,1024]{2,1,0:T(8,128)S(1)}, f32[4,8,1024]{2,1,0:T(8,128)S(1)}, u32[]{:S(2)}, u32[]{:S(2)}) collective-permute-start(f32[4,8,1024]{2,1,0:T(8,128)S(1)} %get-tuple-element.75), channel_id=1, source_target_pairs={{0,1},{1,2},{2,3},{3,4},{4,5},{5,6},{6,7},{7,8},{8,9},{9,10},{10,1... | collective-permute-start | bytes 393224 | tf_op jit(solution)/shard_map/ppermute | solution.py:416
  30.7 13.6 %collective-permute-start.21 = (f32[32,1024]{1,0:T(8,128)S(1)}, f32[32,1024]{1,0:T(8,128)S(1)}, u32[]{:S(2)}, u32[]{:S(2)}) collective-permute-start(f32[32,1024]{1,0:T(8,128)S(1)} %add.129.refs_1_), channel_id=1, source_target_pairs={{0,32},{32,64},{64,96},{96,0},{1,33},{33,65},{65,97},{97,1},{2,34}... | collective-permute-start | bytes 393224 | tf_op jit(solution)/shard_map/ppermute | solution.py:397
  36.2 9.9 %collective-permute-start.20 = (f32[32,1024]{1,0:T(8,128)S(1)}, f32[32,1024]{1,0:T(8,128)S(1)}, u32[]{:S(2)}, u32[]{:S(2)}) collective-permute-start(f32[32,1024]{1,0:T(8,128)S(1)} %add.129.refs_1_), channel_id=1, source_target_pairs={{0,64},{32,96},{64,0},{96,32},{1,65},{33,97},{65,1},{97,33},{2,66}... | collective-permute-start | bytes 393224 | tf_op jit(solution)/shard_map/ppermute | solution.py:397
  36.2 9.9 %collective-permute-start.19 = (f32[32,1024]{1,0:T(8,128)S(1)}, f32[32,1024]{1,0:T(8,128)S(1)}, u32[]{:S(2)}, u32[]{:S(2)}) collective-permute-start(f32[32,1024]{1,0:T(8,128)S(1)} %add.129.refs_1_), channel_id=1, source_target_pairs={{0,96},{32,0},{64,32},{96,64},{1,97},{33,1},{65,33},{97,65},{2,98}... | collective-permute-start | bytes 393224 | tf_op jit(solution)/shard_map/ppermute | solution.py:397
  40.5 9.6 %collective-permute-start.8 = (f32[32,1024]{1,0:T(8,128)S(1)}, f32[32,1024]{1,0:T(8,128)S(1)}, u32[]{:S(2)}, u32[]{:S(2)}) collective-permute-start(f32[32,1024]{1,0:T(8,128)S(1)} %get-tuple-element.67), channel_id=1, source_target_pairs={{0,64},{32,96},{64,0},{96,32},{1,65},{33,97},{65,1},{97,33},{2,66}... | collective-permute-start | bytes 393224 | tf_op jit(solution)/shard_map/ppermute | solution.py:387
  42.9 9.9 %collective-permute-start.9 = (f32[32,1024]{1,0:T(8,128)S(1)}, f32[32,1024]{1,0:T(8,128)S(1)}, u32[]{:S(2)}, u32[]{:S(2)}) collective-permute-start(f32[32,1024]{1,0:T(8,128)S(1)} %get-tuple-element.68), channel_id=1, source_target_pairs={{0,32},{32,64},{64,96},{96,0},{1,33},{33,65},{65,97},{97,1},{2,34}... | collective-permute-start | bytes 393224 | tf_op jit(solution)/shard_map/ppermute | solution.py:387
  44.3 8.4 %collective-permute-start.10 = (f32[32,1024]{1,0:T(8,128)S(1)}, f32[32,1024]{1,0:T(8,128)S(1)}, u32[]{:S(2)}, u32[]{:S(2)}) collective-permute-start(f32[32,1024]{1,0:T(8,128)S(1)} %get-tuple-element.69), channel_id=1, source_target_pairs={{0,96},{32,0},{64,32},{96,64},{1,97},{33,1},{65,33},{97,65},{2,98}... | collective-permute-start | bytes 393224 | tf_op jit(solution)/shard_map/ppermute | solution.py:387
  49.5 7.6 %collective-permute-start.32 = (f32[32,1024]{1,0:T(8,128)S(1)}, f32[32,1024]{1,0:T(8,128)S(1)}, u32[]{:S(2)}, u32[]{:S(2)}) collective-permute-start(f32[32,1024]{1,0:T(8,128)S(1)} %get-tuple-element.87), channel_id=1, source_target_pairs={{0,32},{32,64},{64,96},{96,0},{1,33},{33,65},{65,97},{97,1},{2,34}... | collective-permute-start | bytes 393224 | tf_op jit(solution)/shard_map/ppermute | solution.py:387
  59.6 9.3 %collective-permute-start.14 = (f32[32,1024]{1,0:T(8,128)S(1)}, f32[32,1024]{1,0:T(8,128)S(1)}, u32[]{:S(2)}, u32[]{:S(2)}) collective-permute-start(f32[32,1024]{1,0:T(8,128)S(1)} %add.125.refs_2_), channel_id=1, source_target_pairs={{0,32},{32,64},{64,96},{96,0},{1,33},{33,65},{65,97},{97,1},{2,34}... | collective-permute-start | bytes 393224 | tf_op jit(solution)/shard_map/ppermute | solution.py:397
  59.7 11.2 %collective-permute-start.13 = (f32[32,1024]{1,0:T(8,128)S(1)}, f32[32,1024]{1,0:T(8,128)S(1)}, u32[]{:S(2)}, u32[]{:S(2)}) collective-permute-start(f32[32,1024]{1,0:T(8,128)S(1)} %add.125.refs_2_), channel_id=1, source_target_pairs={{0,64},{32,96},{64,0},{96,32},{1,65},{33,97},{65,1},{97,33},{2,66}... | collective-permute-start | bytes 393224 | tf_op jit(solution)/shard_map/ppermute | solution.py:397
  63.0 9.5 %collective-permute-start.12 = (f32[32,1024]{1,0:T(8,128)S(1)}, f32[32,1024]{1,0:T(8,128)S(1)}, u32[]{:S(2)}, u32[]{:S(2)}) collective-permute-start(f32[32,1024]{1,0:T(8,128)S(1)} %add.125.refs_2_), channel_id=1, source_target_pairs={{0,96},{32,0},{64,32},{96,64},{1,97},{33,1},{65,33},{97,65},{2,98}... | collective-permute-start | bytes 393224 | tf_op jit(solution)/shard_map/ppermute | solution.py:397
  64.1 13.3 %collective-permute-start.38 = (f32[4,8,1024]{2,1,0:T(8,128)S(1)}, f32[4,8,1024]{2,1,0:T(8,128)S(1)}, u32[]{:S(2)}, u32[]{:S(2)}) collective-permute-start(f32[4,8,1024]{2,1,0:T(8,128)S(1)} %get-tuple-element.89), channel_id=1, source_target_pairs={{0,1},{1,2},{2,3},{3,4},{4,5},{5,6},{6,7},{7,8},{8,9},{9,10},{10,1... | collective-permute-start | bytes 393224 | tf_op jit(solution)/shard_map/ppermute | solution.py:416
  64.1 13.2 %collective-permute-start.37 = (f32[32,1024]{1,0:T(8,128)S(1)}, f32[32,1024]{1,0:T(8,128)S(1)}, u32[]{:S(2)}, u32[]{:S(2)}) collective-permute-start(f32[32,1024]{1,0:T(8,128)S(1)} %add.137.refs_2_), channel_id=1, source_target_pairs={{0,32},{32,64},{64,96},{96,0},{1,33},{33,65},{65,97},{97,1},{2,34}... | collective-permute-start | bytes 393224 | tf_op jit(solution)/shard_map/ppermute | solution.py:397
  68.9 11.7 %collective-permute-start.36 = (f32[32,1024]{1,0:T(8,128)S(1)}, f32[32,1024]{1,0:T(8,128)S(1)}, u32[]{:S(2)}, u32[]{:S(2)}) collective-permute-start(f32[32,1024]{1,0:T(8,128)S(1)} %add.137.refs_2_), channel_id=1, source_target_pairs={{0,64},{32,96},{64,0},{96,32},{1,65},{33,97},{65,1},{97,33},{2,66}... | collective-permute-start | bytes 393224 | tf_op jit(solution)/shard_map/ppermute | solution.py:397
  71.0 9.6 %collective-permute-start.35 = (f32[32,1024]{1,0:T(8,128)S(1)}, f32[32,1024]{1,0:T(8,128)S(1)}, u32[]{:S(2)}, u32[]{:S(2)}) collective-permute-start(f32[32,1024]{1,0:T(8,128)S(1)} %add.137.refs_2_), channel_id=1, source_target_pairs={{0,96},{32,0},{64,32},{96,64},{1,97},{33,1},{65,33},{97,65},{2,98}... | collective-permute-start | bytes 393224 | tf_op jit(solution)/shard_map/ppermute | solution.py:397
  75.5 10.3 %collective-permute-start.24 = (f32[32,1024]{1,0:T(8,128)S(1)}, f32[32,1024]{1,0:T(8,128)S(1)}, u32[]{:S(2)}, u32[]{:S(2)}) collective-permute-start(f32[32,1024]{1,0:T(8,128)S(1)} %get-tuple-element.81), channel_id=1, source_target_pairs={{0,64},{32,96},{64,0},{96,32},{1,65},{33,97},{65,1},{97,33},{2,66}... | collective-permute-start | bytes 393224 | tf_op jit(solution)/shard_map/ppermute | solution.py:387
  77.3 10.2 %collective-permute-start.25 = (f32[32,1024]{1,0:T(8,128)S(1)}, f32[32,1024]{1,0:T(8,128)S(1)}, u32[]{:S(2)}, u32[]{:S(2)}) collective-permute-start(f32[32,1024]{1,0:T(8,128)S(1)} %get-tuple-element.82), channel_id=1, source_target_pairs={{0,32},{32,64},{64,96},{96,0},{1,33},{33,65},{65,97},{97,1},{2,34}... | collective-permute-start | bytes 393224 | tf_op jit(solution)/shard_map/ppermute | solution.py:387
  77.3 10.2 %collective-permute-start.26 = (f32[32,1024]{1,0:T(8,128)S(1)}, f32[32,1024]{1,0:T(8,128)S(1)}, u32[]{:S(2)}, u32[]{:S(2)}) collective-permute-start(f32[32,1024]{1,0:T(8,128)S(1)} %get-tuple-element.83), channel_id=1, source_target_pairs={{0,96},{32,0},{64,32},{96,64},{1,97},{33,1},{65,33},{97,65},{2,98}... | collective-permute-start | bytes 393224 | tf_op jit(solution)/shard_map/ppermute | solution.py:387
  84.3 7.8 %collective-permute-start.41 = (f32[32,1024]{1,0:T(8,128)S(1)}, f32[32,1024]{1,0:T(8,128)S(1)}, u32[]{:S(2)}, u32[]{:S(2)}) collective-permute-start(f32[32,1024]{1,0:T(8,128)S(1)} %get-tuple-element.97), channel_id=1, source_target_pairs={{0,32},{32,64},{64,96},{96,0},{1,33},{33,65},{65,97},{97,1},{2,34}... | collective-permute-start | bytes 393224 | tf_op jit(solution)/shard_map/ppermute | solution.py:387
  87.6 8.2 %collective-permute-start.27 = (f32[32,1024]{1,0:T(8,128)S(1)}, f32[32,1024]{1,0:T(8,128)S(1)}, u32[]{:S(2)}, u32[]{:S(2)}) collective-permute-start(f32[32,1024]{1,0:T(8,128)S(1)} %add_add_fusion.4), channel_id=1, source_target_pairs={{0,16},{16,0},{1,17},{17,1},{2,18},{18,2},{3,19},{19,3},{4,20},{20... | collective-permute-start | bytes 393224 | tf_op jit(solution)/shard_map/ppermute | solution.py:393
  95.8 8.9 %collective-permute-start.30 = (f32[32,1024]{1,0:T(8,128)S(1)}, f32[32,1024]{1,0:T(8,128)S(1)}, u32[]{:S(2)}, u32[]{:S(2)}) collective-permute-start(f32[32,1024]{1,0:T(8,128)S(1)} %add.133.refs_2_), channel_id=1, source_target_pairs={{0,32},{32,64},{64,96},{96,0},{1,33},{33,65},{65,97},{97,1},{2,34}... | collective-permute-start | bytes 393224 | tf_op jit(solution)/shard_map/ppermute | solution.py:397
  95.9 8.9 %collective-permute-start.29 = (f32[32,1024]{1,0:T(8,128)S(1)}, f32[32,1024]{1,0:T(8,128)S(1)}, u32[]{:S(2)}, u32[]{:S(2)}) collective-permute-start(f32[32,1024]{1,0:T(8,128)S(1)} %add.133.refs_2_), channel_id=1, source_target_pairs={{0,64},{32,96},{64,0},{96,32},{1,65},{33,97},{65,1},{97,33},{2,66}... | collective-permute-start | bytes 393224 | tf_op jit(solution)/shard_map/ppermute | solution.py:397
  99.2 7.4 %collective-permute-start.28 = (f32[32,1024]{1,0:T(8,128)S(1)}, f32[32,1024]{1,0:T(8,128)S(1)}, u32[]{:S(2)}, u32[]{:S(2)}) collective-permute-start(f32[32,1024]{1,0:T(8,128)S(1)} %add.133.refs_2_), channel_id=1, source_target_pairs={{0,96},{32,0},{64,32},{96,64},{1,97},{33,1},{65,33},{97,65},{2,98}... | collective-permute-start | bytes 393224 | tf_op jit(solution)/shard_map/ppermute | solution.py:397
  99.3 12.8 %collective-permute-start.47 = (f32[4,8,1024]{2,1,0:T(8,128)S(1)}, f32[4,8,1024]{2,1,0:T(8,128)S(1)}, u32[]{:S(2)}, u32[]{:S(2)}) collective-permute-start(f32[4,8,1024]{2,1,0:T(8,128)S(1)} %get-tuple-element.99), channel_id=1, source_target_pairs={{0,1},{1,2},{2,3},{3,4},{4,5},{5,6},{6,7},{7,8},{8,9},{9,10},{10,1... | collective-permute-start | bytes 393224 | tf_op jit(solution)/shard_map/ppermute | solution.py:416
  99.3 14.1 %collective-permute-start.46 = (f32[32,1024]{1,0:T(8,128)S(1)}, f32[32,1024]{1,0:T(8,128)S(1)}, u32[]{:S(2)}, u32[]{:S(2)}) collective-permute-start(f32[32,1024]{1,0:T(8,128)S(1)} %add.141.refs_2_), channel_id=1, source_target_pairs={{0,32},{32,64},{64,96},{96,0},{1,33},{33,65},{65,97},{97,1},{2,34}... | collective-permute-start | bytes 393224 | tf_op jit(solution)/shard_map/ppermute | solution.py:397
  104.8 10.5 %collective-permute-start.45 = (f32[32,1024]{1,0:T(8,128)S(1)}, f32[32,1024]{1,0:T(8,128)S(1)}, u32[]{:S(2)}, u32[]{:S(2)}) collective-permute-start(f32[32,1024]{1,0:T(8,128)S(1)} %add.141.refs_2_), channel_id=1, source_target_pairs={{0,64},{32,96},{64,0},{96,32},{1,65},{33,97},{65,1},{97,33},{2,66}... | collective-permute-start | bytes 393224 | tf_op jit(solution)/shard_map/ppermute | solution.py:397
  104.8 10.5 %collective-permute-start.44 = (f32[32,1024]{1,0:T(8,128)S(1)}, f32[32,1024]{1,0:T(8,128)S(1)}, u32[]{:S(2)}, u32[]{:S(2)}) collective-permute-start(f32[32,1024]{1,0:T(8,128)S(1)} %add.141.refs_2_), channel_id=1, source_target_pairs={{0,96},{32,0},{64,32},{96,64},{1,97},{33,1},{65,33},{97,65},{2,98}... | collective-permute-start | bytes 393224 | tf_op jit(solution)/shard_map/ppermute | solution.py:397
  110.3 9.5 %collective-permute-start.52 = (f32[32,1024]{1,0:T(8,128)S(1)}, f32[32,1024]{1,0:T(8,128)S(1)}, u32[]{:S(2)}, u32[]{:S(2)}) collective-permute-start(f32[32,1024]{1,0:T(8,128)S(1)} %get-tuple-element.106), channel_id=1, source_target_pairs={{0,64},{32,96},{64,0},{96,32},{1,65},{33,97},{65,1},{97,33},{2,66}... | collective-permute-start | bytes 393224 | tf_op jit(solution)/shard_map/ppermute | solution.py:387
  112.0 10.8 %collective-permute-start.53 = (f32[32,1024]{1,0:T(8,128)S(1)}, f32[32,1024]{1,0:T(8,128)S(1)}, u32[]{:S(2)}, u32[]{:S(2)}) collective-permute-start(f32[32,1024]{1,0:T(8,128)S(1)} %get-tuple-element.107), channel_id=1, source_target_pairs={{0,32},{32,64},{64,96},{96,0},{1,33},{33,65},{65,97},{97,1},{2,34}... | collective-permute-start | bytes 393224 | tf_op jit(solution)/shard_map/ppermute | solution.py:387
  113.4 9.4 %collective-permute-start.54 = (f32[32,1024]{1,0:T(8,128)S(1)}, f32[32,1024]{1,0:T(8,128)S(1)}, u32[]{:S(2)}, u32[]{:S(2)}) collective-permute-start(f32[32,1024]{1,0:T(8,128)S(1)} %get-tuple-element.108), channel_id=1, source_target_pairs={{0,96},{32,0},{64,32},{96,64},{1,97},{33,1},{65,33},{97,65},{2,98}... | collective-permute-start | bytes 393224 | tf_op jit(solution)/shard_map/ppermute | solution.py:387
  122.9 7.6 %collective-permute-start.55 = (f32[32,1024]{1,0:T(8,128)S(1)}, f32[32,1024]{1,0:T(8,128)S(1)}, u32[]{:S(2)}, u32[]{:S(2)}) collective-permute-start(f32[32,1024]{1,0:T(8,128)S(1)} %add_add_fusion), channel_id=1, source_target_pairs={{0,16},{16,0},{1,17},{17,1},{2,18},{18,2},{3,19},{19,3},{4,20},{20... | collective-permute-start | bytes 393224 | tf_op jit(solution)/shard_map/ppermute | solution.py:393
  161.1 8.0 %collective-permute-start.56 = (f32[32,1024]{1,0:T(8,128)S(1)}, f32[32,1024]{1,0:T(8,128)S(1)}, u32[]{:S(2)}, u32[]{:S(2)}) collective-permute-start(f32[32,1024]{1,0:T(8,128)S(1)} %get-tuple-element.109), channel_id=1, source_target_pairs={{0,16},{16,0},{1,17},{17,1},{2,18},{18,2},{3,19},{19,3},{4,20},{20... | collective-permute-start | bytes 393224 | tf_op jit(solution)/shard_map/ppermute | solution.py:393
  165.0 7.9 %collective-permute-start.63 = (f32[32,1024]{1,0:T(8,128)S(1)}, f32[32,1024]{1,0:T(8,128)S(1)}, u32[]{:S(2)}, u32[]{:S(2)}) collective-permute-start(f32[32,1024]{1,0:T(8,128)S(1)} %add.151.p0), channel_id=1, source_target_pairs={{0,32},{32,64},{64,96},{96,0},{1,33},{33,65},{65,97},{97,1},{2,34}... | collective-permute-start | bytes 393224 | tf_op jit(solution)/shard_map/ppermute | solution.py:397
  165.7 10.0 %collective-permute-start.62 = (f32[32,1024]{1,0:T(8,128)S(1)}, f32[32,1024]{1,0:T(8,128)S(1)}, u32[]{:S(2)}, u32[]{:S(2)}) collective-permute-start(f32[32,1024]{1,0:T(8,128)S(1)} %add.151.p0), channel_id=1, source_target_pairs={{0,64},{32,96},{64,0},{96,32},{1,65},{33,97},{65,1},{97,33},{2,66}... | collective-permute-start | bytes 393224 | tf_op jit(solution)/shard_map/ppermute | solution.py:397
  168.4 7.7 %collective-permute-start.61 = (f32[32,1024]{1,0:T(8,128)S(1)}, f32[32,1024]{1,0:T(8,128)S(1)}, u32[]{:S(2)}, u32[]{:S(2)}) collective-permute-start(f32[32,1024]{1,0:T(8,128)S(1)} %add.151.p0), channel_id=1, source_target_pairs={{0,96},{32,0},{64,32},{96,64},{1,97},{33,1},{65,33},{97,65},{2,98}... | collective-permute-start | bytes 393224 | tf_op jit(solution)/shard_map/ppermute | solution.py:397
  169.2 9.8 %collective-permute-start.59 = (f32[32,1024]{1,0:T(8,128)S(1)}, f32[32,1024]{1,0:T(8,128)S(1)}, u32[]{:S(2)}, u32[]{:S(2)}) collective-permute-start(f32[32,1024]{1,0:T(8,128)S(1)} %add.150.p0), channel_id=1, source_target_pairs={{0,32},{32,64},{64,96},{96,0},{1,33},{33,65},{65,97},{97,1},{2,34}... | collective-permute-start | bytes 393224 | tf_op jit(solution)/shard_map/ppermute | solution.py:397
  170.5 8.5 %collective-permute-start.58 = (f32[32,1024]{1,0:T(8,128)S(1)}, f32[32,1024]{1,0:T(8,128)S(1)}, u32[]{:S(2)}, u32[]{:S(2)}) collective-permute-start(f32[32,1024]{1,0:T(8,128)S(1)} %add.150.p0), channel_id=1, source_target_pairs={{0,64},{32,96},{64,0},{96,32},{1,65},{33,97},{65,1},{97,33},{2,66}... | collective-permute-start | bytes 393224 | tf_op jit(solution)/shard_map/ppermute | solution.py:397
  (23 other events, 319.9 us)

commit v4 on v3

--- a/solution.py
+++ b/solution.py
@@ -124,10 +124,10 @@
         s[...] = sums[k]
 
 
-def final_kernel(c, meta, weight, eta, p0, p1, p2, p3, *refs):
+def final_kernel(c, which, meta, weight, eta, *refs):
     out, pot_out, field, pot, sems, pot_sems = refs[-6:]
     copies = []
-    for k, p in enumerate((p0, p1, p2, p3)):
+    for k, p in zip(which, refs):
         for rg in range(HALF // 8):
             base = 8 * rg
             v = p[base : base + 8, :]
@@ -321,15 +321,16 @@
     return out[0], out[1:5], *((None, None) if last else out[5:7])
 
 
-def final(c, eta, pots, weight, meta, previous):
-    args = [meta, weight] + [near(x) for x in (eta, *pots)] + list(previous or ())
+def final(c, which, eta, pots, weight, meta, previous):
+    args = [meta, weight, near(eta)] + [near(pots[k]) for k in which] + list(previous or ())
+    count = 3 + len(which)
     return pl.pallas_call(
-        functools.partial(final_kernel, c),
+        functools.partial(final_kernel, c, which),
         out_shape=(shape(GRAINS, PLANES, ROWS, N), shape(PLANES, ROWS, N)),
-        in_specs=[SMEM_SPEC, SMEM_SPEC] + [VMEM_SPEC] * 5 + [ANY_SPEC] * len(previous or ()),
+        in_specs=[SMEM_SPEC, SMEM_SPEC] + [VMEM_SPEC] * (count - 2) + [ANY_SPEC] * len(previous or ()),
         out_specs=(ANY_SPEC, ANY_SPEC),
         scratch_shapes=[CHUNK, STACKED] + [pltpu.SemaphoreType.DMA((PLANES,))] * 2,
-        input_output_aliases={7: 0, 8: 1} if previous else {}, name=f"final{c}", compiler_params=limit(8),
+        input_output_aliases={count: 0, count + 1: 1} if previous else {}, name=f"final{c}_{len(which)}", compiler_params=limit(8),
     )(*args)
 
 
@@ -430,8 +431,9 @@
     pots = row_backward(mixed, meta)
     pots = [to_all(with_partner(p)) for p in pots]
     result = None
-    for c in chunks:
-        result = final(c, eta[c], pots[c], eigen_weight, meta, result)
+    for which in ((0,), (1, 2, 3)):
+        for c in chunks:
+            result = final(c, which, eta[c], pots[c], eigen_weight, meta, result)
     return tuple(result)
 
 

time: 183 us -> 185 us (1.011)
  waiting for transfers between devices: 28.9 us -> 32.2 us
  starting transfers between devices: 93.1 us -> 90.2 us
  Pallas kernels: 38.4 us -> 41 us
    ppermute x10, waiting for transfers between devices: 7.78 us -> 13 us  [with_partner(): return x + lax.ppermute(x, 'xh', [(0, 1), (1, 0)])]
    ppermute x10, starting transfers between devices: 21.3 us -> 17.9 us  [with_partner(): return x + lax.ppermute(x, 'xh', [(0, 1), (1, 0)])]
    pallas_call x2 -> x4, Pallas kernels: 5.75 us -> 8.39 us  [final(): pl.pallas_call(functools.partial(final_kernel, c, which), out_shape=(shap...]
    ppermute x24, waiting for transfers between devices: 12 us -> 9.46 us  [to_all(): parts = {k: lax.ppermute(x, 'z', shift(-k)) for k in (2, 1, 3)}]
  transfers between devices with their start and end apart: 64 -> 64, of which waited for: 16 -> 24; matrix products, arithmetic and copies ran while one was open for 0% -> 0% of each run, Pallas kernels for 16% -> 17%
where the time goes in v4:
time: 185 us
  starting transfers between devices  90.2 us (49%)
  Pallas kernels  41 us (22%)
  waiting for transfers between devices  32.2 us (17%)
  blocking collectives  19.4 us (10%)
    ppermute x24, starting transfers between devices, to_owner(): lax.ppermute(sums[k], 'z', shift(k))  37.4 us
    ppermute x24, starting transfers between devices, to_all(): parts = {k: lax.ppermute(x, 'z', shift(-k)) for k in (2, 1, 3)}  30.9 us
    pallas_call x6, Pallas kernels, advance(): pl.pallas_call(functools.partial(step_kernel, last, len(ready)), out_shap...  19.2 us
    ppermute x10, starting transfers between devices, with_partner(): return x + lax.ppermute(x, 'xh', [(0, 1), (1, 0)])  17.9 us
    ppermute x10, waiting for transfers between devices, with_partner(): return x + lax.ppermute(x, 'xh', [(0, 1), (1, 0)])  13 us
    all_to_all x1, blocking collectives, local(): spectrum = lax.all_to_all(spectrum, ROW_AXES, 0, 0, tiled=True)  10.1 us
    ppermute x24, waiting for transfers between devices, to_all(): parts = {k: lax.ppermute(x, 'z', shift(-k)) for k in (2, 1, 3)}  9.46 us
    ppermute x24, waiting for transfers between devices, to_owner(): lax.ppermute(sums[k], 'z', shift(k))  9.39 us
  transfers between devices with their start and end apart: 64, of which 24 were waited for; matrix products, arithmetic and copies ran while one was open for 0% of the time, Pallas kernels for 17%

profile of v4, /device:TPU:0, one launch (start us, length us, event | category | flops | bytes accessed | tf_op | source)
XLA Modules:
  0.0 184.6 jit_solution(13417048944482491171)
XLA Ops:
  0.7 2.8 %squares1.1 = (f32[4,8,32,1024]{3,2,1,0:T(8,128)S(1)}, f32[32,1024]{1,0:T(8,128)S(1)}, f32[32,1024]{1,0:T(8,128)S(1)}, f32[32,1024]{1,0:T(8,128)S(1)}, f32[32,10...) custom-call(s32[3]{0:T(128)S(1)} %pad_add_fusion.meta, f32[8,4,64,1024]{3,2,1,0:T(8,128)} %order.3), custom_call_target="tpu_custom_call" | custom-call | tf_op jit(solution)/shard_map/squares1/pallas_call | solution.py:305
  3.6 4.1 %collective-permute-start = (f32[32,1024]{1,0:T(8,128)S(1)}, f32[32,1024]{1,0:T(8,128)S(1)}, u32[]{:S(2)}, u32[]{:S(2)}) collective-permute-start(f32[32,1024]{1,0:T(8,128)S(1)} %get-tuple-element.64), channel_id=1, source_target_pairs={{0,64},{32,96},{64,0},{96,32},{1,65},{33,97},{65,1},{97,33},{2,66}... | collective-permute-start | bytes 393224 | tf_op jit(solution)/shard_map/ppermute | solution.py:388
  8.6 2.2 %collective-permute-start.2 = (f32[32,1024]{1,0:T(8,128)S(1)}, f32[32,1024]{1,0:T(8,128)S(1)}, u32[]{:S(2)}, u32[]{:S(2)}) collective-permute-start(f32[32,1024]{1,0:T(8,128)S(1)} %get-tuple-element.66), channel_id=1, source_target_pairs={{0,96},{32,0},{64,32},{96,64},{1,97},{33,1},{65,33},{97,65},{2,98}... | collective-permute-start | bytes 393224 | tf_op jit(solution)/shard_map/ppermute | solution.py:388
  10.9 2.8 %squares0.1 = (f32[4,8,32,1024]{3,2,1,0:T(8,128)S(1)}, f32[32,1024]{1,0:T(8,128)S(1)}, f32[32,1024]{1,0:T(8,128)S(1)}, f32[32,1024]{1,0:T(8,128)S(1)}, f32[32,10...) custom-call(s32[3]{0:T(128)S(1)} %pad_add_fusion.meta, f32[8,4,64,1024]{3,2,1,0:T(8,128)} %order.3), custom_call_target="tpu_custom_call" | custom-call | tf_op jit(solution)/shard_map/squares0/pallas_call | solution.py:305
  14.7 2.5 %collective-permute-start.17 = (f32[32,1024]{1,0:T(8,128)S(1)}, f32[32,1024]{1,0:T(8,128)S(1)}, u32[]{:S(2)}, u32[]{:S(2)}) collective-permute-start(f32[32,1024]{1,0:T(8,128)S(1)} %get-tuple-element.78), channel_id=1, source_target_pairs={{0,96},{32,0},{64,32},{96,64},{1,97},{33,1},{65,33},{97,65},{2,98}... | collective-permute-start | bytes 393224 | tf_op jit(solution)/shard_map/ppermute | solution.py:388
  17.2 3.1 %collective-permute-start.3 = (f32[32,1024]{1,0:T(8,128)S(1)}, f32[32,1024]{1,0:T(8,128)S(1)}, u32[]{:S(2)}, u32[]{:S(2)}) collective-permute-start(f32[32,1024]{1,0:T(8,128)S(1)} %add_add_fusion.7), channel_id=1, source_target_pairs={{0,16},{16,0},{1,17},{17,1},{2,18},{18,2},{3,19},{19,3},{4,20},{20... | collective-permute-start | bytes 393224 | tf_op jit(solution)/shard_map/ppermute | solution.py:394
  22.3 3.1 %collective-permute-start.18 = (f32[32,1024]{1,0:T(8,128)S(1)}, f32[32,1024]{1,0:T(8,128)S(1)}, u32[]{:S(2)}, u32[]{:S(2)}) collective-permute-start(f32[32,1024]{1,0:T(8,128)S(1)} %add_add_fusion.5), channel_id=1, source_target_pairs={{0,16},{16,0},{1,17},{17,1},{2,18},{18,2},{3,19},{19,3},{4,20},{20... | collective-permute-start | bytes 393224 | tf_op jit(solution)/shard_map/ppermute | solution.py:394
  25.4 1.9 %collective-permute-start.7 = (f32[4,8,1024]{2,1,0:T(8,128)S(1)}, f32[4,8,1024]{2,1,0:T(8,128)S(1)}, u32[]{:S(2)}, u32[]{:S(2)}) collective-permute-start(f32[4,8,1024]{2,1,0:T(8,128)S(1)} %get-tuple-element.68), channel_id=1, source_target_pairs={{1,0},{2,1},{3,2},{4,3},{5,4},{6,5},{7,6},{8,7},{9,8},{10,9},{11,1... | collective-permute-start | bytes 393224 | tf_op jit(solution)/shard_map/ppermute | solution.py:418
  29.9 2.4 %collective-permute-start.19 = (f32[32,1024]{1,0:T(8,128)S(1)}, f32[32,1024]{1,0:T(8,128)S(1)}, u32[]{:S(2)}, u32[]{:S(2)}) collective-permute-start(f32[32,1024]{1,0:T(8,128)S(1)} %add.129.refs_1_), channel_id=1, source_target_pairs={{0,96},{32,0},{64,32},{96,64},{1,97},{33,1},{65,33},{97,65},{2,98}... | collective-permute-start | bytes 393224 | tf_op jit(solution)/shard_map/ppermute | solution.py:398
  35.1 2.0 %collective-permute-start.21 = (f32[32,1024]{1,0:T(8,128)S(1)}, f32[32,1024]{1,0:T(8,128)S(1)}, u32[]{:S(2)}, u32[]{:S(2)}) collective-permute-start(f32[32,1024]{1,0:T(8,128)S(1)} %add.129.refs_1_), channel_id=1, source_target_pairs={{0,32},{32,64},{64,96},{96,0},{1,33},{33,65},{65,97},{97,1},{2,34}... | collective-permute-start | bytes 393224 | tf_op jit(solution)/shard_map/ppermute | solution.py:398
  38.0 3.0 %step0_1.1 = (f32[4,8,32,1024]{3,2,1,0:T(8,128)S(1)}, f32[32,1024]{1,0:T(8,128)S(1)}, f32[32,1024]{1,0:T(8,128)S(1)}, f32[32,1024]{1,0:T(8,128)S(1)}, f32[32,102...) custom-call(f32[4,8,32,1024]{3,2,1,0:T(8,128)S(1)} %get-tuple-element.62.refs_0_, ...), custom_call_target="tpu_custom_call" | custom-call | tf_op jit(solution)/shard_map/step0_1/pallas_call | solution.py:316
  41.4 1.9 %collective-permute-start.8 = (f32[32,1024]{1,0:T(8,128)S(1)}, f32[32,1024]{1,0:T(8,128)S(1)}, u32[]{:S(2)}, u32[]{:S(2)}) collective-permute-start(f32[32,1024]{1,0:T(8,128)S(1)} %get-tuple-element.71), channel_id=1, source_target_pairs={{0,64},{32,96},{64,0},{96,32},{1,65},{33,97},{65,1},{97,33},{2,66}... | collective-permute-start | bytes 393224 | tf_op jit(solution)/shard_map/ppermute | solution.py:388
  44.6 3.0 %step0_0.1 = (f32[4,8,32,1024]{3,2,1,0:T(8,128)S(1)}, f32[32,1024]{1,0:T(8,128)S(1)}, f32[32,1024]{1,0:T(8,128)S(1)}, f32[32,1024]{1,0:T(8,128)S(1)}, f32[32,102...) custom-call(f32[4,8,32,1024]{3,2,1,0:T(8,128)S(1)} %get-tuple-element.74.refs_0_, ...), custom_call_target="tpu_custom_call" | custom-call | tf_op jit(solution)/shard_map/step0_0/pallas_call | solution.py:316
  47.6 2.8 %collective-permute-start.31 = (f32[32,1024]{1,0:T(8,128)S(1)}, f32[32,1024]{1,0:T(8,128)S(1)}, u32[]{:S(2)}, u32[]{:S(2)}) collective-permute-start(f32[32,1024]{1,0:T(8,128)S(1)} %get-tuple-element.90), channel_id=1, source_target_pairs={{0,64},{32,96},{64,0},{96,32},{1,65},{33,97},{65,1},{97,33},{2,66}... | collective-permute-start | bytes 393224 | tf_op jit(solution)/shard_map/ppermute | solution.py:388
  50.4 3.2 %collective-permute-start.33 = (f32[32,1024]{1,0:T(8,128)S(1)}, f32[32,1024]{1,0:T(8,128)S(1)}, u32[]{:S(2)}, u32[]{:S(2)}) collective-permute-start(f32[32,1024]{1,0:T(8,128)S(1)} %get-tuple-element.92), channel_id=1, source_target_pairs={{0,96},{32,0},{64,32},{96,64},{1,97},{33,1},{65,33},{97,65},{2,98}... | collective-permute-start | bytes 393224 | tf_op jit(solution)/shard_map/ppermute | solution.py:388
  58.4 1.8 collective-permute-done.11
  63.2 3.3 %collective-permute-start.35 = (f32[32,1024]{1,0:T(8,128)S(1)}, f32[32,1024]{1,0:T(8,128)S(1)}, u32[]{:S(2)}, u32[]{:S(2)}) collective-permute-start(f32[32,1024]{1,0:T(8,128)S(1)} %add.137.refs_2_), channel_id=1, source_target_pairs={{0,96},{32,0},{64,32},{96,64},{1,97},{33,1},{65,33},{97,65},{2,98}... | collective-permute-start | bytes 393224 | tf_op jit(solution)/shard_map/ppermute | solution.py:398
  66.5 3.8 %own_green.1.refs_0_.green = f32[16,24,128]{2,1,0:T(8,128)S(1)} custom-call(s32[3]{0:T(128)S(1)} %pad_add_fusion.meta, f32[1024,1024]{1,0:T(8,128)S(1)} %copy-done), custom_call_target="tpu_custom_call" | custom-call | tf_op jit(solution)/shard_map/own_green/pallas_call | solution.py:361
  70.9 1.7 collective-permute-start.37
  72.6 3.0 %step1_1.1 = (f32[4,8,32,1024]{3,2,1,0:T(8,128)S(1)}, f32[32,1024]{1,0:T(8,128)S(1)}, f32[32,1024]{1,0:T(8,128)S(1)}, f32[32,1024]{1,0:T(8,128)S(1)}, f32[32,102...) custom-call(f32[16,24,128]{2,1,0:T(8,128)S(1)} %own_green.1.refs_0_.green, ...), custom_call_target="tpu_custom_call" | custom-call | tf_op jit(solution)/shard_map/step1_1/pallas_call | solution.py:316
  78.2 2.1 %collective-permute-start.26 = (f32[32,1024]{1,0:T(8,128)S(1)}, f32[32,1024]{1,0:T(8,128)S(1)}, u32[]{:S(2)}, u32[]{:S(2)}) collective-permute-start(f32[32,1024]{1,0:T(8,128)S(1)} %get-tuple-element.87), channel_id=1, source_target_pairs={{0,96},{32,0},{64,32},{96,64},{1,97},{33,1},{65,33},{97,65},{2,98}... | collective-permute-start | bytes 393224 | tf_op jit(solution)/shard_map/ppermute | solution.py:388
  81.4 3.0 %step1_0.1 = (f32[4,8,32,1024]{3,2,1,0:T(8,128)S(1)}, f32[32,1024]{1,0:T(8,128)S(1)}, f32[32,1024]{1,0:T(8,128)S(1)}, f32[32,1024]{1,0:T(8,128)S(1)}, f32[32,102...) custom-call(f32[16,24,128]{2,1,0:T(8,128)S(1)} %own_green.1.refs_0_.green, ...), custom_call_target="tpu_custom_call" | custom-call | tf_op jit(solution)/shard_map/step1_0/pallas_call | solution.py:316
  85.6 2.4 %collective-permute-start.42 = (f32[32,1024]{1,0:T(8,128)S(1)}, f32[32,1024]{1,0:T(8,128)S(1)}, u32[]{:S(2)}, u32[]{:S(2)}) collective-permute-start(f32[32,1024]{1,0:T(8,128)S(1)} %get-tuple-element.102), channel_id=1, source_target_pairs={{0,96},{32,0},{64,32},{96,64},{1,97},{33,1},{65,33},{97,65},{2,98}... | collective-permute-start | bytes 393224 | tf_op jit(solution)/shard_map/ppermute | solution.py:388
  88.1 2.3 %collective-permute-start.27 = (f32[32,1024]{1,0:T(8,128)S(1)}, f32[32,1024]{1,0:T(8,128)S(1)}, u32[]{:S(2)}, u32[]{:S(2)}) collective-permute-start(f32[32,1024]{1,0:T(8,128)S(1)} %add_add_fusion.4), channel_id=1, source_target_pairs={{0,16},{16,0},{1,17},{17,1},{2,18},{18,2},{3,19},{19,3},{4,20},{20... | collective-permute-start | bytes 393224 | tf_op jit(solution)/shard_map/ppermute | solution.py:394
  93.5 1.9 %collective-permute-start.43 = (f32[32,1024]{1,0:T(8,128)S(1)}, f32[32,1024]{1,0:T(8,128)S(1)}, u32[]{:S(2)}, u32[]{:S(2)}) collective-permute-start(f32[32,1024]{1,0:T(8,128)S(1)} %add_add_fusion.2), channel_id=1, source_target_pairs={{0,16},{16,0},{1,17},{17,1},{2,18},{18,2},{3,19},{19,3},{4,20},{20... | collective-permute-start | bytes 393224 | tf_op jit(solution)/shard_map/ppermute | solution.py:394
  95.4 1.9 %collective-permute-start.39 = (f32[4,8,1024]{2,1,0:T(8,128)S(1)}, f32[4,8,1024]{2,1,0:T(8,128)S(1)}, u32[]{:S(2)}, u32[]{:S(2)}) collective-permute-start(f32[4,8,1024]{2,1,0:T(8,128)S(1)} %get-tuple-element.96), channel_id=1, source_target_pairs={{1,0},{2,1},{3,2},{4,3},{5,4},{6,5},{7,6},{8,7},{9,8},{10,9},{11,1... | collective-permute-start | bytes 393224 | tf_op jit(solution)/shard_map/ppermute | solution.py:418
  100.3 1.9 %collective-permute-start.44 = (f32[32,1024]{1,0:T(8,128)S(1)}, f32[32,1024]{1,0:T(8,128)S(1)}, u32[]{:S(2)}, u32[]{:S(2)}) collective-permute-start(f32[32,1024]{1,0:T(8,128)S(1)} %add.141.refs_2_), channel_id=1, source_target_pairs={{0,96},{32,0},{64,32},{96,64},{1,97},{33,1},{65,33},{97,65},{2,98}... | collective-permute-start | bytes 393224 | tf_op jit(solution)/shard_map/ppermute | solution.py:398
  102.9 1.7 collective-permute-start.45
  106.5 2.7 %collective-permute-done.30.refs_5_ = f32[32,1024]{1,0:T(8,128)S(1)} collective-permute-done((f32[32,1024]{1,0:T(8,128)S(1)}, f32[32,1024]{1,0:T(8,128)S(1)}, u32[]{:S(2)}, u32[]{:S(2)}) %collective-permute-start.30) | collective-permute-done | bytes 131104 | tf_op jit(solution)/shard_map/ppermute | solution.py:398
  109.2 3.6 %step2_1.1 = (f32[4,8,32,1024]{3,2,1,0:T(8,128)S(1)}, f32[32,1024]{1,0:T(8,128)S(1)}, f32[32,1024]{1,0:T(8,128)S(1)}, f32[32,1024]{1,0:T(8,128)S(1)}, f32[32,1024]{1,0:T(8,128)S(1)}) custom-call(f32[8]{0:T(128)S(1)} %copy-done.5, f32[4,8,32,1024]{3,2,1,0:T(8,128)S(1)} %get-tuple-element.83.refs_1_, f32[32,1024]{1,0:T(8,128)S(1)} %add.133.refs_2_, ...), custom_call_target="tpu_custom_call" | custom-call | tf_op jit(solution)/shard_map/step2_1/pallas_call | solution.py:316
  113.2 3.1 %collective-permute-start.54 = (f32[32,1024]{1,0:T(8,128)S(1)}, f32[32,1024]{1,0:T(8,128)S(1)}, u32[]{:S(2)}, u32[]{:S(2)}) collective-permute-start(f32[32,1024]{1,0:T(8,128)S(1)} %get-tuple-element.112), channel_id=1, source_target_pairs={{0,96},{32,0},{64,32},{96,64},{1,97},{33,1},{65,33},{97,65},{2,98}... | collective-permute-start | bytes 393224 | tf_op jit(solution)/shard_map/ppermute | solution.py:388
  116.3 3.6 %step2_0.1 = (f32[4,8,32,1024]{3,2,1,0:T(8,128)S(1)}, f32[32,1024]{1,0:T(8,128)S(1)}, f32[32,1024]{1,0:T(8,128)S(1)}, f32[32,1024]{1,0:T(8,128)S(1)}, f32[32,1024]{1,0:T(8,128)S(1)}) custom-call(f32[8]{0:T(128)S(1)} %copy-done.5, f32[4,8,32,1024]{3,2,1,0:T(8,128)S(1)} %get-tuple-element.98.refs_1_, f32[32,1024]{1,0:T(8,128)S(1)} %add.141.refs_2_, ...), custom_call_target="tpu_custom_call" | custom-call | tf_op jit(solution)/shard_map/step2_0/pallas_call | solution.py:316
  119.9 2.3 %collective-permute-start.48 = (f32[32,1024]{1,0:T(8,128)S(1)}, f32[32,1024]{1,0:T(8,128)S(1)}, u32[]{:S(2)}, u32[]{:S(2)}) collective-permute-start(f32[32,1024]{1,0:T(8,128)S(1)} %get-tuple-element.106), channel_id=1, source_target_pairs={{0,64},{32,96},{64,0},{96,32},{1,65},{33,97},{65,1},{97,33},{2,66}... | collective-permute-start | bytes 393224 | tf_op jit(solution)/shard_map/ppermute | solution.py:388
  122.2 3.2 %collective-permute-start.50 = (f32[32,1024]{1,0:T(8,128)S(1)}, f32[32,1024]{1,0:T(8,128)S(1)}, u32[]{:S(2)}, u32[]{:S(2)}) collective-permute-start(f32[32,1024]{1,0:T(8,128)S(1)} %get-tuple-element.108), channel_id=1, source_target_pairs={{0,96},{32,0},{64,32},{96,64},{1,97},{33,1},{65,33},{97,65},{2,98}... | collective-permute-start | bytes 393224 | tf_op jit(solution)/shard_map/ppermute | solution.py:388
  126.5 1.9 %collective-permute-done.49 = f32[32,1024]{1,0:T(8,128)S(1)} collective-permute-done((f32[32,1024]{1,0:T(8,128)S(1)}, f32[32,1024]{1,0:T(8,128)S(1)}, u32[]{:S(2)}, u32[]{:S(2)}) %collective-permute-start.49) | collective-permute-done | bytes 131104 | tf_op jit(solution)/shard_map/ppermute | solution.py:388
  129.2 2.8 %collective-permute-done.55 = f32[32,1024]{1,0:T(8,128)S(1)} collective-permute-done((f32[32,1024]{1,0:T(8,128)S(1)}, f32[32,1024]{1,0:T(8,128)S(1)}, u32[]{:S(2)}, u32[]{:S(2)}) %collective-permute-start.55) | collective-permute-done | bytes 131104 | tf_op jit(solution)/shard_map/ppermute | solution.py:394
  132.1 2.9 %collective-permute-done.51 = f32[32,1024]{1,0:T(8,128)S(1)} collective-permute-done((f32[32,1024]{1,0:T(8,128)S(1)}, f32[32,1024]{1,0:T(8,128)S(1)}, u32[]{:S(2)}, u32[]{:S(2)}) %collective-permute-start.51) | collective-permute-done | bytes 131104 | tf_op jit(solution)/shard_map/ppermute | solution.py:394
  136.3 10.1 %all_to_all.10.recv = f32[16,16,128]{2,1,0:T(8,128)S(1)} all-to-all(f32[16,16,128]{2,1,0:T(8,128)S(1)} %row_forward.1), channel_id=1, replica_groups=mesh['z'=4,'xh'=2,'y'=4,'xl'=2,'c'=2] {'y','xl','c'}, dimensions={0} | all-to-all | bytes 262144 | tf_op jit(solution)/shard_map/all_to_all | solution.py:428
  148.0 9.3 %all_to_all.11.recv = f32[16,16,128]{2,1,0:T(8,128)S(1)} all-to-all(f32[16,16,128]{2,1,0:T(8,128)S(1)} %column.1), channel_id=1, replica_groups=mesh['z'=4,'xh'=2,'y'=4,'xl'=2,'c'=2] {'y','xl','c'}, dimensions={0} | all-to-all | bytes 262144 | tf_op jit(solution)/shard_map/all_to_all | solution.py:430
  158.5 1.9 %collective-permute-start.60 = (f32[32,1024]{1,0:T(8,128)S(1)}, f32[32,1024]{1,0:T(8,128)S(1)}, u32[]{:S(2)}, u32[]{:S(2)}) collective-permute-start(f32[32,1024]{1,0:T(8,128)S(1)} %get-tuple-element.115), channel_id=1, source_target_pairs={{0,16},{16,0},{1,17},{17,1},{2,18},{18,2},{3,19},{19,3},{4,20},{20... | collective-permute-start | bytes 393224 | tf_op jit(solution)/shard_map/ppermute | solution.py:394
  160.4 1.7 collective-permute-start.56
  162.1 4.3 %collective-permute-done.60 = f32[32,1024]{1,0:T(8,128)S(1)} collective-permute-done((f32[32,1024]{1,0:T(8,128)S(1)}, f32[32,1024]{1,0:T(8,128)S(1)}, u32[]{:S(2)}, u32[]{:S(2)}) %collective-permute-start.60) | collective-permute-done | bytes 131104 | tf_op jit(solution)/shard_map/ppermute | solution.py:394
  166.5 2.5 %collective-permute-start.61 = (f32[32,1024]{1,0:T(8,128)S(1)}, f32[32,1024]{1,0:T(8,128)S(1)}, u32[]{:S(2)}, u32[]{:S(2)}) collective-permute-start(f32[32,1024]{1,0:T(8,128)S(1)} %add.151.refs_0_), channel_id=1, source_target_pairs={{0,96},{32,0},{64,32},{96,64},{1,97},{33,1},{65,33},{97,65},{2,98}... | collective-permute-start | bytes 393224 | tf_op jit(solution)/shard_map/ppermute | solution.py:398
  169.9 2.4 %collective-permute-start.57 = (f32[32,1024]{1,0:T(8,128)S(1)}, f32[32,1024]{1,0:T(8,128)S(1)}, u32[]{:S(2)}, u32[]{:S(2)}) collective-permute-start(f32[32,1024]{1,0:T(8,128)S(1)} %add.150.refs_0_), channel_id=1, source_target_pairs={{0,96},{32,0},{64,32},{96,64},{1,97},{33,1},{65,33},{97,65},{2,98}... | collective-permute-start | bytes 393224 | tf_op jit(solution)/shard_map/ppermute | solution.py:398
  172.3 2.3 %collective-permute-start.58 = (f32[32,1024]{1,0:T(8,128)S(1)}, f32[32,1024]{1,0:T(8,128)S(1)}, u32[]{:S(2)}, u32[]{:S(2)}) collective-permute-start(f32[32,1024]{1,0:T(8,128)S(1)} %add.150.refs_0_), channel_id=1, source_target_pairs={{0,64},{32,96},{64,0},{96,32},{1,65},{33,97},{65,1},{97,33},{2,66}... | collective-permute-start | bytes 393224 | tf_op jit(solution)/shard_map/ppermute | solution.py:398
  177.1 1.7 final1_1.1
  179.0 2.5 %final0_3.1 = (f32[8,4,64,1024]{3,2,1,0:T(8,128)}, f32[4,64,1024]{2,1,0:T(8,128)}) custom-call(s32[3]{0:T(128)S(1)} %pad_add_fusion.meta, f32[8]{0:T(128)S(1)} %copy-done.5, f32[4,8,32,1024]{3,2,1,0:T(8,128)S(1)} %get-tuple-element.114.eta, f32[32,1024]{1,0:T(8,128)S(1)} %collective-permute-done.61.refs_0_, ...), custom_call_target="tpu_custom_call", output_to_operand_aliasing={{0}: (6, {}), {1}: (7, {})} | custom-call | tf_op jit(solution)/shard_map/final0_3/pallas_call | solution.py:327
  182.0 2.5 %final1_3.1 = (f32[8,4,64,1024]{3,2,1,0:T(8,128)}, f32[4,64,1024]{2,1,0:T(8,128)}) custom-call(s32[3]{0:T(128)S(1)} %pad_add_fusion.meta, f32[8]{0:T(128)S(1)} %copy-done.5, f32[4,8,32,1024]{3,2,1,0:T(8,128)S(1)} %get-tuple-element.97.eta, f32[32,1024]{1,0:T(8,128)S(1)} %collective-permute-done.57.refs_0_, ...), custom_call_target="tpu_custom_call", output_to_operand_aliasing={{0}: (6, {}), {1}: (7, {})} | custom-call | tf_op jit(solution)/shard_map/final1_3/pallas_call | solution.py:327
  (131 shorter events, 44.4 us)
Async XLA Ops:
  3.6 11.1 %collective-permute-start = (f32[32,1024]{1,0:T(8,128)S(1)}, f32[32,1024]{1,0:T(8,128)S(1)}, u32[]{:S(2)}, u32[]{:S(2)}) collective-permute-start(f32[32,1024]{1,0:T(8,128)S(1)} %get-tuple-element.64), channel_id=1, source_target_pairs={{0,64},{32,96},{64,0},{96,32},{1,65},{33,97},{65,1},{97,33},{2,66}... | collective-permute-start | bytes 393224 | tf_op jit(solution)/shard_map/ppermute | solution.py:388
  7.6 9.5 %collective-permute-start.1 = (f32[32,1024]{1,0:T(8,128)S(1)}, f32[32,1024]{1,0:T(8,128)S(1)}, u32[]{:S(2)}, u32[]{:S(2)}) collective-permute-start(f32[32,1024]{1,0:T(8,128)S(1)} %get-tuple-element.65), channel_id=1, source_target_pairs={{0,32},{32,64},{64,96},{96,0},{1,33},{33,65},{65,97},{97,1},{2,34}... | collective-permute-start | bytes 393224 | tf_op jit(solution)/shard_map/ppermute | solution.py:388
  8.6 8.5 %collective-permute-start.2 = (f32[32,1024]{1,0:T(8,128)S(1)}, f32[32,1024]{1,0:T(8,128)S(1)}, u32[]{:S(2)}, u32[]{:S(2)}) collective-permute-start(f32[32,1024]{1,0:T(8,128)S(1)} %get-tuple-element.66), channel_id=1, source_target_pairs={{0,96},{32,0},{64,32},{96,64},{1,97},{33,1},{65,33},{97,65},{2,98}... | collective-permute-start | bytes 393224 | tf_op jit(solution)/shard_map/ppermute | solution.py:388
  13.7 7.4 %collective-permute-start.15 = (f32[32,1024]{1,0:T(8,128)S(1)}, f32[32,1024]{1,0:T(8,128)S(1)}, u32[]{:S(2)}, u32[]{:S(2)}) collective-permute-start(f32[32,1024]{1,0:T(8,128)S(1)} %get-tuple-element.76), channel_id=1, source_target_pairs={{0,64},{32,96},{64,0},{96,32},{1,65},{33,97},{65,1},{97,33},{2,66}... | collective-permute-start | bytes 393224 | tf_op jit(solution)/shard_map/ppermute | solution.py:388
  13.8 8.5 %collective-permute-start.16 = (f32[32,1024]{1,0:T(8,128)S(1)}, f32[32,1024]{1,0:T(8,128)S(1)}, u32[]{:S(2)}, u32[]{:S(2)}) collective-permute-start(f32[32,1024]{1,0:T(8,128)S(1)} %get-tuple-element.77), channel_id=1, source_target_pairs={{0,32},{32,64},{64,96},{96,0},{1,33},{33,65},{65,97},{97,1},{2,34}... | collective-permute-start | bytes 393224 | tf_op jit(solution)/shard_map/ppermute | solution.py:388
  14.7 7.6 %collective-permute-start.17 = (f32[32,1024]{1,0:T(8,128)S(1)}, f32[32,1024]{1,0:T(8,128)S(1)}, u32[]{:S(2)}, u32[]{:S(2)}) collective-permute-start(f32[32,1024]{1,0:T(8,128)S(1)} %get-tuple-element.78), channel_id=1, source_target_pairs={{0,96},{32,0},{64,32},{96,64},{1,97},{33,1},{65,33},{97,65},{2,98}... | collective-permute-start | bytes 393224 | tf_op jit(solution)/shard_map/ppermute | solution.py:388
  17.2 10.2 %collective-permute-start.3 = (f32[32,1024]{1,0:T(8,128)S(1)}, f32[32,1024]{1,0:T(8,128)S(1)}, u32[]{:S(2)}, u32[]{:S(2)}) collective-permute-start(f32[32,1024]{1,0:T(8,128)S(1)} %add_add_fusion.7), channel_id=1, source_target_pairs={{0,16},{16,0},{1,17},{17,1},{2,18},{18,2},{3,19},{19,3},{4,20},{20... | collective-permute-start | bytes 393224 | tf_op jit(solution)/shard_map/ppermute | solution.py:394
  22.3 7.1 %collective-permute-start.18 = (f32[32,1024]{1,0:T(8,128)S(1)}, f32[32,1024]{1,0:T(8,128)S(1)}, u32[]{:S(2)}, u32[]{:S(2)}) collective-permute-start(f32[32,1024]{1,0:T(8,128)S(1)} %add_add_fusion.5), channel_id=1, source_target_pairs={{0,16},{16,0},{1,17},{17,1},{2,18},{18,2},{3,19},{19,3},{4,20},{20... | collective-permute-start | bytes 393224 | tf_op jit(solution)/shard_map/ppermute | solution.py:394
  27.4 7.6 %collective-permute-start.5 = (f32[32,1024]{1,0:T(8,128)S(1)}, f32[32,1024]{1,0:T(8,128)S(1)}, u32[]{:S(2)}, u32[]{:S(2)}) collective-permute-start(f32[32,1024]{1,0:T(8,128)S(1)} %add.121.refs_1_), channel_id=1, source_target_pairs={{0,64},{32,96},{64,0},{96,32},{1,65},{33,97},{65,1},{97,33},{2,66}... | collective-permute-start | bytes 393224 | tf_op jit(solution)/shard_map/ppermute | solution.py:398
  29.0 9.1 %collective-permute-start.6 = (f32[32,1024]{1,0:T(8,128)S(1)}, f32[32,1024]{1,0:T(8,128)S(1)}, u32[]{:S(2)}, u32[]{:S(2)}) collective-permute-start(f32[32,1024]{1,0:T(8,128)S(1)} %add.121.refs_1_), channel_id=1, source_target_pairs={{0,32},{32,64},{64,96},{96,0},{1,33},{33,65},{65,97},{97,1},{2,34}... | collective-permute-start | bytes 393224 | tf_op jit(solution)/shard_map/ppermute | solution.py:398
  29.5 11.9 %collective-permute-start.22 = (f32[4,8,1024]{2,1,0:T(8,128)S(1)}, f32[4,8,1024]{2,1,0:T(8,128)S(1)}, u32[]{:S(2)}, u32[]{:S(2)}) collective-permute-start(f32[4,8,1024]{2,1,0:T(8,128)S(1)} %get-tuple-element.79), channel_id=1, source_target_pairs={{0,1},{1,2},{2,3},{3,4},{4,5},{5,6},{6,7},{7,8},{8,9},{9,10},{10,1... | collective-permute-start | bytes 393224 | tf_op jit(solution)/shard_map/ppermute | solution.py:417
  29.9 13.4 %collective-permute-start.19 = (f32[32,1024]{1,0:T(8,128)S(1)}, f32[32,1024]{1,0:T(8,128)S(1)}, u32[]{:S(2)}, u32[]{:S(2)}) collective-permute-start(f32[32,1024]{1,0:T(8,128)S(1)} %add.129.refs_1_), channel_id=1, source_target_pairs={{0,96},{32,0},{64,32},{96,64},{1,97},{33,1},{65,33},{97,65},{2,98}... | collective-permute-start | bytes 393224 | tf_op jit(solution)/shard_map/ppermute | solution.py:398
  32.9 11.7 %collective-permute-start.20 = (f32[32,1024]{1,0:T(8,128)S(1)}, f32[32,1024]{1,0:T(8,128)S(1)}, u32[]{:S(2)}, u32[]{:S(2)}) collective-permute-start(f32[32,1024]{1,0:T(8,128)S(1)} %add.129.refs_1_), channel_id=1, source_target_pairs={{0,64},{32,96},{64,0},{96,32},{1,65},{33,97},{65,1},{97,33},{2,66}... | collective-permute-start | bytes 393224 | tf_op jit(solution)/shard_map/ppermute | solution.py:398
  35.1 9.5 %collective-permute-start.21 = (f32[32,1024]{1,0:T(8,128)S(1)}, f32[32,1024]{1,0:T(8,128)S(1)}, u32[]{:S(2)}, u32[]{:S(2)}) collective-permute-start(f32[32,1024]{1,0:T(8,128)S(1)} %add.129.refs_1_), channel_id=1, source_target_pairs={{0,32},{32,64},{64,96},{96,0},{1,33},{33,65},{65,97},{97,1},{2,34}... | collective-permute-start | bytes 393224 | tf_op jit(solution)/shard_map/ppermute | solution.py:398
  41.1 9.3 %collective-permute-start.10 = (f32[32,1024]{1,0:T(8,128)S(1)}, f32[32,1024]{1,0:T(8,128)S(1)}, u32[]{:S(2)}, u32[]{:S(2)}) collective-permute-start(f32[32,1024]{1,0:T(8,128)S(1)} %get-tuple-element.73), channel_id=1, source_target_pairs={{0,96},{32,0},{64,32},{96,64},{1,97},{33,1},{65,33},{97,65},{2,98}... | collective-permute-start | bytes 393224 | tf_op jit(solution)/shard_map/ppermute | solution.py:388
  41.4 12.2 %collective-permute-start.8 = (f32[32,1024]{1,0:T(8,128)S(1)}, f32[32,1024]{1,0:T(8,128)S(1)}, u32[]{:S(2)}, u32[]{:S(2)}) collective-permute-start(f32[32,1024]{1,0:T(8,128)S(1)} %get-tuple-element.71), channel_id=1, source_target_pairs={{0,64},{32,96},{64,0},{96,32},{1,65},{33,97},{65,1},{97,33},{2,66}... | collective-permute-start | bytes 393224 | tf_op jit(solution)/shard_map/ppermute | solution.py:388
  43.3 10.3 %collective-permute-start.9 = (f32[32,1024]{1,0:T(8,128)S(1)}, f32[32,1024]{1,0:T(8,128)S(1)}, u32[]{:S(2)}, u32[]{:S(2)}) collective-permute-start(f32[32,1024]{1,0:T(8,128)S(1)} %get-tuple-element.72), channel_id=1, source_target_pairs={{0,32},{32,64},{64,96},{96,0},{1,33},{33,65},{65,97},{97,1},{2,34}... | collective-permute-start | bytes 393224 | tf_op jit(solution)/shard_map/ppermute | solution.py:388
  47.6 7.6 %collective-permute-start.31 = (f32[32,1024]{1,0:T(8,128)S(1)}, f32[32,1024]{1,0:T(8,128)S(1)}, u32[]{:S(2)}, u32[]{:S(2)}) collective-permute-start(f32[32,1024]{1,0:T(8,128)S(1)} %get-tuple-element.90), channel_id=1, source_target_pairs={{0,64},{32,96},{64,0},{96,32},{1,65},{33,97},{65,1},{97,33},{2,66}... | collective-permute-start | bytes 393224 | tf_op jit(solution)/shard_map/ppermute | solution.py:388
  60.2 10.0 %collective-permute-start.12 = (f32[32,1024]{1,0:T(8,128)S(1)}, f32[32,1024]{1,0:T(8,128)S(1)}, u32[]{:S(2)}, u32[]{:S(2)}) collective-permute-start(f32[32,1024]{1,0:T(8,128)S(1)} %add.125.refs_2_), channel_id=1, source_target_pairs={{0,96},{32,0},{64,32},{96,64},{1,97},{33,1},{65,33},{97,65},{2,98}... | collective-permute-start | bytes 393224 | tf_op jit(solution)/shard_map/ppermute | solution.py:398
  61.4 9.5 %collective-permute-start.13 = (f32[32,1024]{1,0:T(8,128)S(1)}, f32[32,1024]{1,0:T(8,128)S(1)}, u32[]{:S(2)}, u32[]{:S(2)}) collective-permute-start(f32[32,1024]{1,0:T(8,128)S(1)} %add.125.refs_2_), channel_id=1, source_target_pairs={{0,64},{32,96},{64,0},{96,32},{1,65},{33,97},{65,1},{97,33},{2,66}... | collective-permute-start | bytes 393224 | tf_op jit(solution)/shard_map/ppermute | solution.py:398
  61.6 11.0 %collective-permute-start.14 = (f32[32,1024]{1,0:T(8,128)S(1)}, f32[32,1024]{1,0:T(8,128)S(1)}, u32[]{:S(2)}, u32[]{:S(2)}) collective-permute-start(f32[32,1024]{1,0:T(8,128)S(1)} %add.125.refs_2_), channel_id=1, source_target_pairs={{0,32},{32,64},{64,96},{96,0},{1,33},{33,65},{65,97},{97,1},{2,34}... | collective-permute-start | bytes 393224 | tf_op jit(solution)/shard_map/ppermute | solution.py:398
  63.1 13.9 %collective-permute-start.38 = (f32[4,8,1024]{2,1,0:T(8,128)S(1)}, f32[4,8,1024]{2,1,0:T(8,128)S(1)}, u32[]{:S(2)}, u32[]{:S(2)}) collective-permute-start(f32[4,8,1024]{2,1,0:T(8,128)S(1)} %get-tuple-element.93), channel_id=1, source_target_pairs={{0,1},{1,2},{2,3},{3,4},{4,5},{5,6},{6,7},{7,8},{8,9},{9,10},{10,1... | collective-permute-start | bytes 393224 | tf_op jit(solution)/shard_map/ppermute | solution.py:417
  63.2 15.0 %collective-permute-start.35 = (f32[32,1024]{1,0:T(8,128)S(1)}, f32[32,1024]{1,0:T(8,128)S(1)}, u32[]{:S(2)}, u32[]{:S(2)}) collective-permute-start(f32[32,1024]{1,0:T(8,128)S(1)} %add.137.refs_2_), channel_id=1, source_target_pairs={{0,96},{32,0},{64,32},{96,64},{1,97},{33,1},{65,33},{97,65},{2,98}... | collective-permute-start | bytes 393224 | tf_op jit(solution)/shard_map/ppermute | solution.py:398
  70.3 10.0 %collective-permute-start.36 = (f32[32,1024]{1,0:T(8,128)S(1)}, f32[32,1024]{1,0:T(8,128)S(1)}, u32[]{:S(2)}, u32[]{:S(2)}) collective-permute-start(f32[32,1024]{1,0:T(8,128)S(1)} %add.137.refs_2_), channel_id=1, source_target_pairs={{0,64},{32,96},{64,0},{96,32},{1,65},{33,97},{65,1},{97,33},{2,66}... | collective-permute-start | bytes 393224 | tf_op jit(solution)/shard_map/ppermute | solution.py:398
  70.9 10.5 %collective-permute-start.37 = (f32[32,1024]{1,0:T(8,128)S(1)}, f32[32,1024]{1,0:T(8,128)S(1)}, u32[]{:S(2)}, u32[]{:S(2)}) collective-permute-start(f32[32,1024]{1,0:T(8,128)S(1)} %add.137.refs_2_), channel_id=1, source_target_pairs={{0,32},{32,64},{64,96},{96,0},{1,33},{33,65},{65,97},{97,1},{2,34}... | collective-permute-start | bytes 393224 | tf_op jit(solution)/shard_map/ppermute | solution.py:398
  75.7 9.9 %collective-permute-start.24 = (f32[32,1024]{1,0:T(8,128)S(1)}, f32[32,1024]{1,0:T(8,128)S(1)}, u32[]{:S(2)}, u32[]{:S(2)}) collective-permute-start(f32[32,1024]{1,0:T(8,128)S(1)} %get-tuple-element.85), channel_id=1, source_target_pairs={{0,64},{32,96},{64,0},{96,32},{1,65},{33,97},{65,1},{97,33},{2,66}... | collective-permute-start | bytes 393224 | tf_op jit(solution)/shard_map/ppermute | solution.py:388
  77.0 11.1 %collective-permute-start.25 = (f32[32,1024]{1,0:T(8,128)S(1)}, f32[32,1024]{1,0:T(8,128)S(1)}, u32[]{:S(2)}, u32[]{:S(2)}) collective-permute-start(f32[32,1024]{1,0:T(8,128)S(1)} %get-tuple-element.86), channel_id=1, source_target_pairs={{0,32},{32,64},{64,96},{96,0},{1,33},{33,65},{65,97},{97,1},{2,34}... | collective-permute-start | bytes 393224 | tf_op jit(solution)/shard_map/ppermute | solution.py:388
  78.2 9.9 %collective-permute-start.26 = (f32[32,1024]{1,0:T(8,128)S(1)}, f32[32,1024]{1,0:T(8,128)S(1)}, u32[]{:S(2)}, u32[]{:S(2)}) collective-permute-start(f32[32,1024]{1,0:T(8,128)S(1)} %get-tuple-element.87), channel_id=1, source_target_pairs={{0,96},{32,0},{64,32},{96,64},{1,97},{33,1},{65,33},{97,65},{2,98}... | collective-permute-start | bytes 393224 | tf_op jit(solution)/shard_map/ppermute | solution.py:388
  84.4 7.7 %collective-permute-start.40 = (f32[32,1024]{1,0:T(8,128)S(1)}, f32[32,1024]{1,0:T(8,128)S(1)}, u32[]{:S(2)}, u32[]{:S(2)}) collective-permute-start(f32[32,1024]{1,0:T(8,128)S(1)} %get-tuple-element.100), channel_id=1, source_target_pairs={{0,64},{32,96},{64,0},{96,32},{1,65},{33,97},{65,1},{97,33},{2,66}... | collective-permute-start | bytes 393224 | tf_op jit(solution)/shard_map/ppermute | solution.py:388
  84.8 8.7 %collective-permute-start.41 = (f32[32,1024]{1,0:T(8,128)S(1)}, f32[32,1024]{1,0:T(8,128)S(1)}, u32[]{:S(2)}, u32[]{:S(2)}) collective-permute-start(f32[32,1024]{1,0:T(8,128)S(1)} %get-tuple-element.101), channel_id=1, source_target_pairs={{0,32},{32,64},{64,96},{96,0},{1,33},{33,65},{65,97},{97,1},{2,34}... | collective-permute-start | bytes 393224 | tf_op jit(solution)/shard_map/ppermute | solution.py:388
  85.6 7.9 %collective-permute-start.42 = (f32[32,1024]{1,0:T(8,128)S(1)}, f32[32,1024]{1,0:T(8,128)S(1)}, u32[]{:S(2)}, u32[]{:S(2)}) collective-permute-start(f32[32,1024]{1,0:T(8,128)S(1)} %get-tuple-element.102), channel_id=1, source_target_pairs={{0,96},{32,0},{64,32},{96,64},{1,97},{33,1},{65,33},{97,65},{2,98}... | collective-permute-start | bytes 393224 | tf_op jit(solution)/shard_map/ppermute | solution.py:388
  88.1 9.2 %collective-permute-start.27 = (f32[32,1024]{1,0:T(8,128)S(1)}, f32[32,1024]{1,0:T(8,128)S(1)}, u32[]{:S(2)}, u32[]{:S(2)}) collective-permute-start(f32[32,1024]{1,0:T(8,128)S(1)} %add_add_fusion.4), channel_id=1, source_target_pairs={{0,16},{16,0},{1,17},{17,1},{2,18},{18,2},{3,19},{19,3},{4,20},{20... | collective-permute-start | bytes 393224 | tf_op jit(solution)/shard_map/ppermute | solution.py:394
  97.4 7.9 %collective-permute-start.29 = (f32[32,1024]{1,0:T(8,128)S(1)}, f32[32,1024]{1,0:T(8,128)S(1)}, u32[]{:S(2)}, u32[]{:S(2)}) collective-permute-start(f32[32,1024]{1,0:T(8,128)S(1)} %add.133.refs_2_), channel_id=1, source_target_pairs={{0,64},{32,96},{64,0},{96,32},{1,65},{33,97},{65,1},{97,33},{2,66}... | collective-permute-start | bytes 393224 | tf_op jit(solution)/shard_map/ppermute | solution.py:398
  98.7 10.6 %collective-permute-start.30 = (f32[32,1024]{1,0:T(8,128)S(1)}, f32[32,1024]{1,0:T(8,128)S(1)}, u32[]{:S(2)}, u32[]{:S(2)}) collective-permute-start(f32[32,1024]{1,0:T(8,128)S(1)} %add.133.refs_2_), channel_id=1, source_target_pairs={{0,32},{32,64},{64,96},{96,0},{1,33},{33,65},{65,97},{97,1},{2,34}... | collective-permute-start | bytes 393224 | tf_op jit(solution)/shard_map/ppermute | solution.py:398
  100.3 12.7 %collective-permute-start.47 = (f32[4,8,1024]{2,1,0:T(8,128)S(1)}, f32[4,8,1024]{2,1,0:T(8,128)S(1)}, u32[]{:S(2)}, u32[]{:S(2)}) collective-permute-start(f32[4,8,1024]{2,1,0:T(8,128)S(1)} %get-tuple-element.103), channel_id=1, source_target_pairs={{0,1},{1,2},{2,3},{3,4},{4,5},{5,6},{6,7},{7,8},{8,9},{9,10},{10,1... | collective-permute-start | bytes 393224 | tf_op jit(solution)/shard_map/ppermute | solution.py:417
  100.3 12.8 %collective-permute-start.44 = (f32[32,1024]{1,0:T(8,128)S(1)}, f32[32,1024]{1,0:T(8,128)S(1)}, u32[]{:S(2)}, u32[]{:S(2)}) collective-permute-start(f32[32,1024]{1,0:T(8,128)S(1)} %add.141.refs_2_), channel_id=1, source_target_pairs={{0,96},{32,0},{64,32},{96,64},{1,97},{33,1},{65,33},{97,65},{2,98}... | collective-permute-start | bytes 393224 | tf_op jit(solution)/shard_map/ppermute | solution.py:398
  102.9 13.4 %collective-permute-start.45 = (f32[32,1024]{1,0:T(8,128)S(1)}, f32[32,1024]{1,0:T(8,128)S(1)}, u32[]{:S(2)}, u32[]{:S(2)}) collective-permute-start(f32[32,1024]{1,0:T(8,128)S(1)} %add.141.refs_2_), channel_id=1, source_target_pairs={{0,64},{32,96},{64,0},{96,32},{1,65},{33,97},{65,1},{97,33},{2,66}... | collective-permute-start | bytes 393224 | tf_op jit(solution)/shard_map/ppermute | solution.py:398
  105.3 11.0 %collective-permute-start.46 = (f32[32,1024]{1,0:T(8,128)S(1)}, f32[32,1024]{1,0:T(8,128)S(1)}, u32[]{:S(2)}, u32[]{:S(2)}) collective-permute-start(f32[32,1024]{1,0:T(8,128)S(1)} %add.141.refs_2_), channel_id=1, source_target_pairs={{0,32},{32,64},{64,96},{96,0},{1,33},{33,65},{65,97},{97,1},{2,34}... | collective-permute-start | bytes 393224 | tf_op jit(solution)/shard_map/ppermute | solution.py:398
  112.9 9.3 %collective-permute-start.52 = (f32[32,1024]{1,0:T(8,128)S(1)}, f32[32,1024]{1,0:T(8,128)S(1)}, u32[]{:S(2)}, u32[]{:S(2)}) collective-permute-start(f32[32,1024]{1,0:T(8,128)S(1)} %get-tuple-element.110), channel_id=1, source_target_pairs={{0,64},{32,96},{64,0},{96,32},{1,65},{33,97},{65,1},{97,33},{2,66}... | collective-permute-start | bytes 393224 | tf_op jit(solution)/shard_map/ppermute | solution.py:388
  113.0 12.5 %collective-permute-start.53 = (f32[32,1024]{1,0:T(8,128)S(1)}, f32[32,1024]{1,0:T(8,128)S(1)}, u32[]{:S(2)}, u32[]{:S(2)}) collective-permute-start(f32[32,1024]{1,0:T(8,128)S(1)} %get-tuple-element.111), channel_id=1, source_target_pairs={{0,32},{32,64},{64,96},{96,0},{1,33},{33,65},{65,97},{97,1},{2,34}... | collective-permute-start | bytes 393224 | tf_op jit(solution)/shard_map/ppermute | solution.py:388
  113.2 12.3 %collective-permute-start.54 = (f32[32,1024]{1,0:T(8,128)S(1)}, f32[32,1024]{1,0:T(8,128)S(1)}, u32[]{:S(2)}, u32[]{:S(2)}) collective-permute-start(f32[32,1024]{1,0:T(8,128)S(1)} %get-tuple-element.112), channel_id=1, source_target_pairs={{0,96},{32,0},{64,32},{96,64},{1,97},{33,1},{65,33},{97,65},{2,98}... | collective-permute-start | bytes 393224 | tf_op jit(solution)/shard_map/ppermute | solution.py:388
  158.5 8.0 %collective-permute-start.60 = (f32[32,1024]{1,0:T(8,128)S(1)}, f32[32,1024]{1,0:T(8,128)S(1)}, u32[]{:S(2)}, u32[]{:S(2)}) collective-permute-start(f32[32,1024]{1,0:T(8,128)S(1)} %get-tuple-element.115), channel_id=1, source_target_pairs={{0,16},{16,0},{1,17},{17,1},{2,18},{18,2},{3,19},{19,3},{4,20},{20... | collective-permute-start | bytes 393224 | tf_op jit(solution)/shard_map/ppermute | solution.py:394
  160.4 9.5 %collective-permute-start.56 = (f32[32,1024]{1,0:T(8,128)S(1)}, f32[32,1024]{1,0:T(8,128)S(1)}, u32[]{:S(2)}, u32[]{:S(2)}) collective-permute-start(f32[32,1024]{1,0:T(8,128)S(1)} %get-tuple-element.113), channel_id=1, source_target_pairs={{0,16},{16,0},{1,17},{17,1},{2,18},{18,2},{3,19},{19,3},{4,20},{20... | collective-permute-start | bytes 393224 | tf_op jit(solution)/shard_map/ppermute | solution.py:394
  166.5 8.9 %collective-permute-start.61 = (f32[32,1024]{1,0:T(8,128)S(1)}, f32[32,1024]{1,0:T(8,128)S(1)}, u32[]{:S(2)}, u32[]{:S(2)}) collective-permute-start(f32[32,1024]{1,0:T(8,128)S(1)} %add.151.refs_0_), channel_id=1, source_target_pairs={{0,96},{32,0},{64,32},{96,64},{1,97},{33,1},{65,33},{97,65},{2,98}... | collective-permute-start | bytes 393224 | tf_op jit(solution)/shard_map/ppermute | solution.py:398
  169.0 9.8 %collective-permute-start.62 = (f32[32,1024]{1,0:T(8,128)S(1)}, f32[32,1024]{1,0:T(8,128)S(1)}, u32[]{:S(2)}, u32[]{:S(2)}) collective-permute-start(f32[32,1024]{1,0:T(8,128)S(1)} %add.151.refs_0_), channel_id=1, source_target_pairs={{0,64},{32,96},{64,0},{96,32},{1,65},{33,97},{65,1},{97,33},{2,66}... | collective-permute-start | bytes 393224 | tf_op jit(solution)/shard_map/ppermute | solution.py:398
  169.0 10.0 %collective-permute-start.63 = (f32[32,1024]{1,0:T(8,128)S(1)}, f32[32,1024]{1,0:T(8,128)S(1)}, u32[]{:S(2)}, u32[]{:S(2)}) collective-permute-start(f32[32,1024]{1,0:T(8,128)S(1)} %add.151.refs_0_), channel_id=1, source_target_pairs={{0,32},{32,64},{64,96},{96,0},{1,33},{33,65},{65,97},{97,1},{2,34}... | collective-permute-start | bytes 393224 | tf_op jit(solution)/shard_map/ppermute | solution.py:398
  169.9 11.5 %collective-permute-start.57 = (f32[32,1024]{1,0:T(8,128)S(1)}, f32[32,1024]{1,0:T(8,128)S(1)}, u32[]{:S(2)}, u32[]{:S(2)}) collective-permute-start(f32[32,1024]{1,0:T(8,128)S(1)} %add.150.refs_0_), channel_id=1, source_target_pairs={{0,96},{32,0},{64,32},{96,64},{1,97},{33,1},{65,33},{97,65},{2,98}... | collective-permute-start | bytes 393224 | tf_op jit(solution)/shard_map/ppermute | solution.py:398
  172.3 9.2 %collective-permute-start.58 = (f32[32,1024]{1,0:T(8,128)S(1)}, f32[32,1024]{1,0:T(8,128)S(1)}, u32[]{:S(2)}, u32[]{:S(2)}) collective-permute-start(f32[32,1024]{1,0:T(8,128)S(1)} %add.150.refs_0_), channel_id=1, source_target_pairs={{0,64},{32,96},{64,0},{96,32},{1,65},{33,97},{65,1},{97,33},{2,66}... | collective-permute-start | bytes 393224 | tf_op jit(solution)/shard_map/ppermute | solution.py:398
  (23 other events, 307.6 us)
